TPU v7x, 256 devices: a whole 4x4x8 slice. The times are simulated.
256 devices in a mesh: blk: 64 (over y_lo, z, x), rep: 4 (over y_hi, core).
Axes of the slice: x: 4, y: 4 (y_hi: 2, y_lo: 2; y = y_hi * 2 + y_lo), z: 8, core: 2. Of those that a mesh axis runs over, the one named last changes fastest.
Arguments:
- features: bfloat16 [262144, 128], P(('blk', 'rep')), may hold values from -6 to 6
- weight: bfloat16 [128, 512], replicated, may hold values from -0.5 to 0.5
- bias: float32 [512], replicated, may hold values from -3 to 3
- tile_values: bfloat16 [262144, 4096], P(('blk', 'rep')), may hold values from -0.125 to 0.125
- tile_cols: int32 [2048, 32], P(('blk', 'rep')), may hold values from 0 to 95, as said below
- tile_counts: int32 [2048], P(('blk', 'rep')), may hold values from 1 to 32, as said below
- out_grad: bfloat16 [262144, 512], P(('blk', 'rep')), may hold values from -6 to 6
Outputs:
- activations: bfloat16 [262144, 512], P(('blk', 'rep'))
- feature_grad: float32 [262144, 128], P(('blk', 'rep'))
- weight_grad: float32 [128, 512], replicated
- bias_grad: float32 [512], replicated
Inputs may be any that keep to these rules, and one draw needn't show every extreme that they name: `tile_cols`: within one row tile the 32 entries are different. `tile_counts`: slots 0 to count - 1 of a row tile are live.
All inputs are finite; a program needn't handle non-finite values.
Results may differ from a plain program's by a relative error of at most 0.0059.
Values may be sent and summed in bfloat16 or wider, within the bound.
No kernel may reach another device: no remote copies, remote signals or barrier semaphores. Data moves between devices by JAX's collectives and lax.ppermute only.
A program may use at most 128 MiB of HBM per device.

v0:
```python
import functools
import math

import jax
import jax.numpy as jnp
from jax import lax
from jax.experimental import pallas as pl
from jax.experimental.pallas import tpu as pltpu
from jax.sharding import PartitionSpec as P


TILE = 128
REACH = 1
SLOTS = 32
GROUP = 4
PIECE_TILES = 8
PIECES = (2 * REACH + 1) * GROUP
DUMMY = PIECES * PIECE_TILES
AXES = ("y_lo", "z", "x", "y_hi", "core")
NEAR = ("x", "y_hi")
FAR = ("y_lo", "z")
VMEM_LIMIT = 32 << 20
SPLIT = (2, 8, 4, 2, 2)
STEP_TILES = 1


def sent(value, target):
    count = lax.axis_size(AXES)
    return lax.ppermute(value, AXES, [(source, target(source, count)) for source in range(count)])


def to_core(value):
    return sent(value, lambda device, count: device ^ 1)


def to_row(value):
    return sent(value, lambda device, count: device ^ 2)


def to_block(value, steps):
    return sent(value, lambda device, count: (device + GROUP * steps) % count)


def to_all(value, axes):
    count = lax.axis_size(axes)
    copies = jnp.broadcast_to(value[None], (count,) + value.shape)
    return lax.all_to_all(copies, axes, 0, 0, tiled=True)


def gelu_parts(pre_act):
    inner = 0.7978845608028654 * (pre_act + 0.044715 * pre_act * pre_act * pre_act)
    tangent = jnp.tanh(inner)
    value_part = 0.5 * pre_act * (1.0 + tangent)
    slope = 0.5 * (1.0 + tangent) + 0.5 * pre_act * (
        1.0 - tangent * tangent
    ) * 0.7978845608028654 * (1.0 + 0.134145 * pre_act * pre_act)
    return (value_part, slope)


def streamed(step, source_ref, held_ref, arrived):
    def copy(tile):
        rows = pl.ds(pl.multiple_of(tile * TILE, TILE), TILE)
        return pltpu.make_async_copy(source_ref.at[rows], held_ref.at[tile], arrived.at[tile])

    @pl.when(step == 0)
    def _():
        for tile in range(held_ref.shape[0]):
            copy(tile).start()

    copy(step).wait()
    return held_ref.at[step]


def forward_kernel(
    factor, place_ref, core_ref, window_ref, source_ref, grad_ref, weight_ref, bias_ref,
    act_ref, back_ref, own_ref, other_ref, agg_ref, pre_ref, bias_sum_ref, held_ref, arrived,
):
    step = pl.program_id(0)
    values_ref = streamed(step, source_ref, held_ref, arrived)
    weight = weight_ref[...]
    for sub in range(STEP_TILES):
        rows = slice(sub * TILE, (sub + 1) * TILE)
        tile = step * STEP_TILES + sub
        total = None
        for pair in range(SLOTS // 2):
            one = window_ref[place_ref[tile, 2 * pair]]
            two = window_ref[place_ref[tile, 2 * pair + 1]]
            term = jnp.dot(
                values_ref[:, 2 * pair * TILE : (2 * pair + 2) * TILE],
                jnp.concatenate([one, two], axis=0),
                preferred_element_type=jnp.float32,
            )
            total = term if total is None else total + term
        aggregated = total.astype(jnp.bfloat16)
        pre_act = jnp.dot(aggregated, weight, preferred_element_type=jnp.float32) + bias_ref[...]
        value_part, slope = gelu_parts(pre_act)
        act_ref[rows, :] = value_part.astype(jnp.bfloat16)
        pre_wide = (grad_ref[rows, :].astype(jnp.float32) * slope).astype(jnp.bfloat16)
        back_ref[:, rows] = lax.dot_general(
            weight, pre_wide, (((1,), (1,)), ((), ())), preferred_element_type=jnp.float32
        ).astype(jnp.bfloat16)
        place = pl.ds(pl.multiple_of(tile * TILE, TILE), TILE)
        agg_ref[place, :] = aggregated
        pre_ref[place, :] = pre_wide
        part = jnp.sum(pre_wide.astype(jnp.float32).reshape(TILE // 8, 8, -1), axis=0)
        bias_sum_ref[pl.ds(pl.multiple_of(tile * 8, 8), 8), :] = part

    @pl.when(step == pl.num_programs(0) - 1)
    def _():
        sums = factor * lax.dot_general(
            agg_ref[...], pre_ref[...], (((0,), (0,)), ((), ())), preferred_element_type=jnp.float32
        )
        bias_sum = jnp.sum(bias_sum_ref[...], axis=0, keepdims=True) * factor
        count, rows_of, _ = own_ref.shape
        out_dim = sums.shape[1]
        parts = [bias_sum[:, i * TILE : (i + 1) * TILE] for i in range(out_dim // TILE)]
        parts.append(jnp.zeros((rows_of - len(parts), TILE), jnp.float32))
        side = jnp.concatenate(parts, axis=0)
        for turn, sums_ref in enumerate((own_ref, other_ref)):
            core = jnp.bitwise_xor(core_ref[0], turn)
            for chunk in range(count):
                low = sums[2 * chunk * rows_of : (2 * chunk + 1) * rows_of]
                high = sums[(2 * chunk + 1) * rows_of : (2 * chunk + 2) * rows_of]
                sums_ref[chunk, :, :out_dim] = jnp.where(core == 0, low, high)
                sums_ref[chunk, :, out_dim:] = side


def backward_kernel(
    place_ref, back_ref, source_ref, keep_ref, send_ref, total_ref, held_ref, arrived
):
    step = pl.program_id(0)
    values_ref = streamed(step, source_ref, held_ref, arrived)

    @pl.when(step == 0)
    def _():
        total_ref[...] = jnp.zeros_like(total_ref)

    for sub in range(STEP_TILES):
        rows = slice(sub * TILE, (sub + 1) * TILE)
        back = back_ref[:, rows]
        for pair in range(SLOTS // 2):
            term = jnp.dot(
                back,
                values_ref[:, 2 * pair * TILE : (2 * pair + 2) * TILE],
                preferred_element_type=jnp.float32,
            )
            for half in range(2):
                spot = place_ref[step * STEP_TILES + sub, 2 * pair + half]
                total_ref[spot] += term[:, half * TILE : (half + 1) * TILE]

    @pl.when(step == pl.num_programs(0) - 1)
    def _():
        half = DUMMY // 2
        keep_ref[...] = total_ref[:half].astype(jnp.bfloat16)
        send_ref[...] = total_ref[half : 2 * half].astype(jnp.bfloat16)


def layer(features, weight, bias, tile_values, tile_cols, tile_counts, out_grad):
    rows_dev, in_dim = features.shape
    out_dim = weight.shape[1]
    row_tiles = rows_dev // TILE
    nodes = rows_dev * lax.axis_size(AXES)
    factor = 1.0 / math.sqrt(nodes)
    rep = lax.axis_index(("y_hi", "core"))
    core = lax.axis_index("core")
    chunks = lax.axis_size(NEAR)
    chunk_rows = in_dim // (2 * chunks)
    step_rows = STEP_TILES * TILE

    other_row = to_row(features)
    pieces = {0: (features, other_row)}
    for steps in (1, -1):
        pieces[-steps] = (to_block(features, steps), to_block(other_row, steps))
    near = [piece for offset in (-1, 0, 1) for piece in pieces[offset]]
    far = [to_core(piece) for piece in near]
    blank = jnp.zeros_like(features)
    window = jnp.stack(near + far + [blank]).reshape(-1, TILE, in_dim)

    block_tile = tile_cols % (GROUP * PIECE_TILES)
    offset = tile_cols // (GROUP * PIECE_TILES)
    turn = (block_tile // PIECE_TILES) ^ rep
    place = ((turn & 1) * (PIECES // 2) + offset * 2 + (turn >> 1)) * PIECE_TILES
    place = place + block_tile % PIECE_TILES
    is_live = jnp.arange(SLOTS)[None, :] < tile_counts[:, None]
    place = jnp.where(is_live, place, DUMMY).astype(jnp.int32)

    tile_values = pltpu.with_memory_space_constraint(tile_values, pltpu.HBM)
    held = [
        pltpu.VMEM((row_tiles, TILE, SLOTS * TILE), jnp.bfloat16),
        pltpu.SemaphoreType.DMA((row_tiles,)),
    ]
    whole = lambda *shape: pl.BlockSpec(shape, lambda i, *_: (0,) * len(shape))
    act, back, own_sums, other_sums = pl.pallas_call(
        functools.partial(forward_kernel, factor),
        out_shape=(
            jax.ShapeDtypeStruct((rows_dev, out_dim), jnp.bfloat16),
            jax.ShapeDtypeStruct((in_dim, rows_dev), jnp.bfloat16),
            jax.ShapeDtypeStruct((chunks, chunk_rows, out_dim + TILE), jnp.float32),
            jax.ShapeDtypeStruct((chunks, chunk_rows, out_dim + TILE), jnp.float32),
        ),
        grid_spec=pltpu.PrefetchScalarGridSpec(
            num_scalar_prefetch=2,
            grid=(row_tiles // STEP_TILES,),
            in_specs=[
                whole(*window.shape),
                pl.BlockSpec(memory_space=pltpu.HBM),
                pl.BlockSpec((step_rows, out_dim), lambda i, *_: (i, 0)),
                whole(in_dim, out_dim),
                whole(1, out_dim),
            ],
            out_specs=(
                pl.BlockSpec((step_rows, out_dim), lambda i, *_: (i, 0)),
                pl.BlockSpec((in_dim, step_rows), lambda i, *_: (0, i)),
                whole(chunks, chunk_rows, out_dim + TILE),
                whole(chunks, chunk_rows, out_dim + TILE),
            ),
            scratch_shapes=[
                pltpu.VMEM((rows_dev, in_dim), jnp.bfloat16),
                pltpu.VMEM((rows_dev, out_dim), jnp.bfloat16),
                pltpu.VMEM((row_tiles * 8, out_dim), jnp.float32),
                *held,
            ],
        ),
        compiler_params=pltpu.CompilerParams(vmem_limit_bytes=VMEM_LIMIT),
        cost_estimate=pl.CostEstimate(flops=3 << 30, bytes_accessed=15 << 20, transcendentals=1 << 19),
        name="forward",
    )(place, core.reshape(1).astype(jnp.int32), window, tile_values, out_grad, weight, bias.reshape(1, -1))

    half_tiles = DUMMY // 2
    backward = pl.pallas_call(
        backward_kernel,
        out_shape=(jax.ShapeDtypeStruct((half_tiles, in_dim, TILE), jnp.bfloat16),) * 2,
        grid_spec=pltpu.PrefetchScalarGridSpec(
            num_scalar_prefetch=1,
            grid=(row_tiles // STEP_TILES,),
            in_specs=[
                pl.BlockSpec((in_dim, step_rows), lambda i, *_: (0, i)),
                pl.BlockSpec(memory_space=pltpu.HBM),
            ],
            out_specs=(whole(half_tiles, in_dim, TILE),) * 2,
            scratch_shapes=[pltpu.VMEM((DUMMY + 1, in_dim, TILE), jnp.float32), *held],
        ),
        compiler_params=pltpu.CompilerParams(vmem_limit_bytes=VMEM_LIMIT),
        cost_estimate=pl.CostEstimate(flops=2 << 30, bytes_accessed=12 << 20, transcendentals=0),
        name="backward",
    )
    keep, send = backward(place, back, tile_values)

    wide = lambda value: value.astype(jnp.float32)
    moved_sums = to_core(other_sums)
    part = own_sums + moved_sums
    from_core = to_core(send)
    part = jnp.sum(lax.all_to_all(part, NEAR, 0, 0, tiled=True), axis=0)
    part, from_core = lax.optimization_barrier((part, from_core))
    keep, from_core = (value.reshape(3, 2, -1, in_dim, TILE) for value in (keep, from_core))
    moved = []
    for steps in (1, -1):
        term = wide(keep[1 + steps]) + wide(from_core[1 + steps])
        moved.append(to_block(term.astype(jnp.bfloat16), steps))
    part = jnp.sum(to_all(part, FAR), axis=0)
    bias_grad = part[: out_dim // TILE, out_dim:].reshape(out_dim)
    total = wide(keep[1]) + wide(from_core[1]) + wide(moved[0]) + wide(moved[1])
    part, total = lax.optimization_barrier((part, jnp.swapaxes(total, 2, 3)))
    last = to_row(total[1].astype(jnp.bfloat16))
    mine = to_all(part[:, :out_dim], NEAR)
    theirs = to_core(mine)
    odd = core == 1
    weight_grad = jnp.stack([jnp.where(odd, theirs, mine), jnp.where(odd, mine, theirs)], axis=1)
    weight_grad = weight_grad.reshape(in_dim, out_dim)
    feature_grad = (total[0] + wide(last)).reshape(rows_dev, in_dim)
    return (act, feature_grad, weight_grad, bias_grad)


def solution(mesh):
    mesh = jax.sharding.Mesh(mesh.devices.reshape(SPLIT), AXES)
    in_specs = (
        P(AXES, None),
        P(),
        P(),
        P(AXES, None),
        P(AXES, None),
        P(AXES),
        P(AXES, None),
    )
    out_specs = (P(AXES, None), P(AXES, None), P(), P())
    return jax.shard_map(layer, mesh=mesh, in_specs=in_specs, out_specs=out_specs, check_vma=False)
```

profile of v0, /device:TPU:1, one launch (start us, length us, event | category | flops | bytes accessed | tf_op | source)
XLA Modules:
  0.0 111.5 jit_solution(4184151695327332514)
XLA Ops:
  0.7 3.8 %collective-permute-start.1 = (bf16[1024,128]{1,0:T(8,128)(2,1)}, bf16[1024,128]{1,0:T(8,128)(2,1)S(1)}, u32[]{:S(2)}, u32[]{:S(2)}) collective-permute-start(bf16[1024,128]{1,0:T(8,128)(2,1)} %param.7), channel_id=1, source_target_pairs={{0,2},{1,3},{2,0},{3,1},{4,6},{5,7},{6,4},{7,5},{8,10},{9,11},{10,... | collective-permute-start | bytes 786440 | tf_op jit(solution)/shard_map/ppermute | solution.py:29
  4.5 1.2 %collective-permute-start = (bf16[1024,128]{1,0:T(8,128)(2,1)}, bf16[1024,128]{1,0:T(8,128)(2,1)S(1)}, u32[]{:S(2)}, u32[]{:S(2)}) collective-permute-start(bf16[1024,128]{1,0:T(8,128)(2,1)} %param.7), channel_id=1, source_target_pairs={{0,4},{1,5},{2,6},{3,7},{4,8},{5,9},{6,10},{7,11},{8,12},{9,13},{1... | collective-permute-start | bytes 786440 | tf_op jit(solution)/shard_map/ppermute | solution.py:29
  5.7 6.7 %collective-permute-start.3 = (bf16[1024,128]{1,0:T(8,128)(2,1)}, bf16[1024,128]{1,0:T(8,128)(2,1)S(1)}, u32[]{:S(2)}, u32[]{:S(2)}) collective-permute-start(bf16[1024,128]{1,0:T(8,128)(2,1)} %param.7), channel_id=1, source_target_pairs={{0,252},{1,253},{2,254},{3,255},{4,0},{5,1},{6,2},{7,3},{8,4},{9,5... | collective-permute-start | bytes 786440 | tf_op jit(solution)/shard_map/ppermute | solution.py:29
  12.4 1.2 %collective-permute-start.7 = (bf16[1024,128]{1,0:T(8,128)(2,1)}, bf16[1024,128]{1,0:T(8,128)(2,1)S(1)}, u32[]{:S(2)}, u32[]{:S(2)}) collective-permute-start(bf16[1024,128]{1,0:T(8,128)(2,1)} %param.7), channel_id=1, source_target_pairs={{0,1},{1,0},{2,3},{3,2},{4,5},{5,4},{6,7},{7,6},{8,9},{9,8},{10,11... | collective-permute-start | bytes 786440 | tf_op jit(solution)/shard_map/ppermute | solution.py:29
  14.4 11.3 %collective-permute-start.4 = (bf16[1024,128]{1,0:T(8,128)(2,1)S(1)}, bf16[1024,128]{1,0:T(8,128)(2,1)S(1)}, u32[]{:S(2)}, u32[]{:S(2)}) collective-permute-start(bf16[1024,128]{1,0:T(8,128)(2,1)S(1)} %collective-permute-done.1), channel_id=1, source_target_pairs={{0,252},{1,253},{2,254},{3,255},{4,0},{5,1},{6,2},{7,3},{8,4},{9,5... | collective-permute-start | bytes 786440 | tf_op jit(solution)/shard_map/ppermute | solution.py:29
  25.7 1.8 %collective-permute-start.5 = (bf16[1024,128]{1,0:T(8,128)(2,1)S(1)}, bf16[1024,128]{1,0:T(8,128)(2,1)S(1)}, u32[]{:S(2)}, u32[]{:S(2)}) collective-permute-start(bf16[1024,128]{1,0:T(8,128)(2,1)S(1)} %collective-permute-done), channel_id=1, source_target_pairs={{0,1},{1,0},{2,3},{3,2},{4,5},{5,4},{6,7},{7,6},{8,9},{9,8},{10,11... | collective-permute-start | bytes 786440 | tf_op jit(solution)/shard_map/ppermute | solution.py:29
  27.6 2.4 %collective-permute-done.2 = bf16[1024,128]{1,0:T(8,128)(2,1)S(1)} collective-permute-done((bf16[1024,128]{1,0:T(8,128)(2,1)S(1)}, bf16[1024,128]{1,0:T(8,128)(2,1)S(1)}, u32[]{:S(2)}, u32[]{:S(2)}) %collective-permute-start.2) | collective-permute-done | bytes 262176 | tf_op jit(solution)/shard_map/ppermute | solution.py:29
  30.0 2.1 %collective-permute-start.9 = (bf16[1024,128]{1,0:T(8,128)(2,1)S(1)}, bf16[1024,128]{1,0:T(8,128)(2,1)S(1)}, u32[]{:S(2)}, u32[]{:S(2)}) collective-permute-start(bf16[1024,128]{1,0:T(8,128)(2,1)S(1)} %collective-permute-done.3), channel_id=1, source_target_pairs={{0,1},{1,0},{2,3},{3,2},{4,5},{5,4},{6,7},{7,6},{8,9},{9,8},{10,11... | collective-permute-start | bytes 786440 | tf_op jit(solution)/shard_map/ppermute | solution.py:29
  35.4 10.7 %forward.1 = (bf16[1024,512]{1,0:T(8,128)(2,1)}, bf16[128,1024]{1,0:T(8,128)(2,1)S(1)}, f32[8,8,640]{2,1,0:T(8,128)S(1)}, f32[8,8,640]{2,1,0:T(8,128)S(1)}) custom-call(s32[8,32]{1,0:T(8,128)S(1)} %fusion.7.place_ref, s32[1]{0:T(128)} %bitcast.core_ref, bf16[104,128,128]{2,1,0:T(8,128)(2,1)S(1)} %bitcast.46, bf16[1024,4096]{1,0:T(8,128)(2,1)} %source_ref.3, ...), custom_call_target="tpu_custom_call" | custom-call | flops 3221225472 | bytes 15728640 | tf_op jit(solution)/shard_map/forward/pallas_call | solution.py:193
  46.1 6.6 %backward.1 = (bf16[48,128,128]{2,1,0:T(8,128)(2,1)S(1)}, bf16[48,128,128]{2,1,0:T(8,128)(2,1)S(1)}) custom-call(s32[8,32]{1,0:T(8,128)S(1)} %fusion.7.place_ref, bf16[128,1024]{1,0:T(8,128)(2,1)S(1)} %get-tuple-element.17.back_ref, bf16[1024,4096]{1,0:T(8,128)(2,1)} %source_ref.3), custom_call_target="tpu_custom_call" | custom-call | flops 2147483648 | bytes 12582912 | tf_op jit(solution)/shard_map/backward/pallas_call | solution.py:247
  53.3 3.1 %collective-permute-done.11 = f32[8,8,640]{2,1,0:T(8,128)S(1)} collective-permute-done((f32[8,8,640]{2,1,0:T(8,128)S(1)}, f32[8,8,640]{2,1,0:T(8,128)S(1)}, u32[]{:S(2)}, u32[]{:S(2)}) %collective-permute-start.11) | collective-permute-done | bytes 163872 | tf_op jit(solution)/shard_map/ppermute | solution.py:29
  56.4 9.7 %all_to_all.15 = f32[8,8,640]{2,1,0:T(8,128)S(1)} all-to-all(f32[8,8,640]{2,1,0:T(8,128)S(1)} %add.56), channel_id=1, replica_groups=mesh['y_lo'=2,'z'=8,'x'=4,'y_hi'=2,'core'=2] {'x','y_hi'}, dimensions={0} | all-to-all | bytes 327680 | tf_op jit(solution)/shard_map/all_to_all | solution.py:253
  66.2 2.7 %add_convert_fusion.1 = (bf16[16,128,128]{2,1,0:T(8,128)(2,1)}, bf16[16,128,128]{2,1,0:T(8,128)(2,1)S(1)}, f32[16,128,128]{2,1,0:T(8,128)S(1)}) fusion(bf16[48,128,128]{2,1,0:T(8,128)(2,1)} %collective-permute-done.12, bf16[48,128,128]{2,1,0:T(8,128)(2,1)S(1)} %get-tuple-element.20), kind=kLoop, calls=%fused_computation.2 | loop fusion | flops 2883584 | bytes 5242880 | tf_op jit(solution)/shard_map/convert_element_type | solution.py:259
  68.9 5.6 %collective-permute-start.14 = (bf16[2,8,128,128]{3,2,1,0:T(8,128)(2,1)S(1)}, bf16[2,8,128,128]{3,2,1,0:T(8,128)(2,1)}, u32[]{:S(2)}, u32[]{:S(2)}) collective-permute-start(bf16[2,8,128,128]{3,2,1,0:T(8,128)(2,1)S(1)} %bitcast.49), channel_id=1, source_target_pairs={{0,252},{1,253},{2,254},{3,255},{4,0},{5,1},{6,2},{7,3},{8,4},{9,5... | collective-permute-start | bytes 1572872 | tf_op jit(solution)/shard_map/ppermute | solution.py:29
  75.3 4.0 %all-to-all-start.1 = ((f32[16,8,640]{2,1,0:T(8,128)}), f32[16,8,640]{2,1,0:T(8,128)S(1)}, u32[]{:S(2)}, u32[]{:S(2)}) async-start(f32[16,8,640]{2,1,0:T(8,128)} %broadcast_in_dim.9), calls=%async_computation.1 | async-start | bytes 655360 | tf_op jit(solution)/shard_map/all_to_all | solution.py:47
  79.2 6.2 %collective-permute-done.13 = bf16[2,8,128,128]{3,2,1,0:T(8,128)(2,1)} collective-permute-done((bf16[2,8,128,128]{3,2,1,0:T(8,128)(2,1)}, bf16[2,8,128,128]{3,2,1,0:T(8,128)(2,1)}, u32[]{:S(2)}, u32[]{:S(2)}) %collective-permute-start.13) | collective-permute-done | bytes 524320 | tf_op jit(solution)/shard_map/ppermute | solution.py:29
  85.5 1.2 %collective-permute-done.14 = bf16[2,8,128,128]{3,2,1,0:T(8,128)(2,1)} collective-permute-done((bf16[2,8,128,128]{3,2,1,0:T(8,128)(2,1)S(1)}, bf16[2,8,128,128]{3,2,1,0:T(8,128)(2,1)}, u32[]{:S(2)}, u32[]{:S(2)}) %collective-permute-start.14) | collective-permute-done | bytes 524320 | tf_op jit(solution)/shard_map/ppermute | solution.py:29
  86.7 1.4 %add_bitcast_fusion = f32[2,8,128,128]{2,3,1,0:T(8,128)S(1)} fusion(bf16[2,8,128,128]{3,2,1,0:T(8,128)(2,1)} %collective-permute-done.14, f32[2,8,128,128]{3,2,1,0:T(8,128)S(1)} %bitcast.48, bf16[2,8,128,128]{3,2,1,0:T(8,128)(2,1)} %collective-permute-done.13), kind=kLoop, calls=%fused_computation | loop fusion | flops 1048576 | bytes 3145728 | tf_op jit(solution)/shard_map/transpose | solution.py:263
  88.1 2.8 %all-to-all-done.1 = f32[16,8,640]{2,1,0:T(8,128)S(1)} async-done(((f32[16,8,640]{2,1,0:T(8,128)}), f32[16,8,640]{2,1,0:T(8,128)S(1)}, u32[]{:S(2)}, u32[]{:S(2)}) %all-to-all-start.1) | async-done | bytes 327712 | tf_op jit(solution)/shard_map/all_to_all | solution.py:47
  91.6 6.3 %all-to-all-start.2 = ((f32[8,8,512]{2,1,0:T(8,128)}), f32[8,8,512]{2,1,0:T(8,128)S(1)}, u32[]{:S(2)}, u32[]{:S(2)}) async-start(f32[8,8,512]{2,1,0:T(8,128)} %broadcast_in_dim.10), calls=%async_computation.2 | async-start | bytes 262144 | tf_op jit(solution)/shard_map/all_to_all | solution.py:47
  97.9 3.1 %collective-permute-start.15 = (bf16[8,128,128]{1,2,0:T(8,128)(2,1)S(1)}, bf16[8,128,128]{1,2,0:T(8,128)(2,1)S(1)}, u32[]{:S(2)}, u32[]{:S(2)}) collective-permute-start(bf16[8,128,128]{1,2,0:T(8,128)(2,1)S(1)} %fusion), channel_id=1, source_target_pairs={{0,2},{1,3},{2,0},{3,1},{4,6},{5,7},{6,4},{7,5},{8,10},{9,11},{10,... | collective-permute-start | bytes 786440 | tf_op jit(solution)/shard_map/ppermute | solution.py:29
  101.0 3.8 %all-to-all-done.2 = f32[8,8,512]{2,1,0:T(8,128)S(1)} async-done(((f32[8,8,512]{2,1,0:T(8,128)}), f32[8,8,512]{2,1,0:T(8,128)S(1)}, u32[]{:S(2)}, u32[]{:S(2)}) %all-to-all-start.2) | async-done | bytes 131104 | tf_op jit(solution)/shard_map/all_to_all | solution.py:47
  104.7 4.0 %collective-permute-start.16 = (f32[8,8,512]{2,1,0:T(8,128)S(1)}, f32[8,8,512]{2,1,0:T(8,128)S(1)}, u32[]{:S(2)}, u32[]{:S(2)}) collective-permute-start(f32[8,8,512]{2,1,0:T(8,128)S(1)} %all-to-all-done.2), channel_id=1, source_target_pairs={{0,1},{1,0},{2,3},{3,2},{4,5},{5,4},{6,7},{7,6},{8,9},{9,8},{10,11... | collective-permute-start | bytes 393224 | tf_op jit(solution)/shard_map/ppermute | solution.py:29
  110.5 1.0 copy.13
  (51 shorter events, 8.0 us)
Async XLA Ops:
  0.6 34.7 %copy-start.2 = (f32[512]{0:T(512)S(1)}, f32[512]{0:T(512)}, u32[]{:S(2)}) copy-start(f32[512]{0:T(512)} %param.9) | copy-start | bytes 6148
  0.6 34.7 %copy-start = (bf16[1024,512]{1,0:T(8,128)(2,1)S(1)}, bf16[1024,512]{1,0:T(8,128)(2,1)}, u32[]{:S(2)}) copy-start(bf16[1024,512]{1,0:T(8,128)(2,1)} %grad_ref.1) | copy-start | bytes 3145732
  0.7 34.7 %copy-start.1 = (bf16[128,512]{1,0:T(8,128)(2,1)S(1)}, bf16[128,512]{1,0:T(8,128)(2,1)}, u32[]{:S(2)}) copy-start(bf16[128,512]{1,0:T(8,128)(2,1)} %weight_ref.1) | copy-start | bytes 393220
  0.7 12.9 %collective-permute-start.1 = (bf16[1024,128]{1,0:T(8,128)(2,1)}, bf16[1024,128]{1,0:T(8,128)(2,1)S(1)}, u32[]{:S(2)}, u32[]{:S(2)}) collective-permute-start(bf16[1024,128]{1,0:T(8,128)(2,1)} %param.7), channel_id=1, source_target_pairs={{0,2},{1,3},{2,0},{3,1},{4,6},{5,7},{6,4},{7,5},{8,10},{9,11},{10,... | collective-permute-start | bytes 786440 | tf_op jit(solution)/shard_map/ppermute | solution.py:29
  4.5 21.2 %collective-permute-start = (bf16[1024,128]{1,0:T(8,128)(2,1)}, bf16[1024,128]{1,0:T(8,128)(2,1)S(1)}, u32[]{:S(2)}, u32[]{:S(2)}) collective-permute-start(bf16[1024,128]{1,0:T(8,128)(2,1)} %param.7), channel_id=1, source_target_pairs={{0,4},{1,5},{2,6},{3,7},{4,8},{5,9},{6,10},{7,11},{8,12},{9,13},{1... | collective-permute-start | bytes 786440 | tf_op jit(solution)/shard_map/ppermute | solution.py:29
  5.7 21.8 %collective-permute-start.3 = (bf16[1024,128]{1,0:T(8,128)(2,1)}, bf16[1024,128]{1,0:T(8,128)(2,1)S(1)}, u32[]{:S(2)}, u32[]{:S(2)}) collective-permute-start(bf16[1024,128]{1,0:T(8,128)(2,1)} %param.7), channel_id=1, source_target_pairs={{0,252},{1,253},{2,254},{3,255},{4,0},{5,1},{6,2},{7,3},{8,4},{9,5... | collective-permute-start | bytes 786440 | tf_op jit(solution)/shard_map/ppermute | solution.py:29
  12.4 22.6 %collective-permute-start.7 = (bf16[1024,128]{1,0:T(8,128)(2,1)}, bf16[1024,128]{1,0:T(8,128)(2,1)S(1)}, u32[]{:S(2)}, u32[]{:S(2)}) collective-permute-start(bf16[1024,128]{1,0:T(8,128)(2,1)} %param.7), channel_id=1, source_target_pairs={{0,1},{1,0},{2,3},{3,2},{4,5},{5,4},{6,7},{7,6},{8,9},{9,8},{10,11... | collective-permute-start | bytes 786440 | tf_op jit(solution)/shard_map/ppermute | solution.py:29
  13.6 16.4 %collective-permute-start.2 = (bf16[1024,128]{1,0:T(8,128)(2,1)S(1)}, bf16[1024,128]{1,0:T(8,128)(2,1)S(1)}, u32[]{:S(2)}, u32[]{:S(2)}) collective-permute-start(bf16[1024,128]{1,0:T(8,128)(2,1)S(1)} %collective-permute-done.1), channel_id=1, source_target_pairs={{0,4},{1,5},{2,6},{3,7},{4,8},{5,9},{6,10},{7,11},{8,12},{9,13},{1... | collective-permute-start | bytes 786440 | tf_op jit(solution)/shard_map/ppermute | solution.py:29
  14.4 18.9 %collective-permute-start.4 = (bf16[1024,128]{1,0:T(8,128)(2,1)S(1)}, bf16[1024,128]{1,0:T(8,128)(2,1)S(1)}, u32[]{:S(2)}, u32[]{:S(2)}) collective-permute-start(bf16[1024,128]{1,0:T(8,128)(2,1)S(1)} %collective-permute-done.1), channel_id=1, source_target_pairs={{0,252},{1,253},{2,254},{3,255},{4,0},{5,1},{6,2},{7,3},{8,4},{9,5... | collective-permute-start | bytes 786440 | tf_op jit(solution)/shard_map/ppermute | solution.py:29
  25.7 7.7 %collective-permute-start.5 = (bf16[1024,128]{1,0:T(8,128)(2,1)S(1)}, bf16[1024,128]{1,0:T(8,128)(2,1)S(1)}, u32[]{:S(2)}, u32[]{:S(2)}) collective-permute-start(bf16[1024,128]{1,0:T(8,128)(2,1)S(1)} %collective-permute-done), channel_id=1, source_target_pairs={{0,1},{1,0},{2,3},{3,2},{4,5},{5,4},{6,7},{7,6},{8,9},{9,8},{10,11... | collective-permute-start | bytes 786440 | tf_op jit(solution)/shard_map/ppermute | solution.py:29
  27.5 7.5 %collective-permute-start.8 = (bf16[1024,128]{1,0:T(8,128)(2,1)S(1)}, bf16[1024,128]{1,0:T(8,128)(2,1)S(1)}, u32[]{:S(2)}, u32[]{:S(2)}) collective-permute-start(bf16[1024,128]{1,0:T(8,128)(2,1)S(1)} %collective-permute-done.1), channel_id=1, source_target_pairs={{0,1},{1,0},{2,3},{3,2},{4,5},{5,4},{6,7},{7,6},{8,9},{9,8},{10,11... | collective-permute-start | bytes 786440 | tf_op jit(solution)/shard_map/ppermute | solution.py:29
  30.0 5.0 %collective-permute-start.9 = (bf16[1024,128]{1,0:T(8,128)(2,1)S(1)}, bf16[1024,128]{1,0:T(8,128)(2,1)S(1)}, u32[]{:S(2)}, u32[]{:S(2)}) collective-permute-start(bf16[1024,128]{1,0:T(8,128)(2,1)S(1)} %collective-permute-done.3), channel_id=1, source_target_pairs={{0,1},{1,0},{2,3},{3,2},{4,5},{5,4},{6,7},{7,6},{8,9},{9,8},{10,11... | collective-permute-start | bytes 786440 | tf_op jit(solution)/shard_map/ppermute | solution.py:29
  33.3 1.6 %collective-permute-start.6 = (bf16[1024,128]{1,0:T(8,128)(2,1)S(1)}, bf16[1024,128]{1,0:T(8,128)(2,1)S(1)}, u32[]{:S(2)}, u32[]{:S(2)}) collective-permute-start(bf16[1024,128]{1,0:T(8,128)(2,1)S(1)} %collective-permute-done.2), channel_id=1, source_target_pairs={{0,1},{1,0},{2,3},{3,2},{4,5},{5,4},{6,7},{7,6},{8,9},{9,8},{10,11... | collective-permute-start | bytes 786440 | tf_op jit(solution)/shard_map/ppermute | solution.py:29
  33.4 1.8 %collective-permute-start.10 = (bf16[1024,128]{1,0:T(8,128)(2,1)S(1)}, bf16[1024,128]{1,0:T(8,128)(2,1)S(1)}, u32[]{:S(2)}, u32[]{:S(2)}) collective-permute-start(bf16[1024,128]{1,0:T(8,128)(2,1)S(1)} %collective-permute-done.4), channel_id=1, source_target_pairs={{0,1},{1,0},{2,3},{3,2},{4,5},{5,4},{6,7},{7,6},{8,9},{9,8},{10,11... | collective-permute-start | bytes 786440 | tf_op jit(solution)/shard_map/ppermute | solution.py:29
  52.7 13.5 %collective-permute-start.12 = (bf16[48,128,128]{2,1,0:T(8,128)(2,1)S(1)}, bf16[48,128,128]{2,1,0:T(8,128)(2,1)}, u32[]{:S(2)}, u32[]{:S(2)}) collective-permute-start(bf16[48,128,128]{2,1,0:T(8,128)(2,1)S(1)} %get-tuple-element.18), channel_id=1, source_target_pairs={{0,1},{1,0},{2,3},{3,2},{4,5},{5,4},{6,7},{7,6},{8,9},{9,8},{10,11... | collective-permute-start | bytes 4718600 | tf_op jit(solution)/shard_map/ppermute | solution.py:29
  53.0 3.4 %collective-permute-start.11 = (f32[8,8,640]{2,1,0:T(8,128)S(1)}, f32[8,8,640]{2,1,0:T(8,128)S(1)}, u32[]{:S(2)}, u32[]{:S(2)}) collective-permute-start(f32[8,8,640]{2,1,0:T(8,128)S(1)} %get-tuple-element.16), channel_id=1, source_target_pairs={{0,1},{1,0},{2,3},{3,2},{4,5},{5,4},{6,7},{7,6},{8,9},{9,8},{10,11... | collective-permute-start | bytes 491528 | tf_op jit(solution)/shard_map/ppermute | solution.py:29
  68.8 16.6 %collective-permute-start.13 = (bf16[2,8,128,128]{3,2,1,0:T(8,128)(2,1)}, bf16[2,8,128,128]{3,2,1,0:T(8,128)(2,1)}, u32[]{:S(2)}, u32[]{:S(2)}) collective-permute-start(bf16[2,8,128,128]{3,2,1,0:T(8,128)(2,1)} %bitcast.16), channel_id=1, source_target_pairs={{0,4},{1,5},{2,6},{3,7},{4,8},{5,9},{6,10},{7,11},{8,12},{9,13},{1... | collective-permute-start | bytes 1572872 | tf_op jit(solution)/shard_map/ppermute | solution.py:29
  68.9 17.8 %collective-permute-start.14 = (bf16[2,8,128,128]{3,2,1,0:T(8,128)(2,1)S(1)}, bf16[2,8,128,128]{3,2,1,0:T(8,128)(2,1)}, u32[]{:S(2)}, u32[]{:S(2)}) collective-permute-start(bf16[2,8,128,128]{3,2,1,0:T(8,128)(2,1)S(1)} %bitcast.49), channel_id=1, source_target_pairs={{0,252},{1,253},{2,254},{3,255},{4,0},{5,1},{6,2},{7,3},{8,4},{9,5... | collective-permute-start | bytes 1572872 | tf_op jit(solution)/shard_map/ppermute | solution.py:29
  75.3 15.6 %all-to-all-start.1 = ((f32[16,8,640]{2,1,0:T(8,128)}), f32[16,8,640]{2,1,0:T(8,128)S(1)}, u32[]{:S(2)}, u32[]{:S(2)}) async-start(f32[16,8,640]{2,1,0:T(8,128)} %broadcast_in_dim.9), calls=%async_computation.1 | async-start | bytes 655360 | tf_op jit(solution)/shard_map/all_to_all | solution.py:47
  91.6 13.1 %all-to-all-start.2 = ((f32[8,8,512]{2,1,0:T(8,128)}), f32[8,8,512]{2,1,0:T(8,128)S(1)}, u32[]{:S(2)}, u32[]{:S(2)}) async-start(f32[8,8,512]{2,1,0:T(8,128)} %broadcast_in_dim.10), calls=%async_computation.2 | async-start | bytes 262144 | tf_op jit(solution)/shard_map/all_to_all | solution.py:47
  97.9 12.5 %collective-permute-start.15 = (bf16[8,128,128]{1,2,0:T(8,128)(2,1)S(1)}, bf16[8,128,128]{1,2,0:T(8,128)(2,1)S(1)}, u32[]{:S(2)}, u32[]{:S(2)}) collective-permute-start(bf16[8,128,128]{1,2,0:T(8,128)(2,1)S(1)} %fusion), channel_id=1, source_target_pairs={{0,2},{1,3},{2,0},{3,1},{4,6},{5,7},{6,4},{7,5},{8,10},{9,11},{10,... | collective-permute-start | bytes 786440 | tf_op jit(solution)/shard_map/ppermute | solution.py:29
  104.7 4.9 %collective-permute-start.16 = (f32[8,8,512]{2,1,0:T(8,128)S(1)}, f32[8,8,512]{2,1,0:T(8,128)S(1)}, u32[]{:S(2)}, u32[]{:S(2)}) collective-permute-start(f32[8,8,512]{2,1,0:T(8,128)S(1)} %all-to-all-done.2), channel_id=1, source_target_pairs={{0,1},{1,0},{2,3},{3,2},{4,5},{5,4},{6,7},{7,6},{8,9},{9,8},{10,11... | collective-permute-start | bytes 393224 | tf_op jit(solution)/shard_map/ppermute | solution.py:29
where the time goes:
time: 112 us; the launch traced here: 111 us
  starting transfers between devices  52.4 us (47%)
  waiting for transfers between devices  21.1 us (19%)
  Pallas kernels  17.3 us (15%)
  blocking collectives  9.7 us (9%)
  other arithmetic  5.64 us (5%)
  local copies, waits for them, and re-layouts  4.45 us (4%)
    ppermute x17, starting transfers between devices, sent(): lax.ppermute(value, AXES, [(source, target(source, count)) for source in...  42.2 us
    ppermute x17, waiting for transfers between devices, sent(): lax.ppermute(value, AXES, [(source, target(source, count)) for source in...  14.5 us
    pallas_call x1, Pallas kernels, layer(): pl.pallas_call(functools.partial(forward_kernel, factor), out_shape=(jax....  10.7 us
    all_to_all x2, starting transfers between devices, to_all(): return lax.all_to_all(copies, axes, 0, 0, tiled=True)  10.2 us
    all_to_all x1, blocking collectives, layer(): part = jnp.sum(lax.all_to_all(part, NEAR, 0, 0, tiled=True), axis=0)  9.7 us
    all_to_all x2, waiting for transfers between devices, to_all(): return lax.all_to_all(copies, axes, 0, 0, tiled=True)  6.58 us
    pallas_call x1, Pallas kernels, layer(): keep, send = backward(place, back, tile_values)  6.57 us
    convert_element_type x1, other arithmetic, layer(): moved.append(to_block(term.astype(jnp.bfloat16), steps))  2.67 us
  transfers between devices with their start and end apart: 19, of which 9 were waited for; matrix products, arithmetic and copies ran while one was open for 5% of the time, Pallas kernels for 0%

commit v1 on v0

--- a/solution.py
+++ b/solution.py
@@ -57,36 +57,50 @@
     return (value_part, slope)
 
 
-def streamed(step, source_ref, held_ref, arrived):
-    def copy(tile):
-        rows = pl.ds(pl.multiple_of(tile * TILE, TILE), TILE)
-        return pltpu.make_async_copy(source_ref.at[rows], held_ref.at[tile], arrived.at[tile])
-
-    @pl.when(step == 0)
-    def _():
-        for tile in range(held_ref.shape[0]):
-            copy(tile).start()
-
-    copy(step).wait()
-    return held_ref.at[step]
+def load_kernel(source_ref, held_ref, arrived):
+    count = arrived.shape[0]
+    rows = source_ref.shape[0] // count
+    copies = [
+        pltpu.make_async_copy(
+            source_ref.at[pl.ds(i * rows, rows)], held_ref.at[pl.ds(i * rows, rows)], arrived.at[i]
+        )
+        for i in range(count)
+    ]
+    for copy in copies:
+        copy.start()
+    for copy in copies:
+        copy.wait()
+
+
+def merge_kernel(keep_ref, core_ref, up_ref, down_ref, own_ref, other_ref):
+    for row in range(2):
+        for tile in range(PIECE_TILES):
+            refs = (keep_ref.at[1], core_ref.at[1], up_ref, down_ref)
+            terms = [ref[row, tile].astype(jnp.float32) for ref in refs]
+            total = jnp.swapaxes(terms[0] + terms[1] + terms[2] + terms[3], 0, 1)
+            rows = slice(tile * TILE, (tile + 1) * TILE)
+            if row == 0:
+                own_ref[rows, :] = total
+            else:
+                other_ref[rows, :] = total.astype(jnp.bfloat16)
 
 
 def forward_kernel(
-    factor, place_ref, core_ref, window_ref, source_ref, grad_ref, weight_ref, bias_ref,
-    act_ref, back_ref, own_ref, other_ref, agg_ref, pre_ref, bias_sum_ref, held_ref, arrived,
+    factor, place_ref, core_ref, window_ref, values_ref, grad_ref, weight_ref, bias_ref,
+    act_ref, back_ref, own_ref, other_ref, agg_ref, pre_ref, bias_sum_ref,
 ):
     step = pl.program_id(0)
-    values_ref = streamed(step, source_ref, held_ref, arrived)
     weight = weight_ref[...]
     for sub in range(STEP_TILES):
         rows = slice(sub * TILE, (sub + 1) * TILE)
         tile = step * STEP_TILES + sub
+        place = pl.ds(pl.multiple_of(tile * TILE, TILE), TILE)
         total = None
         for pair in range(SLOTS // 2):
             one = window_ref[place_ref[tile, 2 * pair]]
             two = window_ref[place_ref[tile, 2 * pair + 1]]
             term = jnp.dot(
-                values_ref[:, 2 * pair * TILE : (2 * pair + 2) * TILE],
+                values_ref[place, 2 * pair * TILE : (2 * pair + 2) * TILE],
                 jnp.concatenate([one, two], axis=0),
                 preferred_element_type=jnp.float32,
             )
@@ -99,7 +113,6 @@
         back_ref[:, rows] = lax.dot_general(
             weight, pre_wide, (((1,), (1,)), ((), ())), preferred_element_type=jnp.float32
         ).astype(jnp.bfloat16)
-        place = pl.ds(pl.multiple_of(tile * TILE, TILE), TILE)
         agg_ref[place, :] = aggregated
         pre_ref[place, :] = pre_wide
         part = jnp.sum(pre_wide.astype(jnp.float32).reshape(TILE // 8, 8, -1), axis=0)
@@ -126,10 +139,9 @@
 
 
 def backward_kernel(
-    place_ref, back_ref, source_ref, keep_ref, send_ref, total_ref, held_ref, arrived
+    place_ref, back_ref, values_ref, keep_ref, send_ref, total_ref
 ):
     step = pl.program_id(0)
-    values_ref = streamed(step, source_ref, held_ref, arrived)
 
     @pl.when(step == 0)
     def _():
@@ -138,10 +150,12 @@
     for sub in range(STEP_TILES):
         rows = slice(sub * TILE, (sub + 1) * TILE)
         back = back_ref[:, rows]
+        tile = step * STEP_TILES + sub
+        place = pl.ds(pl.multiple_of(tile * TILE, TILE), TILE)
         for pair in range(SLOTS // 2):
             term = jnp.dot(
                 back,
-                values_ref[:, 2 * pair * TILE : (2 * pair + 2) * TILE],
+                values_ref[place, 2 * pair * TILE : (2 * pair + 2) * TILE],
                 preferred_element_type=jnp.float32,
             )
             for half in range(2):
@@ -170,7 +184,9 @@
     other_row = to_row(features)
     pieces = {0: (features, other_row)}
     for steps in (1, -1):
-        pieces[-steps] = (to_block(features, steps), to_block(other_row, steps))
+        near = to_block(features, steps)
+        far = to_block(other_row, steps)
+        pieces[-steps] = (near, far)
     near = [piece for offset in (-1, 0, 1) for piece in pieces[offset]]
     far = [to_core(piece) for piece in near]
     blank = jnp.zeros_like(features)
@@ -184,11 +200,17 @@
     is_live = jnp.arange(SLOTS)[None, :] < tile_counts[:, None]
     place = jnp.where(is_live, place, DUMMY).astype(jnp.int32)
 
-    tile_values = pltpu.with_memory_space_constraint(tile_values, pltpu.HBM)
-    held = [
-        pltpu.VMEM((row_tiles, TILE, SLOTS * TILE), jnp.bfloat16),
-        pltpu.SemaphoreType.DMA((row_tiles,)),
-    ]
+    load = pl.pallas_call(
+        load_kernel,
+        out_shape=pltpu.VMEM(tile_values.shape, tile_values.dtype),
+        in_specs=[pl.BlockSpec(memory_space=pltpu.HBM)],
+        out_specs=pl.BlockSpec(memory_space=pltpu.VMEM),
+        scratch_shapes=[pltpu.SemaphoreType.DMA((row_tiles,))],
+        compiler_params=pltpu.CompilerParams(vmem_limit_bytes=1 << 20),
+        cost_estimate=pl.CostEstimate(flops=0, bytes_accessed=16 << 20, transcendentals=0),
+        name="load",
+    )
+    tile_values = load(tile_values)
     whole = lambda *shape: pl.BlockSpec(shape, lambda i, *_: (0,) * len(shape))
     act, back, own_sums, other_sums = pl.pallas_call(
         functools.partial(forward_kernel, factor),
@@ -203,7 +225,7 @@
             grid=(row_tiles // STEP_TILES,),
             in_specs=[
                 whole(*window.shape),
-                pl.BlockSpec(memory_space=pltpu.HBM),
+                pl.BlockSpec(memory_space=pltpu.VMEM),
                 pl.BlockSpec((step_rows, out_dim), lambda i, *_: (i, 0)),
                 whole(in_dim, out_dim),
                 whole(1, out_dim),
@@ -218,7 +240,6 @@
                 pltpu.VMEM((rows_dev, in_dim), jnp.bfloat16),
                 pltpu.VMEM((rows_dev, out_dim), jnp.bfloat16),
                 pltpu.VMEM((row_tiles * 8, out_dim), jnp.float32),
-                *held,
             ],
         ),
         compiler_params=pltpu.CompilerParams(vmem_limit_bytes=VMEM_LIMIT),
@@ -235,10 +256,10 @@
             grid=(row_tiles // STEP_TILES,),
             in_specs=[
                 pl.BlockSpec((in_dim, step_rows), lambda i, *_: (0, i)),
-                pl.BlockSpec(memory_space=pltpu.HBM),
+                pl.BlockSpec(memory_space=pltpu.VMEM),
             ],
             out_specs=(whole(half_tiles, in_dim, TILE),) * 2,
-            scratch_shapes=[pltpu.VMEM((DUMMY + 1, in_dim, TILE), jnp.float32), *held],
+            scratch_shapes=[pltpu.VMEM((DUMMY + 1, in_dim, TILE), jnp.float32)],
         ),
         compiler_params=pltpu.CompilerParams(vmem_limit_bytes=VMEM_LIMIT),
         cost_estimate=pl.CostEstimate(flops=2 << 30, bytes_accessed=12 << 20, transcendentals=0),
@@ -259,15 +280,23 @@
         moved.append(to_block(term.astype(jnp.bfloat16), steps))
     part = jnp.sum(to_all(part, FAR), axis=0)
     bias_grad = part[: out_dim // TILE, out_dim:].reshape(out_dim)
-    total = wide(keep[1]) + wide(from_core[1]) + wide(moved[0]) + wide(moved[1])
-    part, total = lax.optimization_barrier((part, jnp.swapaxes(total, 2, 3)))
-    last = to_row(total[1].astype(jnp.bfloat16))
+    own, other = pl.pallas_call(
+        merge_kernel,
+        out_shape=(
+            jax.ShapeDtypeStruct((rows_dev, in_dim), jnp.float32),
+            jax.ShapeDtypeStruct((rows_dev, in_dim), jnp.bfloat16),
+        ),
+        compiler_params=pltpu.CompilerParams(vmem_limit_bytes=16 << 20),
+        cost_estimate=pl.CostEstimate(flops=1 << 20, bytes_accessed=4 << 20, transcendentals=0),
+        name="merge",
+    )(keep, from_core, moved[0], moved[1])
+    last = to_row(other)
     mine = to_all(part[:, :out_dim], NEAR)
     theirs = to_core(mine)
     odd = core == 1
     weight_grad = jnp.stack([jnp.where(odd, theirs, mine), jnp.where(odd, mine, theirs)], axis=1)
     weight_grad = weight_grad.reshape(in_dim, out_dim)
-    feature_grad = (total[0] + wide(last)).reshape(rows_dev, in_dim)
+    feature_grad = own + wide(last)
     return (act, feature_grad, weight_grad, bias_grad)
 
 

time: 112 us -> 119 us (1.062)
  waiting for transfers between devices: 21.1 us -> 28.2 us
  local copies, waits for them, and re-layouts: 4.45 us -> 6.64 us
  starting transfers between devices: 52.4 us -> 51 us
    ppermute x17, waiting for transfers between devices: 14.5 us -> 22.1 us  [sent(): lax.ppermute(value, AXES, [(source, target(source, count)) for source in...]
    unnamed x18 -> x24, local copies, waits for them, and re-layouts: 1.38 us -> 4.6 us
    convert_element_type x1, other arithmetic: 2.67 us -> 0.37 us  [layer(): moved.append(to_block(term.astype(jnp.bfloat16), steps))]
    add x1, other arithmetic: 0.05 us -> 1.88 us  [layer(): feature_grad = own + wide(last)]
    ppermute x17, starting transfers between devices: 42.2 us -> 40.4 us  [sent(): lax.ppermute(value, AXES, [(source, target(source, count)) for source in...]
    pallas_call x1, Pallas kernels: 10.7 us -> 9.24 us  [layer(): pl.pallas_call(functools.partial(forward_kernel, factor), out_shape=(jax....]
    transpose x1 -> x0, other arithmetic: 1.37 us -> none  [layer(): part, total = lax.optimization_barrier((part, jnp.swapaxes(total, 2, 3)))]
  transfers between devices with their start and end apart: 19 -> 19, of which waited for: 9 -> 6; matrix products, arithmetic and copies ran while one was open for 5% -> 5% of each run, Pallas kernels for 0% -> 1%
where the time goes in v1:
time: 119 us; the launch traced here: 118 us
  starting transfers between devices  51 us (43%)
  waiting for transfers between devices  28.2 us (24%)
  Pallas kernels  16.6 us (14%)
  blocking collectives  9.97 us (8%)
  local copies, waits for them, and re-layouts  6.64 us (6%)
  other arithmetic  4.78 us (4%)
    ppermute x17, starting transfers between devices, sent(): lax.ppermute(value, AXES, [(source, target(source, count)) for source in...  40.4 us
    ppermute x17, waiting for transfers between devices, sent(): lax.ppermute(value, AXES, [(source, target(source, count)) for source in...  22.1 us
    all_to_all x2, starting transfers between devices, to_all(): return lax.all_to_all(copies, axes, 0, 0, tiled=True)  10.6 us
    all_to_all x1, blocking collectives, layer(): part = jnp.sum(lax.all_to_all(part, NEAR, 0, 0, tiled=True), axis=0)  9.97 us
    pallas_call x1, Pallas kernels, layer(): pl.pallas_call(functools.partial(forward_kernel, factor), out_shape=(jax....  9.24 us
    pallas_call x1, Pallas kernels, layer(): keep, send = backward(place, back, tile_values)  6.42 us
    all_to_all x2, waiting for transfers between devices, to_all(): return lax.all_to_all(copies, axes, 0, 0, tiled=True)  6.14 us
    unnamed x24, local copies, waits for them, and re-layouts  4.6 us
  transfers between devices with their start and end apart: 19, of which 6 were waited for; matrix products, arithmetic and copies ran while one was open for 5% of the time, Pallas kernels for 1%

profile of v1, /device:TPU:1, one launch (start us, length us, event | category | flops | bytes accessed | tf_op | source)
XLA Modules:
  0.0 118.2 jit_solution(18340060816890576769)
XLA Ops:
  0.6 3.8 %collective-permute-start.1 = (bf16[1024,128]{1,0:T(8,128)(2,1)}, bf16[1024,128]{1,0:T(8,128)(2,1)S(1)}, u32[]{:S(2)}, u32[]{:S(2)}) collective-permute-start(bf16[1024,128]{1,0:T(8,128)(2,1)} %param.7), channel_id=1, source_target_pairs={{0,2},{1,3},{2,0},{3,1},{4,6},{5,7},{6,4},{7,5},{8,10},{9,11},{10,... | collective-permute-start | bytes 786440 | tf_op jit(solution)/shard_map/ppermute | solution.py:29
  4.5 1.2 %collective-permute-start = (bf16[1024,128]{1,0:T(8,128)(2,1)}, bf16[1024,128]{1,0:T(8,128)(2,1)S(1)}, u32[]{:S(2)}, u32[]{:S(2)}) collective-permute-start(bf16[1024,128]{1,0:T(8,128)(2,1)} %param.7), channel_id=1, source_target_pairs={{0,4},{1,5},{2,6},{3,7},{4,8},{5,9},{6,10},{7,11},{8,12},{9,13},{1... | collective-permute-start | bytes 786440 | tf_op jit(solution)/shard_map/ppermute | solution.py:29
  5.7 6.7 %collective-permute-start.3 = (bf16[1024,128]{1,0:T(8,128)(2,1)}, bf16[1024,128]{1,0:T(8,128)(2,1)S(1)}, u32[]{:S(2)}, u32[]{:S(2)}) collective-permute-start(bf16[1024,128]{1,0:T(8,128)(2,1)} %param.7), channel_id=1, source_target_pairs={{0,252},{1,253},{2,254},{3,255},{4,0},{5,1},{6,2},{7,3},{8,4},{9,5... | collective-permute-start | bytes 786440 | tf_op jit(solution)/shard_map/ppermute | solution.py:29
  12.3 1.2 %collective-permute-start.7 = (bf16[1024,128]{1,0:T(8,128)(2,1)}, bf16[1024,128]{1,0:T(8,128)(2,1)S(1)}, u32[]{:S(2)}, u32[]{:S(2)}) collective-permute-start(bf16[1024,128]{1,0:T(8,128)(2,1)} %param.7), channel_id=1, source_target_pairs={{0,1},{1,0},{2,3},{3,2},{4,5},{5,4},{6,7},{7,6},{8,9},{9,8},{10,11... | collective-permute-start | bytes 786440 | tf_op jit(solution)/shard_map/ppermute | solution.py:29
  14.3 3.4 %copy-done = bf16[1024,4096]{1,0:T(8,128)(2,1)S(1)} copy-done((bf16[1024,4096]{1,0:T(8,128)(2,1)S(1)}, bf16[1024,4096]{1,0:T(8,128)(2,1)}, u32[]{:S(2)}) %copy-start) | copy-done | bytes 8388632
  18.4 11.3 %collective-permute-start.4 = (bf16[1024,128]{1,0:T(8,128)(2,1)S(1)}, bf16[1024,128]{1,0:T(8,128)(2,1)S(1)}, u32[]{:S(2)}, u32[]{:S(2)}) collective-permute-start(bf16[1024,128]{1,0:T(8,128)(2,1)S(1)} %collective-permute-done.1), channel_id=1, source_target_pairs={{0,252},{1,253},{2,254},{3,255},{4,0},{5,1},{6,2},{7,3},{8,4},{9,5... | collective-permute-start | bytes 786440 | tf_op jit(solution)/shard_map/ppermute | solution.py:29
  29.8 1.8 %collective-permute-start.5 = (bf16[1024,128]{1,0:T(8,128)(2,1)S(1)}, bf16[1024,128]{1,0:T(8,128)(2,1)S(1)}, u32[]{:S(2)}, u32[]{:S(2)}) collective-permute-start(bf16[1024,128]{1,0:T(8,128)(2,1)S(1)} %collective-permute-done), channel_id=1, source_target_pairs={{0,1},{1,0},{2,3},{3,2},{4,5},{5,4},{6,7},{7,6},{8,9},{9,8},{10,11... | collective-permute-start | bytes 786440 | tf_op jit(solution)/shard_map/ppermute | solution.py:29
  32.4 1.5 %collective-permute-done.4 = bf16[1024,128]{1,0:T(8,128)(2,1)S(1)} collective-permute-done((bf16[1024,128]{1,0:T(8,128)(2,1)S(1)}, bf16[1024,128]{1,0:T(8,128)(2,1)S(1)}, u32[]{:S(2)}, u32[]{:S(2)}) %collective-permute-start.4) | collective-permute-done | bytes 262176 | tf_op jit(solution)/shard_map/ppermute | solution.py:29
  33.9 2.4 %collective-permute-start.6 = (bf16[1024,128]{1,0:T(8,128)(2,1)S(1)}, bf16[1024,128]{1,0:T(8,128)(2,1)S(1)}, u32[]{:S(2)}, u32[]{:S(2)}) collective-permute-start(bf16[1024,128]{1,0:T(8,128)(2,1)S(1)} %collective-permute-done.2), channel_id=1, source_target_pairs={{0,1},{1,0},{2,3},{3,2},{4,5},{5,4},{6,7},{7,6},{8,9},{9,8},{10,11... | collective-permute-start | bytes 786440 | tf_op jit(solution)/shard_map/ppermute | solution.py:29
  36.5 1.0 collective-permute-done.6
  38.1 9.2 %forward.1 = (bf16[1024,512]{1,0:T(8,128)(2,1)}, bf16[128,1024]{1,0:T(8,128)(2,1)S(1)}, f32[8,8,640]{2,1,0:T(8,128)S(1)}, f32[8,8,640]{2,1,0:T(8,128)S(1)}) custom-call(s32[8,32]{1,0:T(8,128)S(1)} %fusion.6.place_ref, s32[1]{0:T(128)} %bitcast.core_ref, bf16[104,128,128]{2,1,0:T(8,128)(2,1)S(1)} %bitcast.42, bf16[1024,4096]{1,0:T(8,128)(2,1)S(1)} %load.1.values_ref, ...), custom_call_target="tpu_custom_call" | custom-call | flops 3221225472 | bytes 15728640 | tf_op jit(solution)/shard_map/forward/pallas_call | solution.py:215
  47.3 6.4 %backward.1 = (bf16[48,128,128]{2,1,0:T(8,128)(2,1)S(1)}, bf16[48,128,128]{2,1,0:T(8,128)(2,1)}) custom-call(s32[8,32]{1,0:T(8,128)S(1)} %fusion.6.place_ref, bf16[128,1024]{1,0:T(8,128)(2,1)S(1)} %get-tuple-element.15.back_ref, bf16[1024,4096]{1,0:T(8,128)(2,1)S(1)} %load.1.values_ref), custom_call_target="tpu_custom_call" | custom-call | flops 2147483648 | bytes 12582912 | tf_op jit(solution)/shard_map/backward/pallas_call | solution.py:268
  54.2 3.3 %collective-permute-done.11 = f32[8,8,640]{2,1,0:T(8,128)S(1)} collective-permute-done((f32[8,8,640]{2,1,0:T(8,128)S(1)}, f32[8,8,640]{2,1,0:T(8,128)S(1)}, u32[]{:S(2)}, u32[]{:S(2)}) %collective-permute-start.11) | collective-permute-done | bytes 163872 | tf_op jit(solution)/shard_map/ppermute | solution.py:29
  57.6 10.0 %all_to_all.15 = f32[8,8,640]{2,1,0:T(8,128)S(1)} all-to-all(f32[8,8,640]{2,1,0:T(8,128)S(1)} %add.44), channel_id=1, replica_groups=mesh['y_lo'=2,'z'=8,'x'=4,'y_hi'=2,'core'=2] {'x','y_hi'}, dimensions={0} | all-to-all | bytes 327680 | tf_op jit(solution)/shard_map/all_to_all | solution.py:274
  68.3 7.3 %all-to-all-start.1 = ((f32[16,8,640]{2,1,0:T(8,128)}), f32[16,8,640]{2,1,0:T(8,128)}, u32[]{:S(2)}, u32[]{:S(2)}) async-start(f32[16,8,640]{2,1,0:T(8,128)} %broadcast_in_dim.9), calls=%async_computation.1 | async-start | bytes 655360 | tf_op jit(solution)/shard_map/all_to_all | solution.py:47
  76.3 5.6 %collective-permute-start.14 = (bf16[2,8,128,128]{3,2,1,0:T(8,128)(2,1)S(1)}, bf16[2,8,128,128]{3,2,1,0:T(8,128)(2,1)S(1)}, u32[]{:S(2)}, u32[]{:S(2)}) collective-permute-start(bf16[2,8,128,128]{3,2,1,0:T(8,128)(2,1)S(1)} %bitcast.44), channel_id=1, source_target_pairs={{0,252},{1,253},{2,254},{3,255},{4,0},{5,1},{6,2},{7,3},{8,4},{9,5... | collective-permute-start | bytes 1572872 | tf_op jit(solution)/shard_map/ppermute | solution.py:29
  81.9 15.9 %collective-permute-done.13.up_ref = bf16[2,8,128,128]{3,2,1,0:T(8,128)(2,1)S(1)} collective-permute-done((bf16[2,8,128,128]{3,2,1,0:T(8,128)(2,1)S(1)}, bf16[2,8,128,128]{3,2,1,0:T(8,128)(2,1)S(1)}, u32[]{:S(2)}, u32[]{:S(2)}) %collective-permute-start.13) | collective-permute-done | bytes 524320 | tf_op jit(solution)/shard_map/ppermute | solution.py:29
  98.2 0.8 copy-done.2
  99.0 1.6 %collective-permute-start.15 = (bf16[1024,128]{1,0:T(8,128)(2,1)S(1)}, bf16[1024,128]{1,0:T(8,128)(2,1)S(1)}, u32[]{:S(2)}, u32[]{:S(2)}) collective-permute-start(bf16[1024,128]{1,0:T(8,128)(2,1)S(1)} %get-tuple-element.22), channel_id=1, source_target_pairs={{0,2},{1,3},{2,0},{3,1},{4,6},{5,7},{6,4},{7,5},{8,10},{9,11},{10,... | collective-permute-start | bytes 786440 | tf_op jit(solution)/shard_map/ppermute | solution.py:29
  100.6 1.0 reduce_sum.19
  102.3 3.4 %all-to-all-start.2 = ((f32[8,8,512]{2,1,0:T(8,128)}), f32[8,8,512]{2,1,0:T(8,128)S(1)}, u32[]{:S(2)}, u32[]{:S(2)}) async-start(f32[8,8,512]{2,1,0:T(8,128)} %broadcast_in_dim.10), calls=%async_computation.2 | async-start | bytes 262144 | tf_op jit(solution)/shard_map/all_to_all | solution.py:47
  106.3 6.1 %all-to-all-done.2 = f32[8,8,512]{2,1,0:T(8,128)S(1)} async-done(((f32[8,8,512]{2,1,0:T(8,128)}), f32[8,8,512]{2,1,0:T(8,128)S(1)}, u32[]{:S(2)}, u32[]{:S(2)}) %all-to-all-start.2) | async-done | bytes 131104 | tf_op jit(solution)/shard_map/all_to_all | solution.py:47
  112.4 3.1 %collective-permute-start.16 = (f32[8,8,512]{2,1,0:T(8,128)S(1)}, f32[8,8,512]{2,1,0:T(8,128)S(1)}, u32[]{:S(2)}, u32[]{:S(2)}) collective-permute-start(f32[8,8,512]{2,1,0:T(8,128)S(1)} %all-to-all-done.2), channel_id=1, source_target_pairs={{0,1},{1,0},{2,3},{3,2},{4,5},{5,4},{6,7},{7,6},{8,9},{9,8},{10,11... | collective-permute-start | bytes 393224 | tf_op jit(solution)/shard_map/ppermute | solution.py:29
  115.5 1.9 %convert_add_fusion = f32[1024,128]{1,0:T(8,128)} fusion(f32[1024,128]{1,0:T(8,128)} %copy-done.2, bf16[1024,128]{1,0:T(8,128)(2,1)S(1)} %collective-permute-done.15), kind=kLoop, calls=%fused_computation.2 | loop fusion | flops 262144 | bytes 1310720 | tf_op jit(solution)/shard_map/add | solution.py:299
  (56 shorter events, 7.2 us)
Async XLA Ops:
  0.6 12.9 %collective-permute-start.1 = (bf16[1024,128]{1,0:T(8,128)(2,1)}, bf16[1024,128]{1,0:T(8,128)(2,1)S(1)}, u32[]{:S(2)}, u32[]{:S(2)}) collective-permute-start(bf16[1024,128]{1,0:T(8,128)(2,1)} %param.7), channel_id=1, source_target_pairs={{0,2},{1,3},{2,0},{3,1},{4,6},{5,7},{6,4},{7,5},{8,10},{9,11},{10,... | collective-permute-start | bytes 786440 | tf_op jit(solution)/shard_map/ppermute | solution.py:29
  4.5 25.3 %collective-permute-start = (bf16[1024,128]{1,0:T(8,128)(2,1)}, bf16[1024,128]{1,0:T(8,128)(2,1)S(1)}, u32[]{:S(2)}, u32[]{:S(2)}) collective-permute-start(bf16[1024,128]{1,0:T(8,128)(2,1)} %param.7), channel_id=1, source_target_pairs={{0,4},{1,5},{2,6},{3,7},{4,8},{5,9},{6,10},{7,11},{8,12},{9,13},{1... | collective-permute-start | bytes 786440 | tf_op jit(solution)/shard_map/ppermute | solution.py:29
  5.7 25.9 %collective-permute-start.3 = (bf16[1024,128]{1,0:T(8,128)(2,1)}, bf16[1024,128]{1,0:T(8,128)(2,1)S(1)}, u32[]{:S(2)}, u32[]{:S(2)}) collective-permute-start(bf16[1024,128]{1,0:T(8,128)(2,1)} %param.7), channel_id=1, source_target_pairs={{0,252},{1,253},{2,254},{3,255},{4,0},{5,1},{6,2},{7,3},{8,4},{9,5... | collective-permute-start | bytes 786440 | tf_op jit(solution)/shard_map/ppermute | solution.py:29
  12.3 25.1 %collective-permute-start.7 = (bf16[1024,128]{1,0:T(8,128)(2,1)}, bf16[1024,128]{1,0:T(8,128)(2,1)S(1)}, u32[]{:S(2)}, u32[]{:S(2)}) collective-permute-start(bf16[1024,128]{1,0:T(8,128)(2,1)} %param.7), channel_id=1, source_target_pairs={{0,1},{1,0},{2,3},{3,2},{4,5},{5,4},{6,7},{7,6},{8,9},{9,8},{10,11... | collective-permute-start | bytes 786440 | tf_op jit(solution)/shard_map/ppermute | solution.py:29
  13.6 18.1 %collective-permute-start.2 = (bf16[1024,128]{1,0:T(8,128)(2,1)S(1)}, bf16[1024,128]{1,0:T(8,128)(2,1)S(1)}, u32[]{:S(2)}, u32[]{:S(2)}) collective-permute-start(bf16[1024,128]{1,0:T(8,128)(2,1)S(1)} %collective-permute-done.1), channel_id=1, source_target_pairs={{0,4},{1,5},{2,6},{3,7},{4,8},{5,9},{6,10},{7,11},{8,12},{9,13},{1... | collective-permute-start | bytes 786440 | tf_op jit(solution)/shard_map/ppermute | solution.py:29
  14.3 3.4 %copy-start = (bf16[1024,4096]{1,0:T(8,128)(2,1)S(1)}, bf16[1024,4096]{1,0:T(8,128)(2,1)}, u32[]{:S(2)}) copy-start(bf16[1024,4096]{1,0:T(8,128)(2,1)} %source_ref.1) | copy-start | bytes 25165828
  17.7 14.5 %copy-start.5 = (bf16[1024,128]{1,0:T(8,128)(2,1)S(1)}, bf16[1024,128]{1,0:T(8,128)(2,1)}, u32[]{:S(2)}) copy-start(bf16[1024,128]{1,0:T(8,128)(2,1)} %param.7) | copy-start | bytes 786436
  18.4 19.7 %copy-start.1 = (bf16[1024,512]{1,0:T(8,128)(2,1)S(1)}, bf16[1024,512]{1,0:T(8,128)(2,1)}, u32[]{:S(2)}) copy-start(bf16[1024,512]{1,0:T(8,128)(2,1)} %grad_ref.1) | copy-start | bytes 3145732
  18.4 19.7 %copy-start.3 = (bf16[128,512]{1,0:T(8,128)(2,1)S(1)}, bf16[128,512]{1,0:T(8,128)(2,1)}, u32[]{:S(2)}) copy-start(bf16[128,512]{1,0:T(8,128)(2,1)} %weight_ref.1) | copy-start | bytes 393220
  18.4 19.7 %copy-start.4 = (f32[512]{0:T(512)S(1)}, f32[512]{0:T(512)}, u32[]{:S(2)}) copy-start(f32[512]{0:T(512)} %param.9) | copy-start | bytes 6148
  18.4 15.5 %collective-permute-start.4 = (bf16[1024,128]{1,0:T(8,128)(2,1)S(1)}, bf16[1024,128]{1,0:T(8,128)(2,1)S(1)}, u32[]{:S(2)}, u32[]{:S(2)}) collective-permute-start(bf16[1024,128]{1,0:T(8,128)(2,1)S(1)} %collective-permute-done.1), channel_id=1, source_target_pairs={{0,252},{1,253},{2,254},{3,255},{4,0},{5,1},{6,2},{7,3},{8,4},{9,5... | collective-permute-start | bytes 786440 | tf_op jit(solution)/shard_map/ppermute | solution.py:29
  29.8 6.6 %collective-permute-start.5 = (bf16[1024,128]{1,0:T(8,128)(2,1)S(1)}, bf16[1024,128]{1,0:T(8,128)(2,1)S(1)}, u32[]{:S(2)}, u32[]{:S(2)}) collective-permute-start(bf16[1024,128]{1,0:T(8,128)(2,1)S(1)} %collective-permute-done), channel_id=1, source_target_pairs={{0,1},{1,0},{2,3},{3,2},{4,5},{5,4},{6,7},{7,6},{8,9},{9,8},{10,11... | collective-permute-start | bytes 786440 | tf_op jit(solution)/shard_map/ppermute | solution.py:29
  31.6 5.9 %collective-permute-start.8 = (bf16[1024,128]{1,0:T(8,128)(2,1)S(1)}, bf16[1024,128]{1,0:T(8,128)(2,1)S(1)}, u32[]{:S(2)}, u32[]{:S(2)}) collective-permute-start(bf16[1024,128]{1,0:T(8,128)(2,1)S(1)} %collective-permute-done.1), channel_id=1, source_target_pairs={{0,1},{1,0},{2,3},{3,2},{4,5},{5,4},{6,7},{7,6},{8,9},{9,8},{10,11... | collective-permute-start | bytes 786440 | tf_op jit(solution)/shard_map/ppermute | solution.py:29
  31.7 5.9 %collective-permute-start.9 = (bf16[1024,128]{1,0:T(8,128)(2,1)S(1)}, bf16[1024,128]{1,0:T(8,128)(2,1)S(1)}, u32[]{:S(2)}, u32[]{:S(2)}) collective-permute-start(bf16[1024,128]{1,0:T(8,128)(2,1)S(1)} %collective-permute-done.3), channel_id=1, source_target_pairs={{0,1},{1,0},{2,3},{3,2},{4,5},{5,4},{6,7},{7,6},{8,9},{9,8},{10,11... | collective-permute-start | bytes 786440 | tf_op jit(solution)/shard_map/ppermute | solution.py:29
  33.9 3.5 %collective-permute-start.6 = (bf16[1024,128]{1,0:T(8,128)(2,1)S(1)}, bf16[1024,128]{1,0:T(8,128)(2,1)S(1)}, u32[]{:S(2)}, u32[]{:S(2)}) collective-permute-start(bf16[1024,128]{1,0:T(8,128)(2,1)S(1)} %collective-permute-done.2), channel_id=1, source_target_pairs={{0,1},{1,0},{2,3},{3,2},{4,5},{5,4},{6,7},{7,6},{8,9},{9,8},{10,11... | collective-permute-start | bytes 786440 | tf_op jit(solution)/shard_map/ppermute | solution.py:29
  36.3 1.6 %collective-permute-start.10 = (bf16[1024,128]{1,0:T(8,128)(2,1)S(1)}, bf16[1024,128]{1,0:T(8,128)(2,1)S(1)}, u32[]{:S(2)}, u32[]{:S(2)}) collective-permute-start(bf16[1024,128]{1,0:T(8,128)(2,1)S(1)} %collective-permute-done.4), channel_id=1, source_target_pairs={{0,1},{1,0},{2,3},{3,2},{4,5},{5,4},{6,7},{7,6},{8,9},{9,8},{10,11... | collective-permute-start | bytes 786440 | tf_op jit(solution)/shard_map/ppermute | solution.py:29
  53.7 13.9 %collective-permute-start.12 = (bf16[48,128,128]{2,1,0:T(8,128)(2,1)}, bf16[48,128,128]{2,1,0:T(8,128)(2,1)S(1)}, u32[]{:S(2)}, u32[]{:S(2)}) collective-permute-start(bf16[48,128,128]{2,1,0:T(8,128)(2,1)} %get-tuple-element.19), channel_id=1, source_target_pairs={{0,1},{1,0},{2,3},{3,2},{4,5},{5,4},{6,7},{7,6},{8,9},{9,8},{10,11... | collective-permute-start | bytes 4718600 | tf_op jit(solution)/shard_map/ppermute | solution.py:29
  54.0 3.6 %collective-permute-start.11 = (f32[8,8,640]{2,1,0:T(8,128)S(1)}, f32[8,8,640]{2,1,0:T(8,128)S(1)}, u32[]{:S(2)}, u32[]{:S(2)}) collective-permute-start(f32[8,8,640]{2,1,0:T(8,128)S(1)} %get-tuple-element.18), channel_id=1, source_target_pairs={{0,1},{1,0},{2,3},{3,2},{4,5},{5,4},{6,7},{7,6},{8,9},{9,8},{10,11... | collective-permute-start | bytes 491528 | tf_op jit(solution)/shard_map/ppermute | solution.py:29
  68.3 32.3 %all-to-all-start.1 = ((f32[16,8,640]{2,1,0:T(8,128)}), f32[16,8,640]{2,1,0:T(8,128)}, u32[]{:S(2)}, u32[]{:S(2)}) async-start(f32[16,8,640]{2,1,0:T(8,128)} %broadcast_in_dim.9), calls=%async_computation.1 | async-start | bytes 655360 | tf_op jit(solution)/shard_map/all_to_all | solution.py:47
  76.0 21.9 %collective-permute-start.13 = (bf16[2,8,128,128]{3,2,1,0:T(8,128)(2,1)S(1)}, bf16[2,8,128,128]{3,2,1,0:T(8,128)(2,1)S(1)}, u32[]{:S(2)}, u32[]{:S(2)}) collective-permute-start(bf16[2,8,128,128]{3,2,1,0:T(8,128)(2,1)S(1)} %bitcast.45), channel_id=1, source_target_pairs={{0,4},{1,5},{2,6},{3,7},{4,8},{5,9},{6,10},{7,11},{8,12},{9,13},{1... | collective-permute-start | bytes 1572872 | tf_op jit(solution)/shard_map/ppermute | solution.py:29
  76.3 21.6 %collective-permute-start.14 = (bf16[2,8,128,128]{3,2,1,0:T(8,128)(2,1)S(1)}, bf16[2,8,128,128]{3,2,1,0:T(8,128)(2,1)S(1)}, u32[]{:S(2)}, u32[]{:S(2)}) collective-permute-start(bf16[2,8,128,128]{3,2,1,0:T(8,128)(2,1)S(1)} %bitcast.44), channel_id=1, source_target_pairs={{0,252},{1,253},{2,254},{3,255},{4,0},{5,1},{6,2},{7,3},{8,4},{9,5... | collective-permute-start | bytes 1572872 | tf_op jit(solution)/shard_map/ppermute | solution.py:29
  99.0 16.6 %collective-permute-start.15 = (bf16[1024,128]{1,0:T(8,128)(2,1)S(1)}, bf16[1024,128]{1,0:T(8,128)(2,1)S(1)}, u32[]{:S(2)}, u32[]{:S(2)}) collective-permute-start(bf16[1024,128]{1,0:T(8,128)(2,1)S(1)} %get-tuple-element.22), channel_id=1, source_target_pairs={{0,2},{1,3},{2,0},{3,1},{4,6},{5,7},{6,4},{7,5},{8,10},{9,11},{10,... | collective-permute-start | bytes 786440 | tf_op jit(solution)/shard_map/ppermute | solution.py:29
  102.3 10.1 %all-to-all-start.2 = ((f32[8,8,512]{2,1,0:T(8,128)}), f32[8,8,512]{2,1,0:T(8,128)S(1)}, u32[]{:S(2)}, u32[]{:S(2)}) async-start(f32[8,8,512]{2,1,0:T(8,128)} %broadcast_in_dim.10), calls=%async_computation.2 | async-start | bytes 262144 | tf_op jit(solution)/shard_map/all_to_all | solution.py:47
  112.4 5.0 %collective-permute-start.16 = (f32[8,8,512]{2,1,0:T(8,128)S(1)}, f32[8,8,512]{2,1,0:T(8,128)S(1)}, u32[]{:S(2)}, u32[]{:S(2)}) collective-permute-start(f32[8,8,512]{2,1,0:T(8,128)S(1)} %all-to-all-done.2), channel_id=1, source_target_pairs={{0,1},{1,0},{2,3},{3,2},{4,5},{5,4},{6,7},{7,6},{8,9},{9,8},{10,11... | collective-permute-start | bytes 393224 | tf_op jit(solution)/shard_map/ppermute | solution.py:29
  (1 other events, 0.8 us)

commit v2 on v1

--- a/solution.py
+++ b/solution.py
@@ -19,7 +19,7 @@
 AXES = ("y_lo", "z", "x", "y_hi", "core")
 NEAR = ("x", "y_hi")
 FAR = ("y_lo", "z")
-VMEM_LIMIT = 32 << 20
+VMEM_LIMIT = 14 << 20
 SPLIT = (2, 8, 4, 2, 2)
 STEP_TILES = 1
 
@@ -72,17 +72,22 @@
         copy.wait()
 
 
-def merge_kernel(keep_ref, core_ref, up_ref, down_ref, own_ref, other_ref):
-    for row in range(2):
-        for tile in range(PIECE_TILES):
-            refs = (keep_ref.at[1], core_ref.at[1], up_ref, down_ref)
-            terms = [ref[row, tile].astype(jnp.float32) for ref in refs]
-            total = jnp.swapaxes(terms[0] + terms[1] + terms[2] + terms[3], 0, 1)
-            rows = slice(tile * TILE, (tile + 1) * TILE)
-            if row == 0:
-                own_ref[rows, :] = total
-            else:
-                other_ref[rows, :] = total.astype(jnp.bfloat16)
+def turned(refs, index):
+    terms = [ref[index].astype(jnp.float32) for ref in refs]
+    return jnp.swapaxes(terms[0] + terms[1] + terms[2] + terms[3], 0, 1)
+
+
+def merge_kernel(keep_ref, core_ref, up_ref, down_ref, out_ref):
+    refs = (keep_ref.at[0, 0], core_ref.at[0, 0], up_ref.at[0], down_ref.at[0])
+    for tile in range(PIECE_TILES):
+        out_ref[tile * TILE : (tile + 1) * TILE, :] = turned(refs, tile).astype(jnp.bfloat16)
+
+
+def final_kernel(keep_ref, core_ref, up_ref, down_ref, last_ref, out_ref):
+    refs = (keep_ref.at[0, 0], core_ref.at[0, 0], up_ref.at[0], down_ref.at[0])
+    for tile in range(out_ref.shape[0] // TILE):
+        rows = slice(tile * TILE, (tile + 1) * TILE)
+        out_ref[rows, :] = turned(refs, tile) + last_ref[rows, :].astype(jnp.float32)
 
 
 def forward_kernel(
@@ -110,7 +115,7 @@
         value_part, slope = gelu_parts(pre_act)
         act_ref[rows, :] = value_part.astype(jnp.bfloat16)
         pre_wide = (grad_ref[rows, :].astype(jnp.float32) * slope).astype(jnp.bfloat16)
-        back_ref[:, rows] = lax.dot_general(
+        back_ref[tile] = lax.dot_general(
             weight, pre_wide, (((1,), (1,)), ((), ())), preferred_element_type=jnp.float32
         ).astype(jnp.bfloat16)
         agg_ref[place, :] = aggregated
@@ -148,9 +153,8 @@
         total_ref[...] = jnp.zeros_like(total_ref)
 
     for sub in range(STEP_TILES):
-        rows = slice(sub * TILE, (sub + 1) * TILE)
-        back = back_ref[:, rows]
         tile = step * STEP_TILES + sub
+        back = back_ref[tile]
         place = pl.ds(pl.multiple_of(tile * TILE, TILE), TILE)
         for pair in range(SLOTS // 2):
             term = jnp.dot(
@@ -210,13 +214,13 @@
         cost_estimate=pl.CostEstimate(flops=0, bytes_accessed=16 << 20, transcendentals=0),
         name="load",
     )
-    tile_values = load(tile_values)
-    whole = lambda *shape: pl.BlockSpec(shape, lambda i, *_: (0,) * len(shape))
+    tile_values = load(pltpu.with_memory_space_constraint(tile_values, pltpu.HBM))
+    whole = pl.BlockSpec(memory_space=pltpu.VMEM)
     act, back, own_sums, other_sums = pl.pallas_call(
         functools.partial(forward_kernel, factor),
         out_shape=(
             jax.ShapeDtypeStruct((rows_dev, out_dim), jnp.bfloat16),
-            jax.ShapeDtypeStruct((in_dim, rows_dev), jnp.bfloat16),
+            jax.ShapeDtypeStruct((row_tiles, in_dim, TILE), jnp.bfloat16),
             jax.ShapeDtypeStruct((chunks, chunk_rows, out_dim + TILE), jnp.float32),
             jax.ShapeDtypeStruct((chunks, chunk_rows, out_dim + TILE), jnp.float32),
         ),
@@ -224,17 +228,17 @@
             num_scalar_prefetch=2,
             grid=(row_tiles // STEP_TILES,),
             in_specs=[
-                whole(*window.shape),
-                pl.BlockSpec(memory_space=pltpu.VMEM),
+                whole,
+                whole,
                 pl.BlockSpec((step_rows, out_dim), lambda i, *_: (i, 0)),
-                whole(in_dim, out_dim),
-                whole(1, out_dim),
+                whole,
+                whole,
             ],
             out_specs=(
                 pl.BlockSpec((step_rows, out_dim), lambda i, *_: (i, 0)),
-                pl.BlockSpec((in_dim, step_rows), lambda i, *_: (0, i)),
-                whole(chunks, chunk_rows, out_dim + TILE),
-                whole(chunks, chunk_rows, out_dim + TILE),
+                whole,
+                whole,
+                whole,
             ),
             scratch_shapes=[
                 pltpu.VMEM((rows_dev, in_dim), jnp.bfloat16),
@@ -255,10 +259,10 @@
             num_scalar_prefetch=1,
             grid=(row_tiles // STEP_TILES,),
             in_specs=[
-                pl.BlockSpec((in_dim, step_rows), lambda i, *_: (0, i)),
-                pl.BlockSpec(memory_space=pltpu.VMEM),
+                whole,
+                whole,
             ],
-            out_specs=(whole(half_tiles, in_dim, TILE),) * 2,
+            out_specs=(whole,) * 2,
             scratch_shapes=[pltpu.VMEM((DUMMY + 1, in_dim, TILE), jnp.float32)],
         ),
         compiler_params=pltpu.CompilerParams(vmem_limit_bytes=VMEM_LIMIT),
@@ -278,25 +282,44 @@
     for steps in (1, -1):
         term = wide(keep[1 + steps]) + wide(from_core[1 + steps])
         moved.append(to_block(term.astype(jnp.bfloat16), steps))
-    part = jnp.sum(to_all(part, FAR), axis=0)
+    part = to_all(part, FAR)
+    part = jnp.sum(part, axis=0)
     bias_grad = part[: out_dim // TILE, out_dim:].reshape(out_dim)
-    own, other = pl.pallas_call(
+
+    def pieces_of(row, tiles):
+        outer = pl.BlockSpec((1, 1, tiles, in_dim, TILE), lambda i: (1, row, i, 0, 0))
+        inner = pl.BlockSpec((1, tiles, in_dim, TILE), lambda i: (row, i, 0, 0))
+        return [outer, outer, inner, inner]
+
+    operands = (keep, from_core, moved[0], moved[1])
+    other = pl.pallas_call(
         merge_kernel,
-        out_shape=(
-            jax.ShapeDtypeStruct((rows_dev, in_dim), jnp.float32),
-            jax.ShapeDtypeStruct((rows_dev, in_dim), jnp.bfloat16),
-        ),
-        compiler_params=pltpu.CompilerParams(vmem_limit_bytes=16 << 20),
-        cost_estimate=pl.CostEstimate(flops=1 << 20, bytes_accessed=4 << 20, transcendentals=0),
+        out_shape=jax.ShapeDtypeStruct((rows_dev, in_dim), jnp.bfloat16),
+        grid=(1,),
+        in_specs=pieces_of(1, PIECE_TILES),
+        out_specs=pl.BlockSpec((rows_dev, in_dim), lambda i: (0, 0)),
+        compiler_params=pltpu.CompilerParams(vmem_limit_bytes=6 << 20),
+        cost_estimate=pl.CostEstimate(flops=1 << 20, bytes_accessed=2 << 20, transcendentals=0),
         name="merge",
-    )(keep, from_core, moved[0], moved[1])
+    )(*operands)
     last = to_row(other)
     mine = to_all(part[:, :out_dim], NEAR)
     theirs = to_core(mine)
     odd = core == 1
     weight_grad = jnp.stack([jnp.where(odd, theirs, mine), jnp.where(odd, mine, theirs)], axis=1)
     weight_grad = weight_grad.reshape(in_dim, out_dim)
-    feature_grad = own + wide(last)
+    final_tiles = 2
+    rows_spec = pl.BlockSpec((final_tiles * TILE, in_dim), lambda i: (i, 0))
+    feature_grad = pl.pallas_call(
+        final_kernel,
+        out_shape=jax.ShapeDtypeStruct((rows_dev, in_dim), jnp.float32),
+        grid=(PIECE_TILES // final_tiles,),
+        in_specs=[*pieces_of(0, final_tiles), rows_spec],
+        out_specs=rows_spec,
+        compiler_params=pltpu.CompilerParams(vmem_limit_bytes=6 << 20),
+        cost_estimate=pl.CostEstimate(flops=1 << 20, bytes_accessed=2 << 20, transcendentals=0),
+        name="final",
+    )(*operands, last)
     return (act, feature_grad, weight_grad, bias_grad)
 
 

time: 119 us -> 113 us (0.950)
  the two profiles are of different devices: /device:TPU:1 before, /device:TPU:8 now
where the time goes in v2:
time: 113 us; the launch traced here: 112 us
  starting transfers between devices  45.7 us (40%)
  Pallas kernels  24.2 us (21%)
  waiting for transfers between devices  22.6 us (20%)
  blocking collectives  12.6 us (11%)
  local copies, waits for them, and re-layouts  3.18 us (3%)
  other arithmetic  2.9 us (3%)
    ppermute x17, starting transfers between devices, sent(): lax.ppermute(value, AXES, [(source, target(source, count)) for source in...  31.9 us
    ppermute x17, waiting for transfers between devices, sent(): lax.ppermute(value, AXES, [(source, target(source, count)) for source in...  20.6 us
    all_to_all x2, starting transfers between devices, to_all(): return lax.all_to_all(copies, axes, 0, 0, tiled=True)  13.8 us
    all_to_all x1, blocking collectives, layer(): part = jnp.sum(lax.all_to_all(part, NEAR, 0, 0, tiled=True), axis=0)  12.6 us
    pallas_call x1, Pallas kernels, layer(): pl.pallas_call(functools.partial(forward_kernel, factor), out_shape=(jax....  9.19 us
    pallas_call x1, Pallas kernels, layer(): keep, send = backward(place, back, tile_values)  6.29 us
    pallas_call x1, Pallas kernels, layer(): load(pltpu.with_memory_space_constraint(tile_values, pltpu.HBM))  3.51 us
    pallas_call x1, Pallas kernels, layer(): pl.pallas_call(final_kernel, out_shape=jax.ShapeDtypeStruct((rows_dev, in...  3.28 us
  transfers between devices with their start and end apart: 19, of which 7 were waited for; matrix products, arithmetic and copies ran while one was open for 4% of the time, Pallas kernels for 8%

profile of v2, /device:TPU:8, one launch (start us, length us, event | category | flops | bytes accessed | tf_op | source)
XLA Modules:
  0.0 112.0 jit_solution(10411506845960368221)
XLA Ops:
  0.6 2.4 %collective-permute-start.1 = (bf16[1024,128]{1,0:T(8,128)(2,1)}, bf16[1024,128]{1,0:T(8,128)(2,1)S(1)}, u32[]{:S(2)}, u32[]{:S(2)}) collective-permute-start(bf16[1024,128]{1,0:T(8,128)(2,1)} %param.7), channel_id=1, source_target_pairs={{0,2},{1,3},{2,0},{3,1},{4,6},{5,7},{6,4},{7,5},{8,10},{9,11},{10,... | collective-permute-start | bytes 786440 | tf_op jit(solution)/shard_map/ppermute | solution.py:29
  3.0 1.5 %collective-permute-start = (bf16[1024,128]{1,0:T(8,128)(2,1)}, bf16[1024,128]{1,0:T(8,128)(2,1)S(1)}, u32[]{:S(2)}, u32[]{:S(2)}) collective-permute-start(bf16[1024,128]{1,0:T(8,128)(2,1)} %param.7), channel_id=1, source_target_pairs={{0,4},{1,5},{2,6},{3,7},{4,8},{5,9},{6,10},{7,11},{8,12},{9,13},{1... | collective-permute-start | bytes 786440 | tf_op jit(solution)/shard_map/ppermute | solution.py:29
  4.5 7.3 %collective-permute-start.3 = (bf16[1024,128]{1,0:T(8,128)(2,1)}, bf16[1024,128]{1,0:T(8,128)(2,1)S(1)}, u32[]{:S(2)}, u32[]{:S(2)}) collective-permute-start(bf16[1024,128]{1,0:T(8,128)(2,1)} %param.7), channel_id=1, source_target_pairs={{0,252},{1,253},{2,254},{3,255},{4,0},{5,1},{6,2},{7,3},{8,4},{9,5... | collective-permute-start | bytes 786440 | tf_op jit(solution)/shard_map/ppermute | solution.py:29
  12.0 0.8 fusion.6.place_ref
  12.7 3.5 %load.1.values_ref = bf16[1024,4096]{1,0:T(8,128)(2,1)S(1)} custom-call(bf16[1024,4096]{1,0:T(8,128)(2,1)} %source_ref.1), custom_call_target="tpu_custom_call" | custom-call | bytes 16777216 | tf_op jit(solution)/shard_map/load/pallas_call | solution.py:217
  16.3 11.5 %collective-permute-start.4 = (bf16[1024,128]{1,0:T(8,128)(2,1)S(1)}, bf16[1024,128]{1,0:T(8,128)(2,1)S(1)}, u32[]{:S(2)}, u32[]{:S(2)}) collective-permute-start(bf16[1024,128]{1,0:T(8,128)(2,1)S(1)} %collective-permute-done.1), channel_id=1, source_target_pairs={{0,252},{1,253},{2,254},{3,255},{4,0},{5,1},{6,2},{7,3},{8,4},{9,5... | collective-permute-start | bytes 786440 | tf_op jit(solution)/shard_map/ppermute | solution.py:29
  28.7 3.0 %collective-permute-done.4 = bf16[1024,128]{1,0:T(8,128)(2,1)S(1)} collective-permute-done((bf16[1024,128]{1,0:T(8,128)(2,1)S(1)}, bf16[1024,128]{1,0:T(8,128)(2,1)S(1)}, u32[]{:S(2)}, u32[]{:S(2)}) %collective-permute-start.4) | collective-permute-done | bytes 262176 | tf_op jit(solution)/shard_map/ppermute | solution.py:29
  32.3 0.9 collective-permute-done.6
  33.7 9.2 %forward.1 = (bf16[1024,512]{1,0:T(8,128)(2,1)}, bf16[8,128,128]{2,1,0:T(8,128)(2,1)S(1)}, f32[8,8,640]{2,1,0:T(8,128)S(1)}, f32[8,8,640]{2,1,0:T(8,128)S(1)}) custom-call(s32[8,32]{1,0:T(8,128)S(1)} %fusion.6.place_ref, s32[1]{0:T(128)} %bitcast.core_ref, bf16[104,128,128]{2,1,0:T(8,128)(2,1)S(1)} %bitcast.44, bf16[1024,4096]{1,0:T(8,128)(2,1)S(1)} %load.1.values_ref, ...), custom_call_target="tpu_custom_call" | custom-call | flops 3221225472 | bytes 15728640 | tf_op jit(solution)/shard_map/forward/pallas_call | solution.py:219
  42.9 6.3 %backward.1 = (bf16[48,128,128]{2,1,0:T(8,128)(2,1)S(1)}, bf16[48,128,128]{2,1,0:T(8,128)(2,1)}) custom-call(s32[8,32]{1,0:T(8,128)S(1)} %fusion.6.place_ref, bf16[8,128,128]{2,1,0:T(8,128)(2,1)S(1)} %get-tuple-element.13.back_ref, bf16[1024,4096]{1,0:T(8,128)(2,1)S(1)} %load.1.values_ref), custom_call_target="tpu_custom_call" | custom-call | flops 2147483648 | bytes 12582912 | tf_op jit(solution)/shard_map/backward/pallas_call | solution.py:272
  49.7 3.3 %collective-permute-done.11 = f32[8,8,640]{2,1,0:T(8,128)S(1)} collective-permute-done((f32[8,8,640]{2,1,0:T(8,128)S(1)}, f32[8,8,640]{2,1,0:T(8,128)S(1)}, u32[]{:S(2)}, u32[]{:S(2)}) %collective-permute-start.11) | collective-permute-done | bytes 163872 | tf_op jit(solution)/shard_map/ppermute | solution.py:29
  53.0 12.6 %all_to_all.15 = f32[8,8,640]{2,1,0:T(8,128)S(1)} all-to-all(f32[8,8,640]{2,1,0:T(8,128)S(1)} %add.41), channel_id=1, replica_groups=mesh['y_lo'=2,'z'=8,'x'=4,'y_hi'=2,'core'=2] {'x','y_hi'}, dimensions={0} | all-to-all | bytes 327680 | tf_op jit(solution)/shard_map/all_to_all | solution.py:278
  65.6 0.8 broadcast_in_dim.9
  66.4 9.3 %all-to-all-start.1 = ((f32[16,8,640]{2,1,0:T(8,128)}), f32[16,8,640]{2,1,0:T(8,128)S(1)}, u32[]{:S(2)}, u32[]{:S(2)}) async-start(f32[16,8,640]{2,1,0:T(8,128)} %broadcast_in_dim.9), calls=%async_computation.1 | async-start | bytes 655360 | tf_op jit(solution)/shard_map/all_to_all | solution.py:47
  75.7 1.3 %add_convert_fusion = (bf16[16,128,128]{2,1,0:T(8,128)(2,1)}, bf16[16,128,128]{2,1,0:T(8,128)(2,1)}) fusion(bf16[48,128,128]{2,1,0:T(8,128)(2,1)S(1)} %collective-permute-done.12, bf16[48,128,128]{2,1,0:T(8,128)(2,1)S(1)} %get-tuple-element.14), kind=kLoop, calls=%fused_computation | loop fusion | flops 2097152 | bytes 3145728 | tf_op jit(solution)/shard_map/convert_element_type | solution.py:284
  77.3 6.0 %collective-permute-start.14 = (bf16[2,8,128,128]{3,2,1,0:T(8,128)(2,1)}, bf16[2,8,128,128]{3,2,1,0:T(8,128)(2,1)}, u32[]{:S(2)}, u32[]{:S(2)}) collective-permute-start(bf16[2,8,128,128]{3,2,1,0:T(8,128)(2,1)} %bitcast.18), channel_id=1, source_target_pairs={{0,252},{1,253},{2,254},{3,255},{4,0},{5,1},{6,2},{7,3},{8,4},{9,5... | collective-permute-start | bytes 1572872 | tf_op jit(solution)/shard_map/ppermute | solution.py:29
  83.3 1.9 %all-to-all-done.1 = f32[16,8,640]{2,1,0:T(8,128)S(1)} async-done(((f32[16,8,640]{2,1,0:T(8,128)}), f32[16,8,640]{2,1,0:T(8,128)S(1)}, u32[]{:S(2)}, u32[]{:S(2)}) %all-to-all-start.1) | async-done | bytes 327712 | tf_op jit(solution)/shard_map/all_to_all | solution.py:47
  85.9 4.5 %all-to-all-start.2 = ((f32[8,8,512]{2,1,0:T(8,128)}), f32[8,8,512]{2,1,0:T(8,128)S(1)}, u32[]{:S(2)}, u32[]{:S(2)}) async-start(f32[8,8,512]{2,1,0:T(8,128)} %broadcast_in_dim.10), calls=%async_computation.2 | async-start | bytes 262144 | tf_op jit(solution)/shard_map/all_to_all | solution.py:47
  90.4 6.8 %collective-permute-done.13.up_ref = bf16[2,8,128,128]{3,2,1,0:T(8,128)(2,1)} collective-permute-done((bf16[2,8,128,128]{3,2,1,0:T(8,128)(2,1)}, bf16[2,8,128,128]{3,2,1,0:T(8,128)(2,1)}, u32[]{:S(2)}, u32[]{:S(2)}) %collective-permute-start.13) | collective-permute-done | bytes 524320 | tf_op jit(solution)/shard_map/ppermute | solution.py:29
  97.3 1.9 %merge.1 = bf16[1024,128]{1,0:T(8,128)(2,1)} custom-call(bf16[3,2,8,128,128]{4,3,2,1,0:T(8,128)(2,1)S(1)} %bitcast.40, bf16[3,2,8,128,128]{4,3,2,1,0:T(8,128)(2,1)S(1)} %bitcast.42, bf16[2,8,128,128]{3,2,1,0:T(8,128)(2,1)} %collective-permute-done.13.up_ref, bf16[2,8,128,128]{3,2,1,0:T(8,128)(2,1)} %collective-permute-done.14.down_ref), custom_call_target="tpu_custom_call" | custom-call | flops 1048576 | bytes 2097152 | tf_op jit(solution)/shard_map/merge/pallas_call | solution.py:295
  99.2 1.1 collective-permute-start.15
  100.3 1.3 %slice_bitcast_fusion = f32[512]{0:T(512)} fusion(f32[8,640]{1,0:T(8,128)} %copy-done.4), kind=kLoop, calls=%fused_computation.44 | loop fusion | bytes 4096 | tf_op jit(solution)/shard_map/reshape | solution.py:287
  101.6 6.4 %collective-permute-done.15.last_ref = bf16[1024,128]{1,0:T(8,128)(2,1)S(1)} collective-permute-done((bf16[1024,128]{1,0:T(8,128)(2,1)}, bf16[1024,128]{1,0:T(8,128)(2,1)S(1)}, u32[]{:S(2)}, u32[]{:S(2)}) %collective-permute-start.15) | collective-permute-done | bytes 262176 | tf_op jit(solution)/shard_map/ppermute | solution.py:29
  108.0 3.3 %final.1 = f32[1024,128]{1,0:T(8,128)} custom-call(bf16[3,2,8,128,128]{4,3,2,1,0:T(8,128)(2,1)S(1)} %bitcast.41, bf16[3,2,8,128,128]{4,3,2,1,0:T(8,128)(2,1)S(1)} %bitcast.43, bf16[2,8,128,128]{3,2,1,0:T(8,128)(2,1)} %collective-permute-done.13.up_ref, bf16[2,8,128,128]{3,2,1,0:T(8,128)(2,1)} %collective-permute-done.14.down_ref, ...), custom_call_target="tpu_custom_call" | custom-call | flops 1048576 | bytes 2097152 | tf_op jit(solution)/shard_map/final/pallas_call | solution.py:313
  (54 shorter events, 4.3 us)
Async XLA Ops:
  0.6 11.2 %collective-permute-start.1 = (bf16[1024,128]{1,0:T(8,128)(2,1)}, bf16[1024,128]{1,0:T(8,128)(2,1)S(1)}, u32[]{:S(2)}, u32[]{:S(2)}) collective-permute-start(bf16[1024,128]{1,0:T(8,128)(2,1)} %param.7), channel_id=1, source_target_pairs={{0,2},{1,3},{2,0},{3,1},{4,6},{5,7},{6,4},{7,5},{8,10},{9,11},{10,... | collective-permute-start | bytes 786440 | tf_op jit(solution)/shard_map/ppermute | solution.py:29
  3.0 24.7 %collective-permute-start = (bf16[1024,128]{1,0:T(8,128)(2,1)}, bf16[1024,128]{1,0:T(8,128)(2,1)S(1)}, u32[]{:S(2)}, u32[]{:S(2)}) collective-permute-start(bf16[1024,128]{1,0:T(8,128)(2,1)} %param.7), channel_id=1, source_target_pairs={{0,4},{1,5},{2,6},{3,7},{4,8},{5,9},{6,10},{7,11},{8,12},{9,13},{1... | collective-permute-start | bytes 786440 | tf_op jit(solution)/shard_map/ppermute | solution.py:29
  4.5 23.3 %collective-permute-start.3 = (bf16[1024,128]{1,0:T(8,128)(2,1)}, bf16[1024,128]{1,0:T(8,128)(2,1)S(1)}, u32[]{:S(2)}, u32[]{:S(2)}) collective-permute-start(bf16[1024,128]{1,0:T(8,128)(2,1)} %param.7), channel_id=1, source_target_pairs={{0,252},{1,253},{2,254},{3,255},{4,0},{5,1},{6,2},{7,3},{8,4},{9,5... | collective-permute-start | bytes 786440 | tf_op jit(solution)/shard_map/ppermute | solution.py:29
  11.9 21.4 %collective-permute-start.7 = (bf16[1024,128]{1,0:T(8,128)(2,1)}, bf16[1024,128]{1,0:T(8,128)(2,1)S(1)}, u32[]{:S(2)}, u32[]{:S(2)}) collective-permute-start(bf16[1024,128]{1,0:T(8,128)(2,1)} %param.7), channel_id=1, source_target_pairs={{0,1},{1,0},{2,3},{3,2},{4,5},{5,4},{6,7},{7,6},{8,9},{9,8},{10,11... | collective-permute-start | bytes 786440 | tf_op jit(solution)/shard_map/ppermute | solution.py:29
  11.9 16.5 %collective-permute-start.2 = (bf16[1024,128]{1,0:T(8,128)(2,1)S(1)}, bf16[1024,128]{1,0:T(8,128)(2,1)S(1)}, u32[]{:S(2)}, u32[]{:S(2)}) collective-permute-start(bf16[1024,128]{1,0:T(8,128)(2,1)S(1)} %collective-permute-done.1), channel_id=1, source_target_pairs={{0,4},{1,5},{2,6},{3,7},{4,8},{5,9},{6,10},{7,11},{8,12},{9,13},{1... | collective-permute-start | bytes 786440 | tf_op jit(solution)/shard_map/ppermute | solution.py:29
  12.7 15.8 %copy-start.3 = (bf16[1024,128]{1,0:T(8,128)(2,1)S(1)}, bf16[1024,128]{1,0:T(8,128)(2,1)}, u32[]{:S(2)}) copy-start(bf16[1024,128]{1,0:T(8,128)(2,1)} %param.7) | copy-start | bytes 786436
  16.2 17.4 %copy-start = (bf16[1024,512]{1,0:T(8,128)(2,1)S(1)}, bf16[1024,512]{1,0:T(8,128)(2,1)}, u32[]{:S(2)}) copy-start(bf16[1024,512]{1,0:T(8,128)(2,1)} %grad_ref.1) | copy-start | bytes 3145732
  16.3 17.4 %copy-start.1 = (bf16[128,512]{1,0:T(8,128)(2,1)S(1)}, bf16[128,512]{1,0:T(8,128)(2,1)}, u32[]{:S(2)}) copy-start(bf16[128,512]{1,0:T(8,128)(2,1)} %weight_ref.1) | copy-start | bytes 393220
  16.3 17.4 %copy-start.2 = (f32[512]{0:T(512)S(1)}, f32[512]{0:T(512)}, u32[]{:S(2)}) copy-start(f32[512]{0:T(512)} %param.9) | copy-start | bytes 6148
  16.3 15.3 %collective-permute-start.4 = (bf16[1024,128]{1,0:T(8,128)(2,1)S(1)}, bf16[1024,128]{1,0:T(8,128)(2,1)S(1)}, u32[]{:S(2)}, u32[]{:S(2)}) collective-permute-start(bf16[1024,128]{1,0:T(8,128)(2,1)S(1)} %collective-permute-done.1), channel_id=1, source_target_pairs={{0,252},{1,253},{2,254},{3,255},{4,0},{5,1},{6,2},{7,3},{8,4},{9,5... | collective-permute-start | bytes 786440 | tf_op jit(solution)/shard_map/ppermute | solution.py:29
  27.7 3.9 %collective-permute-start.5 = (bf16[1024,128]{1,0:T(8,128)(2,1)S(1)}, bf16[1024,128]{1,0:T(8,128)(2,1)S(1)}, u32[]{:S(2)}, u32[]{:S(2)}) collective-permute-start(bf16[1024,128]{1,0:T(8,128)(2,1)S(1)} %collective-permute-done), channel_id=1, source_target_pairs={{0,1},{1,0},{2,3},{3,2},{4,5},{5,4},{6,7},{7,6},{8,9},{9,8},{10,11... | collective-permute-start | bytes 786440 | tf_op jit(solution)/shard_map/ppermute | solution.py:29
  27.8 5.5 %collective-permute-start.8 = (bf16[1024,128]{1,0:T(8,128)(2,1)S(1)}, bf16[1024,128]{1,0:T(8,128)(2,1)S(1)}, u32[]{:S(2)}, u32[]{:S(2)}) collective-permute-start(bf16[1024,128]{1,0:T(8,128)(2,1)S(1)} %collective-permute-done.1), channel_id=1, source_target_pairs={{0,1},{1,0},{2,3},{3,2},{4,5},{5,4},{6,7},{7,6},{8,9},{9,8},{10,11... | collective-permute-start | bytes 786440 | tf_op jit(solution)/shard_map/ppermute | solution.py:29
  28.4 4.9 %collective-permute-start.9 = (bf16[1024,128]{1,0:T(8,128)(2,1)S(1)}, bf16[1024,128]{1,0:T(8,128)(2,1)S(1)}, u32[]{:S(2)}, u32[]{:S(2)}) collective-permute-start(bf16[1024,128]{1,0:T(8,128)(2,1)S(1)} %collective-permute-done.3), channel_id=1, source_target_pairs={{0,1},{1,0},{2,3},{3,2},{4,5},{5,4},{6,7},{7,6},{8,9},{9,8},{10,11... | collective-permute-start | bytes 786440 | tf_op jit(solution)/shard_map/ppermute | solution.py:29
  31.6 1.5 %collective-permute-start.6 = (bf16[1024,128]{1,0:T(8,128)(2,1)S(1)}, bf16[1024,128]{1,0:T(8,128)(2,1)S(1)}, u32[]{:S(2)}, u32[]{:S(2)}) collective-permute-start(bf16[1024,128]{1,0:T(8,128)(2,1)S(1)} %collective-permute-done.2), channel_id=1, source_target_pairs={{0,1},{1,0},{2,3},{3,2},{4,5},{5,4},{6,7},{7,6},{8,9},{9,8},{10,11... | collective-permute-start | bytes 786440 | tf_op jit(solution)/shard_map/ppermute | solution.py:29
  31.7 1.9 %collective-permute-start.10 = (bf16[1024,128]{1,0:T(8,128)(2,1)S(1)}, bf16[1024,128]{1,0:T(8,128)(2,1)S(1)}, u32[]{:S(2)}, u32[]{:S(2)}) collective-permute-start(bf16[1024,128]{1,0:T(8,128)(2,1)S(1)} %collective-permute-done.4), channel_id=1, source_target_pairs={{0,1},{1,0},{2,3},{3,2},{4,5},{5,4},{6,7},{7,6},{8,9},{9,8},{10,11... | collective-permute-start | bytes 786440 | tf_op jit(solution)/shard_map/ppermute | solution.py:29
  49.1 16.5 %collective-permute-start.12 = (bf16[48,128,128]{2,1,0:T(8,128)(2,1)}, bf16[48,128,128]{2,1,0:T(8,128)(2,1)S(1)}, u32[]{:S(2)}, u32[]{:S(2)}) collective-permute-start(bf16[48,128,128]{2,1,0:T(8,128)(2,1)} %get-tuple-element.17), channel_id=1, source_target_pairs={{0,1},{1,0},{2,3},{3,2},{4,5},{5,4},{6,7},{7,6},{8,9},{9,8},{10,11... | collective-permute-start | bytes 4718600 | tf_op jit(solution)/shard_map/ppermute | solution.py:29
  49.4 3.6 %collective-permute-start.11 = (f32[8,8,640]{2,1,0:T(8,128)S(1)}, f32[8,8,640]{2,1,0:T(8,128)S(1)}, u32[]{:S(2)}, u32[]{:S(2)}) collective-permute-start(f32[8,8,640]{2,1,0:T(8,128)S(1)} %get-tuple-element.16), channel_id=1, source_target_pairs={{0,1},{1,0},{2,3},{3,2},{4,5},{5,4},{6,7},{7,6},{8,9},{9,8},{10,11... | collective-permute-start | bytes 491528 | tf_op jit(solution)/shard_map/ppermute | solution.py:29
  66.4 18.8 %all-to-all-start.1 = ((f32[16,8,640]{2,1,0:T(8,128)}), f32[16,8,640]{2,1,0:T(8,128)S(1)}, u32[]{:S(2)}, u32[]{:S(2)}) async-start(f32[16,8,640]{2,1,0:T(8,128)} %broadcast_in_dim.9), calls=%async_computation.1 | async-start | bytes 655360 | tf_op jit(solution)/shard_map/all_to_all | solution.py:47
  77.0 20.3 %collective-permute-start.13 = (bf16[2,8,128,128]{3,2,1,0:T(8,128)(2,1)}, bf16[2,8,128,128]{3,2,1,0:T(8,128)(2,1)}, u32[]{:S(2)}, u32[]{:S(2)}) collective-permute-start(bf16[2,8,128,128]{3,2,1,0:T(8,128)(2,1)} %bitcast.17), channel_id=1, source_target_pairs={{0,4},{1,5},{2,6},{3,7},{4,8},{5,9},{6,10},{7,11},{8,12},{9,13},{1... | collective-permute-start | bytes 1572872 | tf_op jit(solution)/shard_map/ppermute | solution.py:29
  77.3 20.0 %collective-permute-start.14 = (bf16[2,8,128,128]{3,2,1,0:T(8,128)(2,1)}, bf16[2,8,128,128]{3,2,1,0:T(8,128)(2,1)}, u32[]{:S(2)}, u32[]{:S(2)}) collective-permute-start(bf16[2,8,128,128]{3,2,1,0:T(8,128)(2,1)} %bitcast.18), channel_id=1, source_target_pairs={{0,252},{1,253},{2,254},{3,255},{4,0},{5,1},{6,2},{7,3},{8,4},{9,5... | collective-permute-start | bytes 1572872 | tf_op jit(solution)/shard_map/ppermute | solution.py:29
  85.2 12.1 %copy-start.4 = (f32[8,640]{1,0:T(8,128)}, f32[8,640]{1,0:T(8,128)S(1)}, u32[]{:S(2)}) copy-start(f32[8,640]{1,0:T(8,128)S(1)} %reduce_sum.19) | copy-start | bytes 61444
  85.9 14.4 %all-to-all-start.2 = ((f32[8,8,512]{2,1,0:T(8,128)}), f32[8,8,512]{2,1,0:T(8,128)S(1)}, u32[]{:S(2)}, u32[]{:S(2)}) async-start(f32[8,8,512]{2,1,0:T(8,128)} %broadcast_in_dim.10), calls=%async_computation.2 | async-start | bytes 262144 | tf_op jit(solution)/shard_map/all_to_all | solution.py:47
  99.2 8.8 %collective-permute-start.15 = (bf16[1024,128]{1,0:T(8,128)(2,1)}, bf16[1024,128]{1,0:T(8,128)(2,1)S(1)}, u32[]{:S(2)}, u32[]{:S(2)}) collective-permute-start(bf16[1024,128]{1,0:T(8,128)(2,1)} %merge.1), channel_id=1, source_target_pairs={{0,2},{1,3},{2,0},{3,1},{4,6},{5,7},{6,4},{7,5},{8,10},{9,11},{10,... | collective-permute-start | bytes 786440 | tf_op jit(solution)/shard_map/ppermute | solution.py:29
  100.3 10.9 %collective-permute-start.16 = (f32[8,8,512]{2,1,0:T(8,128)S(1)}, f32[8,8,512]{2,1,0:T(8,128)S(1)}, u32[]{:S(2)}, u32[]{:S(2)}) collective-permute-start(f32[8,8,512]{2,1,0:T(8,128)S(1)} %all-to-all-done.2), channel_id=1, source_target_pairs={{0,1},{1,0},{2,3},{3,2},{4,5},{5,4},{6,7},{7,6},{8,9},{9,8},{10,11... | collective-permute-start | bytes 393224 | tf_op jit(solution)/shard_map/ppermute | solution.py:29

commit v3 on v2

--- a/solution.py
+++ b/solution.py
@@ -78,16 +78,19 @@
 
 
 def merge_kernel(keep_ref, core_ref, up_ref, down_ref, out_ref):
-    refs = (keep_ref.at[0, 0], core_ref.at[0, 0], up_ref.at[0], down_ref.at[0])
+    refs = (keep_ref.at[1, 1], core_ref.at[1, 1], up_ref.at[1], down_ref.at[1])
     for tile in range(PIECE_TILES):
         out_ref[tile * TILE : (tile + 1) * TILE, :] = turned(refs, tile).astype(jnp.bfloat16)
 
 
 def final_kernel(keep_ref, core_ref, up_ref, down_ref, last_ref, out_ref):
-    refs = (keep_ref.at[0, 0], core_ref.at[0, 0], up_ref.at[0], down_ref.at[0])
-    for tile in range(out_ref.shape[0] // TILE):
-        rows = slice(tile * TILE, (tile + 1) * TILE)
-        out_ref[rows, :] = turned(refs, tile) + last_ref[rows, :].astype(jnp.float32)
+    refs = (keep_ref.at[1, 0], core_ref.at[1, 0], up_ref.at[0], down_ref.at[0])
+    count = out_ref.shape[0] // TILE
+    for sub in range(count):
+        tile = pl.program_id(0) * count + sub
+        rows = pl.ds(pl.multiple_of(tile * TILE, TILE), TILE)
+        total = turned(refs, tile) + last_ref[rows, :].astype(jnp.float32)
+        out_ref[sub * TILE : (sub + 1) * TILE, :] = total
 
 
 def forward_kernel(
@@ -285,19 +288,12 @@
     part = to_all(part, FAR)
     part = jnp.sum(part, axis=0)
     bias_grad = part[: out_dim // TILE, out_dim:].reshape(out_dim)
-
-    def pieces_of(row, tiles):
-        outer = pl.BlockSpec((1, 1, tiles, in_dim, TILE), lambda i: (1, row, i, 0, 0))
-        inner = pl.BlockSpec((1, tiles, in_dim, TILE), lambda i: (row, i, 0, 0))
-        return [outer, outer, inner, inner]
-
     operands = (keep, from_core, moved[0], moved[1])
     other = pl.pallas_call(
         merge_kernel,
         out_shape=jax.ShapeDtypeStruct((rows_dev, in_dim), jnp.bfloat16),
-        grid=(1,),
-        in_specs=pieces_of(1, PIECE_TILES),
-        out_specs=pl.BlockSpec((rows_dev, in_dim), lambda i: (0, 0)),
+        in_specs=[whole] * 4,
+        out_specs=whole,
         compiler_params=pltpu.CompilerParams(vmem_limit_bytes=6 << 20),
         cost_estimate=pl.CostEstimate(flops=1 << 20, bytes_accessed=2 << 20, transcendentals=0),
         name="merge",
@@ -310,16 +306,17 @@
     weight_grad = weight_grad.reshape(in_dim, out_dim)
     final_tiles = 2
     rows_spec = pl.BlockSpec((final_tiles * TILE, in_dim), lambda i: (i, 0))
-    feature_grad = pl.pallas_call(
+    final = pl.pallas_call(
         final_kernel,
         out_shape=jax.ShapeDtypeStruct((rows_dev, in_dim), jnp.float32),
         grid=(PIECE_TILES // final_tiles,),
-        in_specs=[*pieces_of(0, final_tiles), rows_spec],
+        in_specs=[whole] * 5,
         out_specs=rows_spec,
         compiler_params=pltpu.CompilerParams(vmem_limit_bytes=6 << 20),
         cost_estimate=pl.CostEstimate(flops=1 << 20, bytes_accessed=2 << 20, transcendentals=0),
         name="final",
-    )(*operands, last)
+    )
+    feature_grad = final(*operands, last)
     return (act, feature_grad, weight_grad, bias_grad)
 
 

time: 113 us -> 112 us (level)
  no operation moved by 1% of the time
where the time goes in v3:
time: 112 us
  starting transfers between devices  45.7 us (41%)
  Pallas kernels  23.9 us (21%)
  waiting for transfers between devices  22.6 us (20%)
  blocking collectives  12.6 us (11%)
  local copies, waits for them, and re-layouts  3.18 us (3%)
  other arithmetic  2.9 us (3%)
    ppermute x17, starting transfers between devices, sent(): lax.ppermute(value, AXES, [(source, target(source, count)) for source in...  31.9 us
    ppermute x17, waiting for transfers between devices, sent(): lax.ppermute(value, AXES, [(source, target(source, count)) for source in...  20.6 us
    all_to_all x2, starting transfers between devices, to_all(): return lax.all_to_all(copies, axes, 0, 0, tiled=True)  13.8 us
    all_to_all x1, blocking collectives, layer(): part = jnp.sum(lax.all_to_all(part, NEAR, 0, 0, tiled=True), axis=0)  12.6 us
    pallas_call x1, Pallas kernels, layer(): pl.pallas_call(functools.partial(forward_kernel, factor), out_shape=(jax....  9.19 us
    pallas_call x1, Pallas kernels, layer(): keep, send = backward(place, back, tile_values)  6.29 us
    pallas_call x1, Pallas kernels, layer(): load(pltpu.with_memory_space_constraint(tile_values, pltpu.HBM))  3.51 us
    pallas_call x1, Pallas kernels, layer(): feature_grad = final(*operands, last)  2.85 us
  transfers between devices with their start and end apart: 19, of which 7 were waited for; matrix products, arithmetic and copies ran while one was open for 4% of the time, Pallas kernels for 8%

profile of v3, /device:TPU:8, one launch (start us, length us, event | category | flops | bytes accessed | tf_op | source)
XLA Modules:
  0.0 111.8 jit_solution(8740299368078224502)
XLA Ops:
  0.6 2.4 %collective-permute-start.1 = (bf16[1024,128]{1,0:T(8,128)(2,1)}, bf16[1024,128]{1,0:T(8,128)(2,1)S(1)}, u32[]{:S(2)}, u32[]{:S(2)}) collective-permute-start(bf16[1024,128]{1,0:T(8,128)(2,1)} %param.7), channel_id=1, source_target_pairs={{0,2},{1,3},{2,0},{3,1},{4,6},{5,7},{6,4},{7,5},{8,10},{9,11},{10,... | collective-permute-start | bytes 786440 | tf_op jit(solution)/shard_map/ppermute | solution.py:29
  3.0 1.5 %collective-permute-start = (bf16[1024,128]{1,0:T(8,128)(2,1)}, bf16[1024,128]{1,0:T(8,128)(2,1)S(1)}, u32[]{:S(2)}, u32[]{:S(2)}) collective-permute-start(bf16[1024,128]{1,0:T(8,128)(2,1)} %param.7), channel_id=1, source_target_pairs={{0,4},{1,5},{2,6},{3,7},{4,8},{5,9},{6,10},{7,11},{8,12},{9,13},{1... | collective-permute-start | bytes 786440 | tf_op jit(solution)/shard_map/ppermute | solution.py:29
  4.5 7.3 %collective-permute-start.3 = (bf16[1024,128]{1,0:T(8,128)(2,1)}, bf16[1024,128]{1,0:T(8,128)(2,1)S(1)}, u32[]{:S(2)}, u32[]{:S(2)}) collective-permute-start(bf16[1024,128]{1,0:T(8,128)(2,1)} %param.7), channel_id=1, source_target_pairs={{0,252},{1,253},{2,254},{3,255},{4,0},{5,1},{6,2},{7,3},{8,4},{9,5... | collective-permute-start | bytes 786440 | tf_op jit(solution)/shard_map/ppermute | solution.py:29
  12.0 0.8 fusion.6.place_ref
  12.7 3.5 %load.1.values_ref = bf16[1024,4096]{1,0:T(8,128)(2,1)S(1)} custom-call(bf16[1024,4096]{1,0:T(8,128)(2,1)} %source_ref.1), custom_call_target="tpu_custom_call" | custom-call | bytes 16777216 | tf_op jit(solution)/shard_map/load/pallas_call | solution.py:220
  16.3 11.5 %collective-permute-start.4 = (bf16[1024,128]{1,0:T(8,128)(2,1)S(1)}, bf16[1024,128]{1,0:T(8,128)(2,1)S(1)}, u32[]{:S(2)}, u32[]{:S(2)}) collective-permute-start(bf16[1024,128]{1,0:T(8,128)(2,1)S(1)} %collective-permute-done.1), channel_id=1, source_target_pairs={{0,252},{1,253},{2,254},{3,255},{4,0},{5,1},{6,2},{7,3},{8,4},{9,5... | collective-permute-start | bytes 786440 | tf_op jit(solution)/shard_map/ppermute | solution.py:29
  28.7 3.0 %collective-permute-done.4 = bf16[1024,128]{1,0:T(8,128)(2,1)S(1)} collective-permute-done((bf16[1024,128]{1,0:T(8,128)(2,1)S(1)}, bf16[1024,128]{1,0:T(8,128)(2,1)S(1)}, u32[]{:S(2)}, u32[]{:S(2)}) %collective-permute-start.4) | collective-permute-done | bytes 262176 | tf_op jit(solution)/shard_map/ppermute | solution.py:29
  32.3 0.9 collective-permute-done.6
  33.7 9.2 %forward.1 = (bf16[1024,512]{1,0:T(8,128)(2,1)}, bf16[8,128,128]{2,1,0:T(8,128)(2,1)S(1)}, f32[8,8,640]{2,1,0:T(8,128)S(1)}, f32[8,8,640]{2,1,0:T(8,128)S(1)}) custom-call(s32[8,32]{1,0:T(8,128)S(1)} %fusion.6.place_ref, s32[1]{0:T(128)} %bitcast.core_ref, bf16[104,128,128]{2,1,0:T(8,128)(2,1)S(1)} %bitcast.44, bf16[1024,4096]{1,0:T(8,128)(2,1)S(1)} %load.1.values_ref, ...), custom_call_target="tpu_custom_call" | custom-call | flops 3221225472 | bytes 15728640 | tf_op jit(solution)/shard_map/forward/pallas_call | solution.py:222
  42.9 6.3 %backward.1 = (bf16[48,128,128]{2,1,0:T(8,128)(2,1)S(1)}, bf16[48,128,128]{2,1,0:T(8,128)(2,1)}) custom-call(s32[8,32]{1,0:T(8,128)S(1)} %fusion.6.place_ref, bf16[8,128,128]{2,1,0:T(8,128)(2,1)S(1)} %get-tuple-element.13.back_ref, bf16[1024,4096]{1,0:T(8,128)(2,1)S(1)} %load.1.values_ref), custom_call_target="tpu_custom_call" | custom-call | flops 2147483648 | bytes 12582912 | tf_op jit(solution)/shard_map/backward/pallas_call | solution.py:275
  49.7 3.3 %collective-permute-done.11 = f32[8,8,640]{2,1,0:T(8,128)S(1)} collective-permute-done((f32[8,8,640]{2,1,0:T(8,128)S(1)}, f32[8,8,640]{2,1,0:T(8,128)S(1)}, u32[]{:S(2)}, u32[]{:S(2)}) %collective-permute-start.11) | collective-permute-done | bytes 163872 | tf_op jit(solution)/shard_map/ppermute | solution.py:29
  53.0 12.6 %all_to_all.15 = f32[8,8,640]{2,1,0:T(8,128)S(1)} all-to-all(f32[8,8,640]{2,1,0:T(8,128)S(1)} %add.41), channel_id=1, replica_groups=mesh['y_lo'=2,'z'=8,'x'=4,'y_hi'=2,'core'=2] {'x','y_hi'}, dimensions={0} | all-to-all | bytes 327680 | tf_op jit(solution)/shard_map/all_to_all | solution.py:281
  65.6 0.8 broadcast_in_dim.9
  66.4 9.3 %all-to-all-start.1 = ((f32[16,8,640]{2,1,0:T(8,128)}), f32[16,8,640]{2,1,0:T(8,128)S(1)}, u32[]{:S(2)}, u32[]{:S(2)}) async-start(f32[16,8,640]{2,1,0:T(8,128)} %broadcast_in_dim.9), calls=%async_computation.1 | async-start | bytes 655360 | tf_op jit(solution)/shard_map/all_to_all | solution.py:47
  75.7 1.3 %add_convert_fusion = (bf16[16,128,128]{2,1,0:T(8,128)(2,1)}, bf16[16,128,128]{2,1,0:T(8,128)(2,1)}) fusion(bf16[48,128,128]{2,1,0:T(8,128)(2,1)S(1)} %collective-permute-done.12, bf16[48,128,128]{2,1,0:T(8,128)(2,1)S(1)} %get-tuple-element.14), kind=kLoop, calls=%fused_computation | loop fusion | flops 2097152 | bytes 3145728 | tf_op jit(solution)/shard_map/convert_element_type | solution.py:287
  77.3 6.0 %collective-permute-start.14 = (bf16[2,8,128,128]{3,2,1,0:T(8,128)(2,1)}, bf16[2,8,128,128]{3,2,1,0:T(8,128)(2,1)}, u32[]{:S(2)}, u32[]{:S(2)}) collective-permute-start(bf16[2,8,128,128]{3,2,1,0:T(8,128)(2,1)} %bitcast.18), channel_id=1, source_target_pairs={{0,252},{1,253},{2,254},{3,255},{4,0},{5,1},{6,2},{7,3},{8,4},{9,5... | collective-permute-start | bytes 1572872 | tf_op jit(solution)/shard_map/ppermute | solution.py:29
  83.3 1.9 %all-to-all-done.1 = f32[16,8,640]{2,1,0:T(8,128)S(1)} async-done(((f32[16,8,640]{2,1,0:T(8,128)}), f32[16,8,640]{2,1,0:T(8,128)S(1)}, u32[]{:S(2)}, u32[]{:S(2)}) %all-to-all-start.1) | async-done | bytes 327712 | tf_op jit(solution)/shard_map/all_to_all | solution.py:47
  85.9 4.5 %all-to-all-start.2 = ((f32[8,8,512]{2,1,0:T(8,128)}), f32[8,8,512]{2,1,0:T(8,128)S(1)}, u32[]{:S(2)}, u32[]{:S(2)}) async-start(f32[8,8,512]{2,1,0:T(8,128)} %broadcast_in_dim.10), calls=%async_computation.2 | async-start | bytes 262144 | tf_op jit(solution)/shard_map/all_to_all | solution.py:47
  90.4 6.8 %collective-permute-done.13.up_ref = bf16[2,8,128,128]{3,2,1,0:T(8,128)(2,1)} collective-permute-done((bf16[2,8,128,128]{3,2,1,0:T(8,128)(2,1)}, bf16[2,8,128,128]{3,2,1,0:T(8,128)(2,1)}, u32[]{:S(2)}, u32[]{:S(2)}) %collective-permute-start.13) | collective-permute-done | bytes 524320 | tf_op jit(solution)/shard_map/ppermute | solution.py:29
  97.3 2.1 %merge.1 = bf16[1024,128]{1,0:T(8,128)(2,1)} custom-call(bf16[3,2,8,128,128]{4,3,2,1,0:T(8,128)(2,1)S(1)} %bitcast.40, bf16[3,2,8,128,128]{4,3,2,1,0:T(8,128)(2,1)S(1)} %bitcast.42, bf16[2,8,128,128]{3,2,1,0:T(8,128)(2,1)} %collective-permute-done.13.up_ref, bf16[2,8,128,128]{3,2,1,0:T(8,128)(2,1)} %collective-permute-done.14.down_ref), custom_call_target="tpu_custom_call" | custom-call | flops 1048576 | bytes 2097152 | tf_op jit(solution)/shard_map/merge/pallas_call | solution.py:292
  99.4 1.1 collective-permute-start.15
  100.5 1.3 %slice_bitcast_fusion = f32[512]{0:T(512)} fusion(f32[8,640]{1,0:T(8,128)} %copy-done.4), kind=kLoop, calls=%fused_computation.44 | loop fusion | bytes 4096 | tf_op jit(solution)/shard_map/reshape | solution.py:290
  101.8 6.4 %collective-permute-done.15.last_ref = bf16[1024,128]{1,0:T(8,128)(2,1)S(1)} collective-permute-done((bf16[1024,128]{1,0:T(8,128)(2,1)}, bf16[1024,128]{1,0:T(8,128)(2,1)S(1)}, u32[]{:S(2)}, u32[]{:S(2)}) %collective-permute-start.15) | collective-permute-done | bytes 262176 | tf_op jit(solution)/shard_map/ppermute | solution.py:29
  108.2 2.8 %final.1 = f32[1024,128]{1,0:T(8,128)} custom-call(bf16[3,2,8,128,128]{4,3,2,1,0:T(8,128)(2,1)S(1)} %bitcast.41, bf16[3,2,8,128,128]{4,3,2,1,0:T(8,128)(2,1)S(1)} %bitcast.43, bf16[2,8,128,128]{3,2,1,0:T(8,128)(2,1)} %collective-permute-done.13.up_ref, bf16[2,8,128,128]{3,2,1,0:T(8,128)(2,1)} %collective-permute-done.14.down_ref, ...), custom_call_target="tpu_custom_call" | custom-call | flops 1048576 | bytes 2097152 | tf_op jit(solution)/shard_map/final/pallas_call | solution.py:319
  (54 shorter events, 4.3 us)
Async XLA Ops:
  0.6 11.2 %collective-permute-start.1 = (bf16[1024,128]{1,0:T(8,128)(2,1)}, bf16[1024,128]{1,0:T(8,128)(2,1)S(1)}, u32[]{:S(2)}, u32[]{:S(2)}) collective-permute-start(bf16[1024,128]{1,0:T(8,128)(2,1)} %param.7), channel_id=1, source_target_pairs={{0,2},{1,3},{2,0},{3,1},{4,6},{5,7},{6,4},{7,5},{8,10},{9,11},{10,... | collective-permute-start | bytes 786440 | tf_op jit(solution)/shard_map/ppermute | solution.py:29
  3.0 24.7 %collective-permute-start = (bf16[1024,128]{1,0:T(8,128)(2,1)}, bf16[1024,128]{1,0:T(8,128)(2,1)S(1)}, u32[]{:S(2)}, u32[]{:S(2)}) collective-permute-start(bf16[1024,128]{1,0:T(8,128)(2,1)} %param.7), channel_id=1, source_target_pairs={{0,4},{1,5},{2,6},{3,7},{4,8},{5,9},{6,10},{7,11},{8,12},{9,13},{1... | collective-permute-start | bytes 786440 | tf_op jit(solution)/shard_map/ppermute | solution.py:29
  4.5 23.3 %collective-permute-start.3 = (bf16[1024,128]{1,0:T(8,128)(2,1)}, bf16[1024,128]{1,0:T(8,128)(2,1)S(1)}, u32[]{:S(2)}, u32[]{:S(2)}) collective-permute-start(bf16[1024,128]{1,0:T(8,128)(2,1)} %param.7), channel_id=1, source_target_pairs={{0,252},{1,253},{2,254},{3,255},{4,0},{5,1},{6,2},{7,3},{8,4},{9,5... | collective-permute-start | bytes 786440 | tf_op jit(solution)/shard_map/ppermute | solution.py:29
  11.9 21.4 %collective-permute-start.7 = (bf16[1024,128]{1,0:T(8,128)(2,1)}, bf16[1024,128]{1,0:T(8,128)(2,1)S(1)}, u32[]{:S(2)}, u32[]{:S(2)}) collective-permute-start(bf16[1024,128]{1,0:T(8,128)(2,1)} %param.7), channel_id=1, source_target_pairs={{0,1},{1,0},{2,3},{3,2},{4,5},{5,4},{6,7},{7,6},{8,9},{9,8},{10,11... | collective-permute-start | bytes 786440 | tf_op jit(solution)/shard_map/ppermute | solution.py:29
  11.9 16.5 %collective-permute-start.2 = (bf16[1024,128]{1,0:T(8,128)(2,1)S(1)}, bf16[1024,128]{1,0:T(8,128)(2,1)S(1)}, u32[]{:S(2)}, u32[]{:S(2)}) collective-permute-start(bf16[1024,128]{1,0:T(8,128)(2,1)S(1)} %collective-permute-done.1), channel_id=1, source_target_pairs={{0,4},{1,5},{2,6},{3,7},{4,8},{5,9},{6,10},{7,11},{8,12},{9,13},{1... | collective-permute-start | bytes 786440 | tf_op jit(solution)/shard_map/ppermute | solution.py:29
  12.7 15.8 %copy-start.3 = (bf16[1024,128]{1,0:T(8,128)(2,1)S(1)}, bf16[1024,128]{1,0:T(8,128)(2,1)}, u32[]{:S(2)}) copy-start(bf16[1024,128]{1,0:T(8,128)(2,1)} %param.7) | copy-start | bytes 786436
  16.2 17.4 %copy-start = (bf16[1024,512]{1,0:T(8,128)(2,1)S(1)}, bf16[1024,512]{1,0:T(8,128)(2,1)}, u32[]{:S(2)}) copy-start(bf16[1024,512]{1,0:T(8,128)(2,1)} %grad_ref.1) | copy-start | bytes 3145732
  16.3 17.4 %copy-start.1 = (bf16[128,512]{1,0:T(8,128)(2,1)S(1)}, bf16[128,512]{1,0:T(8,128)(2,1)}, u32[]{:S(2)}) copy-start(bf16[128,512]{1,0:T(8,128)(2,1)} %weight_ref.1) | copy-start | bytes 393220
  16.3 17.4 %copy-start.2 = (f32[512]{0:T(512)S(1)}, f32[512]{0:T(512)}, u32[]{:S(2)}) copy-start(f32[512]{0:T(512)} %param.9) | copy-start | bytes 6148
  16.3 15.3 %collective-permute-start.4 = (bf16[1024,128]{1,0:T(8,128)(2,1)S(1)}, bf16[1024,128]{1,0:T(8,128)(2,1)S(1)}, u32[]{:S(2)}, u32[]{:S(2)}) collective-permute-start(bf16[1024,128]{1,0:T(8,128)(2,1)S(1)} %collective-permute-done.1), channel_id=1, source_target_pairs={{0,252},{1,253},{2,254},{3,255},{4,0},{5,1},{6,2},{7,3},{8,4},{9,5... | collective-permute-start | bytes 786440 | tf_op jit(solution)/shard_map/ppermute | solution.py:29
  27.7 3.9 %collective-permute-start.5 = (bf16[1024,128]{1,0:T(8,128)(2,1)S(1)}, bf16[1024,128]{1,0:T(8,128)(2,1)S(1)}, u32[]{:S(2)}, u32[]{:S(2)}) collective-permute-start(bf16[1024,128]{1,0:T(8,128)(2,1)S(1)} %collective-permute-done), channel_id=1, source_target_pairs={{0,1},{1,0},{2,3},{3,2},{4,5},{5,4},{6,7},{7,6},{8,9},{9,8},{10,11... | collective-permute-start | bytes 786440 | tf_op jit(solution)/shard_map/ppermute | solution.py:29
  27.8 5.5 %collective-permute-start.8 = (bf16[1024,128]{1,0:T(8,128)(2,1)S(1)}, bf16[1024,128]{1,0:T(8,128)(2,1)S(1)}, u32[]{:S(2)}, u32[]{:S(2)}) collective-permute-start(bf16[1024,128]{1,0:T(8,128)(2,1)S(1)} %collective-permute-done.1), channel_id=1, source_target_pairs={{0,1},{1,0},{2,3},{3,2},{4,5},{5,4},{6,7},{7,6},{8,9},{9,8},{10,11... | collective-permute-start | bytes 786440 | tf_op jit(solution)/shard_map/ppermute | solution.py:29
  28.4 4.9 %collective-permute-start.9 = (bf16[1024,128]{1,0:T(8,128)(2,1)S(1)}, bf16[1024,128]{1,0:T(8,128)(2,1)S(1)}, u32[]{:S(2)}, u32[]{:S(2)}) collective-permute-start(bf16[1024,128]{1,0:T(8,128)(2,1)S(1)} %collective-permute-done.3), channel_id=1, source_target_pairs={{0,1},{1,0},{2,3},{3,2},{4,5},{5,4},{6,7},{7,6},{8,9},{9,8},{10,11... | collective-permute-start | bytes 786440 | tf_op jit(solution)/shard_map/ppermute | solution.py:29
  31.6 1.5 %collective-permute-start.6 = (bf16[1024,128]{1,0:T(8,128)(2,1)S(1)}, bf16[1024,128]{1,0:T(8,128)(2,1)S(1)}, u32[]{:S(2)}, u32[]{:S(2)}) collective-permute-start(bf16[1024,128]{1,0:T(8,128)(2,1)S(1)} %collective-permute-done.2), channel_id=1, source_target_pairs={{0,1},{1,0},{2,3},{3,2},{4,5},{5,4},{6,7},{7,6},{8,9},{9,8},{10,11... | collective-permute-start | bytes 786440 | tf_op jit(solution)/shard_map/ppermute | solution.py:29
  31.7 1.9 %collective-permute-start.10 = (bf16[1024,128]{1,0:T(8,128)(2,1)S(1)}, bf16[1024,128]{1,0:T(8,128)(2,1)S(1)}, u32[]{:S(2)}, u32[]{:S(2)}) collective-permute-start(bf16[1024,128]{1,0:T(8,128)(2,1)S(1)} %collective-permute-done.4), channel_id=1, source_target_pairs={{0,1},{1,0},{2,3},{3,2},{4,5},{5,4},{6,7},{7,6},{8,9},{9,8},{10,11... | collective-permute-start | bytes 786440 | tf_op jit(solution)/shard_map/ppermute | solution.py:29
  49.1 16.5 %collective-permute-start.12 = (bf16[48,128,128]{2,1,0:T(8,128)(2,1)}, bf16[48,128,128]{2,1,0:T(8,128)(2,1)S(1)}, u32[]{:S(2)}, u32[]{:S(2)}) collective-permute-start(bf16[48,128,128]{2,1,0:T(8,128)(2,1)} %get-tuple-element.17), channel_id=1, source_target_pairs={{0,1},{1,0},{2,3},{3,2},{4,5},{5,4},{6,7},{7,6},{8,9},{9,8},{10,11... | collective-permute-start | bytes 4718600 | tf_op jit(solution)/shard_map/ppermute | solution.py:29
  49.4 3.6 %collective-permute-start.11 = (f32[8,8,640]{2,1,0:T(8,128)S(1)}, f32[8,8,640]{2,1,0:T(8,128)S(1)}, u32[]{:S(2)}, u32[]{:S(2)}) collective-permute-start(f32[8,8,640]{2,1,0:T(8,128)S(1)} %get-tuple-element.16), channel_id=1, source_target_pairs={{0,1},{1,0},{2,3},{3,2},{4,5},{5,4},{6,7},{7,6},{8,9},{9,8},{10,11... | collective-permute-start | bytes 491528 | tf_op jit(solution)/shard_map/ppermute | solution.py:29
  66.4 18.8 %all-to-all-start.1 = ((f32[16,8,640]{2,1,0:T(8,128)}), f32[16,8,640]{2,1,0:T(8,128)S(1)}, u32[]{:S(2)}, u32[]{:S(2)}) async-start(f32[16,8,640]{2,1,0:T(8,128)} %broadcast_in_dim.9), calls=%async_computation.1 | async-start | bytes 655360 | tf_op jit(solution)/shard_map/all_to_all | solution.py:47
  77.0 20.3 %collective-permute-start.13 = (bf16[2,8,128,128]{3,2,1,0:T(8,128)(2,1)}, bf16[2,8,128,128]{3,2,1,0:T(8,128)(2,1)}, u32[]{:S(2)}, u32[]{:S(2)}) collective-permute-start(bf16[2,8,128,128]{3,2,1,0:T(8,128)(2,1)} %bitcast.17), channel_id=1, source_target_pairs={{0,4},{1,5},{2,6},{3,7},{4,8},{5,9},{6,10},{7,11},{8,12},{9,13},{1... | collective-permute-start | bytes 1572872 | tf_op jit(solution)/shard_map/ppermute | solution.py:29
  77.3 20.0 %collective-permute-start.14 = (bf16[2,8,128,128]{3,2,1,0:T(8,128)(2,1)}, bf16[2,8,128,128]{3,2,1,0:T(8,128)(2,1)}, u32[]{:S(2)}, u32[]{:S(2)}) collective-permute-start(bf16[2,8,128,128]{3,2,1,0:T(8,128)(2,1)} %bitcast.18), channel_id=1, source_target_pairs={{0,252},{1,253},{2,254},{3,255},{4,0},{5,1},{6,2},{7,3},{8,4},{9,5... | collective-permute-start | bytes 1572872 | tf_op jit(solution)/shard_map/ppermute | solution.py:29
  85.2 12.1 %copy-start.4 = (f32[8,640]{1,0:T(8,128)}, f32[8,640]{1,0:T(8,128)S(1)}, u32[]{:S(2)}) copy-start(f32[8,640]{1,0:T(8,128)S(1)} %reduce_sum.19) | copy-start | bytes 61444
  85.9 14.6 %all-to-all-start.2 = ((f32[8,8,512]{2,1,0:T(8,128)}), f32[8,8,512]{2,1,0:T(8,128)S(1)}, u32[]{:S(2)}, u32[]{:S(2)}) async-start(f32[8,8,512]{2,1,0:T(8,128)} %broadcast_in_dim.10), calls=%async_computation.2 | async-start | bytes 262144 | tf_op jit(solution)/shard_map/all_to_all | solution.py:47
  99.4 8.8 %collective-permute-start.15 = (bf16[1024,128]{1,0:T(8,128)(2,1)}, bf16[1024,128]{1,0:T(8,128)(2,1)S(1)}, u32[]{:S(2)}, u32[]{:S(2)}) collective-permute-start(bf16[1024,128]{1,0:T(8,128)(2,1)} %merge.1), channel_id=1, source_target_pairs={{0,2},{1,3},{2,0},{3,1},{4,6},{5,7},{6,4},{7,5},{8,10},{9,11},{10,... | collective-permute-start | bytes 786440 | tf_op jit(solution)/shard_map/ppermute | solution.py:29
  100.5 10.5 %collective-permute-start.16 = (f32[8,8,512]{2,1,0:T(8,128)S(1)}, f32[8,8,512]{2,1,0:T(8,128)S(1)}, u32[]{:S(2)}, u32[]{:S(2)}) collective-permute-start(f32[8,8,512]{2,1,0:T(8,128)S(1)} %all-to-all-done.2), channel_id=1, source_target_pairs={{0,1},{1,0},{2,3},{3,2},{4,5},{5,4},{6,7},{7,6},{8,9},{9,8},{10,11... | collective-permute-start | bytes 393224 | tf_op jit(solution)/shard_map/ppermute | solution.py:29

commit v4 on v3

--- a/solution.py
+++ b/solution.py
@@ -37,8 +37,25 @@
     return sent(value, lambda device, count: device ^ 2)
 
 
+def is_long(first, second, count):
+    half = count // GROUP // SPLIT[0]
+    return first // GROUP // half != second // GROUP // half
+
+
 def to_block(value, steps):
-    return sent(value, lambda device, count: (device + GROUP * steps) % count)
+    count = lax.axis_size(AXES)
+    pairs = [(source, (source + GROUP * steps) % count) for source in range(count)]
+    return lax.ppermute(value, AXES, [pair for pair in pairs if not is_long(*pair, count)])
+
+
+def to_long(value, turn):
+    count = lax.axis_size(AXES)
+    pairs = [
+        (source, ((source + GROUP * steps) % count) ^ turn)
+        for steps in (1, -1)
+        for source in range(count)
+    ]
+    return lax.ppermute(value, AXES, [pair for pair in pairs if is_long(*pair, count)])
 
 
 def to_all(value, axes):
@@ -74,17 +91,17 @@
 
 def turned(refs, index):
     terms = [ref[index].astype(jnp.float32) for ref in refs]
-    return jnp.swapaxes(terms[0] + terms[1] + terms[2] + terms[3], 0, 1)
-
-
-def merge_kernel(keep_ref, core_ref, up_ref, down_ref, out_ref):
-    refs = (keep_ref.at[1, 1], core_ref.at[1, 1], up_ref.at[1], down_ref.at[1])
+    return jnp.swapaxes(sum(terms[1:], terms[0]), 0, 1)
+
+
+def merge_kernel(keep_ref, core_ref, up_ref, down_ref, long_ref, out_ref):
+    refs = (keep_ref.at[1, 1], core_ref.at[1, 1], up_ref.at[1], down_ref.at[1], long_ref.at[1])
     for tile in range(PIECE_TILES):
         out_ref[tile * TILE : (tile + 1) * TILE, :] = turned(refs, tile).astype(jnp.bfloat16)
 
 
-def final_kernel(keep_ref, core_ref, up_ref, down_ref, last_ref, out_ref):
-    refs = (keep_ref.at[1, 0], core_ref.at[1, 0], up_ref.at[0], down_ref.at[0])
+def final_kernel(keep_ref, core_ref, up_ref, down_ref, long_ref, last_ref, out_ref):
+    refs = (keep_ref.at[1, 0], core_ref.at[1, 0], up_ref.at[0], down_ref.at[0], long_ref.at[0])
     count = out_ref.shape[0] // TILE
     for sub in range(count):
         tile = pl.program_id(0) * count + sub
@@ -188,12 +205,22 @@
     chunk_rows = in_dim // (2 * chunks)
     step_rows = STEP_TILES * TILE
 
+    block = lax.axis_index(("y_lo", "z", "x"))
+    half_blocks = lax.axis_size(("z", "x"))
+    is_ends = {-1: block % half_blocks == 0, 1: block % half_blocks == half_blocks - 1}
     other_row = to_row(features)
     pieces = {0: (features, other_row)}
+    direct = {}
     for steps in (1, -1):
-        near = to_block(features, steps)
-        far = to_block(other_row, steps)
-        pieces[-steps] = (near, far)
+        direct[steps] = to_block(features, steps)
+    long_one = to_long(features, 0)
+    long_two = to_long(features, 2)
+    for steps in (1, -1):
+        crossed = to_block(other_row, steps)
+        pieces[-steps] = (
+            jnp.where(is_ends[-steps], long_one, direct[steps]),
+            jnp.where(is_ends[-steps], long_two, crossed),
+        )
     near = [piece for offset in (-1, 0, 1) for piece in pieces[offset]]
     far = [to_core(piece) for piece in near]
     blank = jnp.zeros_like(features)
@@ -281,36 +308,34 @@
     part = jnp.sum(lax.all_to_all(part, NEAR, 0, 0, tiled=True), axis=0)
     part, from_core = lax.optimization_barrier((part, from_core))
     keep, from_core = (value.reshape(3, 2, -1, in_dim, TILE) for value in (keep, from_core))
-    moved = []
+    moved, terms = [], {}
     for steps in (1, -1):
-        term = wide(keep[1 + steps]) + wide(from_core[1 + steps])
-        moved.append(to_block(term.astype(jnp.bfloat16), steps))
+        terms[steps] = (wide(keep[1 + steps]) + wide(from_core[1 + steps])).astype(jnp.bfloat16)
+        moved.append(to_block(terms[steps], steps))
+    moved.append(to_long(jnp.where(is_ends[-1], terms[-1], terms[1]), 0))
     part = to_all(part, FAR)
     part = jnp.sum(part, axis=0)
     bias_grad = part[: out_dim // TILE, out_dim:].reshape(out_dim)
-    operands = (keep, from_core, moved[0], moved[1])
+    operands = (keep, from_core, *moved)
     other = pl.pallas_call(
         merge_kernel,
         out_shape=jax.ShapeDtypeStruct((rows_dev, in_dim), jnp.bfloat16),
-        in_specs=[whole] * 4,
+        in_specs=[whole] * 5,
         out_specs=whole,
         compiler_params=pltpu.CompilerParams(vmem_limit_bytes=6 << 20),
         cost_estimate=pl.CostEstimate(flops=1 << 20, bytes_accessed=2 << 20, transcendentals=0),
         name="merge",
     )(*operands)
     last = to_row(other)
-    mine = to_all(part[:, :out_dim], NEAR)
-    theirs = to_core(mine)
-    odd = core == 1
-    weight_grad = jnp.stack([jnp.where(odd, theirs, mine), jnp.where(odd, mine, theirs)], axis=1)
-    weight_grad = weight_grad.reshape(in_dim, out_dim)
+    mine = to_all(part[:, :out_dim], (*NEAR, "core"))
+    weight_grad = mine.reshape(in_dim, out_dim)
     final_tiles = 2
     rows_spec = pl.BlockSpec((final_tiles * TILE, in_dim), lambda i: (i, 0))
     final = pl.pallas_call(
         final_kernel,
         out_shape=jax.ShapeDtypeStruct((rows_dev, in_dim), jnp.float32),
         grid=(PIECE_TILES // final_tiles,),
-        in_specs=[whole] * 5,
+        in_specs=[whole] * 6,
         out_specs=rows_spec,
         compiler_params=pltpu.CompilerParams(vmem_limit_bytes=6 << 20),
         cost_estimate=pl.CostEstimate(flops=1 << 20, bytes_accessed=2 << 20, transcendentals=0),

time: 112 us -> 127 us (1.13)
  the two profiles are of different devices: /device:TPU:8 before, /device:TPU:1 now
where the time goes in v4:
time: 127 us; the launch traced here: 126 us
  starting transfers between devices  50.6 us (40%)
  waiting for transfers between devices  31.8 us (25%)
  Pallas kernels  21.8 us (17%)
  blocking collectives  9.38 us (7%)
  local copies, waits for them, and re-layouts  8.74 us (7%)
  other arithmetic  2.66 us (2%)
    ppermute x3, waiting for transfers between devices, to_long(): lax.ppermute(value, AXES, [pair for pair in pairs if is_long(*pair, count)])  17.3 us
    ppermute x3, starting transfers between devices, to_long(): lax.ppermute(value, AXES, [pair for pair in pairs if is_long(*pair, count)])  16 us
    all_to_all x2, starting transfers between devices, to_all(): return lax.all_to_all(copies, axes, 0, 0, tiled=True)  13.7 us
    ppermute x10, starting transfers between devices, sent(): lax.ppermute(value, AXES, [(source, target(source, count)) for source in...  11.3 us
    ppermute x6, starting transfers between devices, to_block(): lax.ppermute(value, AXES, [pair for pair in pairs if not is_long(*pair, c...  9.6 us
    all_to_all x1, blocking collectives, layer(): part = jnp.sum(lax.all_to_all(part, NEAR, 0, 0, tiled=True), axis=0)  9.38 us
    pallas_call x1, Pallas kernels, layer(): pl.pallas_call(functools.partial(forward_kernel, factor), out_shape=(jax....  9.12 us
    ppermute x6, waiting for transfers between devices, to_block(): lax.ppermute(value, AXES, [pair for pair in pairs if not is_long(*pair, c...  7.19 us
  transfers between devices with their start and end apart: 21, of which 7 were waited for; matrix products, arithmetic and copies ran while one was open for 3% of the time, Pallas kernels for 5%

profile of v4, /device:TPU:1, one launch (start us, length us, event | category | flops | bytes accessed | tf_op | source)
XLA Modules:
  0.0 125.9 jit_solution(1458600351194261926)
XLA Ops:
  0.6 3.8 %collective-permute-start.3 = (bf16[1024,128]{1,0:T(8,128)(2,1)}, bf16[1024,128]{1,0:T(8,128)(2,1)S(1)}, u32[]{:S(2)}, u32[]{:S(2)}) collective-permute-start(bf16[1024,128]{1,0:T(8,128)(2,1)} %param.7), channel_id=1, source_target_pairs={{0,2},{1,3},{2,0},{3,1},{4,6},{5,7},{6,4},{7,5},{8,10},{9,11},{10,... | collective-permute-start | bytes 786440 | tf_op jit(solution)/shard_map/ppermute | solution.py:29
  4.5 3.1 %collective-permute-start.1 = (bf16[1024,128]{1,0:T(8,128)(2,1)}, bf16[1024,128]{1,0:T(8,128)(2,1)S(1)}, u32[]{:S(2)}, u32[]{:S(2)}) collective-permute-start(bf16[1024,128]{1,0:T(8,128)(2,1)} %param.7), channel_id=1, source_target_pairs={{0,4},{1,5},{2,6},{3,7},{4,8},{5,9},{6,10},{7,11},{8,12},{9,13},{1... | collective-permute-start | bytes 786440 | tf_op jit(solution)/shard_map/ppermute | solution.py:48
  7.6 8.0 %collective-permute-start = (bf16[1024,128]{1,0:T(8,128)(2,1)}, bf16[1024,128]{1,0:T(8,128)(2,1)S(1)}, u32[]{:S(2)}, u32[]{:S(2)}) collective-permute-start(bf16[1024,128]{1,0:T(8,128)(2,1)} %param.7), channel_id=1, source_target_pairs={{124,128},{125,129},{126,130},{127,131},{252,0},{253,1},{254,2},{2... | collective-permute-start | bytes 786440 | tf_op jit(solution)/shard_map/ppermute | solution.py:58
  15.5 2.3 %collective-permute-start.2 = (bf16[1024,128]{1,0:T(8,128)(2,1)}, bf16[1024,128]{1,0:T(8,128)(2,1)S(1)}, u32[]{:S(2)}, u32[]{:S(2)}) collective-permute-start(bf16[1024,128]{1,0:T(8,128)(2,1)} %param.7), channel_id=1, source_target_pairs={{124,130},{125,131},{126,128},{127,129},{252,2},{253,3},{254,0},{2... | collective-permute-start | bytes 786440 | tf_op jit(solution)/shard_map/ppermute | solution.py:58
  17.8 1.3 %collective-permute-start.9 = (bf16[1024,128]{1,0:T(8,128)(2,1)}, bf16[1024,128]{1,0:T(8,128)(2,1)S(1)}, u32[]{:S(2)}, u32[]{:S(2)}) collective-permute-start(bf16[1024,128]{1,0:T(8,128)(2,1)} %param.7), channel_id=1, source_target_pairs={{0,1},{1,0},{2,3},{3,2},{4,5},{5,4},{6,7},{7,6},{8,9},{9,8},{10,11... | collective-permute-start | bytes 786440 | tf_op jit(solution)/shard_map/ppermute | solution.py:29
  19.2 1.3 %collective-permute-start.4 = (bf16[1024,128]{1,0:T(8,128)(2,1)S(1)}, bf16[1024,128]{1,0:T(8,128)(2,1)S(1)}, u32[]{:S(2)}, u32[]{:S(2)}) collective-permute-start(bf16[1024,128]{1,0:T(8,128)(2,1)S(1)} %collective-permute-done.3), channel_id=1, source_target_pairs={{0,4},{1,5},{2,6},{3,7},{4,8},{5,9},{6,10},{7,11},{8,12},{9,13},{1... | collective-permute-start | bytes 786440 | tf_op jit(solution)/shard_map/ppermute | solution.py:48
  21.2 3.5 %load.1.values_ref = bf16[1024,4096]{1,0:T(8,128)(2,1)S(1)} custom-call(bf16[1024,4096]{1,0:T(8,128)(2,1)} %source_ref.1), custom_call_target="tpu_custom_call" | custom-call | bytes 16777216 | tf_op jit(solution)/shard_map/load/pallas_call | solution.py:247
  26.3 3.4 %collective-permute-done.2 = bf16[1024,128]{1,0:T(8,128)(2,1)S(1)} collective-permute-done((bf16[1024,128]{1,0:T(8,128)(2,1)}, bf16[1024,128]{1,0:T(8,128)(2,1)S(1)}, u32[]{:S(2)}, u32[]{:S(2)}) %collective-permute-start.2) | collective-permute-done | bytes 262176 | tf_op jit(solution)/shard_map/ppermute | solution.py:58
  29.7 2.1 %collective-permute-start.10 = (bf16[1024,128]{1,0:T(8,128)(2,1)S(1)}, bf16[1024,128]{1,0:T(8,128)(2,1)S(1)}, u32[]{:S(2)}, u32[]{:S(2)}) collective-permute-start(bf16[1024,128]{1,0:T(8,128)(2,1)S(1)} %collective-permute-done.3), channel_id=1, source_target_pairs={{0,1},{1,0},{2,3},{3,2},{4,5},{5,4},{6,7},{7,6},{8,9},{9,8},{10,11... | collective-permute-start | bytes 786440 | tf_op jit(solution)/shard_map/ppermute | solution.py:29
  35.5 6.0 %collective-permute-done.6 = bf16[1024,128]{1,0:T(8,128)(2,1)S(1)} collective-permute-done((bf16[1024,128]{1,0:T(8,128)(2,1)S(1)}, bf16[1024,128]{1,0:T(8,128)(2,1)S(1)}, u32[]{:S(2)}, u32[]{:S(2)}) %collective-permute-start.6) | collective-permute-done | bytes 262176 | tf_op jit(solution)/shard_map/ppermute | solution.py:48
  44.3 9.1 %forward.1 = (bf16[1024,512]{1,0:T(8,128)(2,1)}, bf16[8,128,128]{2,1,0:T(8,128)(2,1)S(1)}, f32[8,8,640]{2,1,0:T(8,128)S(1)}, f32[8,8,640]{2,1,0:T(8,128)S(1)}) custom-call(s32[8,32]{1,0:T(8,128)S(1)} %fusion.6.place_ref, s32[1]{0:T(128)} %bitcast.core_ref, bf16[104,128,128]{2,1,0:T(8,128)(2,1)S(1)} %bitcast.38, bf16[1024,4096]{1,0:T(8,128)(2,1)S(1)} %load.1.values_ref, ...), custom_call_target="tpu_custom_call" | custom-call | flops 3221225472 | bytes 15728640 | tf_op jit(solution)/shard_map/forward/pallas_call | solution.py:249
  53.5 6.3 %backward.1 = (bf16[48,128,128]{2,1,0:T(8,128)(2,1)S(1)}, bf16[48,128,128]{2,1,0:T(8,128)(2,1)}) custom-call(s32[8,32]{1,0:T(8,128)S(1)} %fusion.6.place_ref, bf16[8,128,128]{2,1,0:T(8,128)(2,1)S(1)} %get-tuple-element.13.back_ref, bf16[1024,4096]{1,0:T(8,128)(2,1)S(1)} %load.1.values_ref), custom_call_target="tpu_custom_call" | custom-call | flops 2147483648 | bytes 12582912 | tf_op jit(solution)/shard_map/backward/pallas_call | solution.py:302
  60.3 3.3 %collective-permute-done.13 = f32[8,8,640]{2,1,0:T(8,128)S(1)} collective-permute-done((f32[8,8,640]{2,1,0:T(8,128)S(1)}, f32[8,8,640]{2,1,0:T(8,128)S(1)}, u32[]{:S(2)}, u32[]{:S(2)}) %collective-permute-start.13) | collective-permute-done | bytes 163872 | tf_op jit(solution)/shard_map/ppermute | solution.py:29
  63.6 9.4 %all_to_all.15 = f32[8,8,640]{2,1,0:T(8,128)S(1)} all-to-all(f32[8,8,640]{2,1,0:T(8,128)S(1)} %add.55), channel_id=1, replica_groups=mesh['y_lo'=2,'z'=8,'x'=4,'y_hi'=2,'core'=2] {'x','y_hi'}, dimensions={0} | all-to-all | bytes 327680 | tf_op jit(solution)/shard_map/all_to_all | solution.py:308
  73.8 8.0 %all-to-all-start.1 = ((f32[16,8,640]{2,1,0:T(8,128)}), f32[16,8,640]{2,1,0:T(8,128)}, u32[]{:S(2)}, u32[]{:S(2)}) async-start(f32[16,8,640]{2,1,0:T(8,128)} %broadcast_in_dim.9), calls=%async_computation.1 | async-start | bytes 655360 | tf_op jit(solution)/shard_map/all_to_all | solution.py:64
  82.2 5.7 %collective-permute-start.17 = (bf16[2,8,128,128]{3,2,1,0:T(8,128)(2,1)S(1)}, bf16[2,8,128,128]{3,2,1,0:T(8,128)(2,1)S(1)}, u32[]{:S(2)}, u32[]{:S(2)}) collective-permute-start(bf16[2,8,128,128]{3,2,1,0:T(8,128)(2,1)S(1)} %broadcast_select_fusion), channel_id=1, source_target_pairs={{124,128},{125,129},{126,130},{127,131},{252,0},{253,1},{254,2},{2... | collective-permute-start | bytes 1572872 | tf_op jit(solution)/shard_map/ppermute | solution.py:58
  88.0 1.3 %collective-permute-start.15 = (bf16[2,8,128,128]{3,2,1,0:T(8,128)(2,1)S(1)}, bf16[2,8,128,128]{3,2,1,0:T(8,128)(2,1)S(1)}, u32[]{:S(2)}, u32[]{:S(2)}) collective-permute-start(bf16[2,8,128,128]{3,2,1,0:T(8,128)(2,1)S(1)} %bitcast.43), channel_id=1, source_target_pairs={{0,4},{1,5},{2,6},{3,7},{4,8},{5,9},{6,10},{7,11},{8,12},{9,13},{1... | collective-permute-start | bytes 1572872 | tf_op jit(solution)/shard_map/ppermute | solution.py:48
  89.3 1.3 %collective-permute-start.16 = (bf16[2,8,128,128]{3,2,1,0:T(8,128)(2,1)S(1)}, bf16[2,8,128,128]{3,2,1,0:T(8,128)(2,1)S(1)}, u32[]{:S(2)}, u32[]{:S(2)}) collective-permute-start(bf16[2,8,128,128]{3,2,1,0:T(8,128)(2,1)S(1)} %bitcast.41), channel_id=1, source_target_pairs={{4,0},{5,1},{6,2},{7,3},{8,4},{9,5},{10,6},{11,7},{12,8},{13,9},{1... | collective-permute-start | bytes 1572872 | tf_op jit(solution)/shard_map/ppermute | solution.py:48
  90.6 13.9 %collective-permute-done.17.long_ref = bf16[2,8,128,128]{3,2,1,0:T(8,128)(2,1)S(1)} collective-permute-done((bf16[2,8,128,128]{3,2,1,0:T(8,128)(2,1)S(1)}, bf16[2,8,128,128]{3,2,1,0:T(8,128)(2,1)S(1)}, u32[]{:S(2)}, u32[]{:S(2)}) %collective-permute-start.17) | collective-permute-done | bytes 524320 | tf_op jit(solution)/shard_map/ppermute | solution.py:58
  106.2 1.5 %collective-permute-start.18 = (bf16[1024,128]{1,0:T(8,128)(2,1)S(1)}, bf16[1024,128]{1,0:T(8,128)(2,1)}, u32[]{:S(2)}, u32[]{:S(2)}) collective-permute-start(bf16[1024,128]{1,0:T(8,128)(2,1)S(1)} %merge.1), channel_id=1, source_target_pairs={{0,2},{1,3},{2,0},{3,1},{4,6},{5,7},{6,4},{7,5},{8,10},{9,11},{10,... | collective-permute-start | bytes 786440 | tf_op jit(solution)/shard_map/ppermute | solution.py:29
  109.5 5.7 %all-to-all-start.2 = ((f32[16,8,512]{2,1,0:T(8,128)}), f32[16,8,512]{2,1,0:T(8,128)}, u32[]{:S(2)}, u32[]{:S(2)}) async-start(f32[16,8,512]{2,1,0:T(8,128)} %broadcast_in_dim.10), calls=%async_computation.2 | async-start | bytes 524288 | tf_op jit(solution)/shard_map/all_to_all | solution.py:64
  118.9 2.6 %final.1 = f32[1024,128]{1,0:T(8,128)} custom-call(bf16[3,2,8,128,128]{4,3,2,1,0:T(8,128)(2,1)S(1)} %bitcast.35, bf16[3,2,8,128,128]{4,3,2,1,0:T(8,128)(2,1)S(1)} %bitcast.37, bf16[2,8,128,128]{3,2,1,0:T(8,128)(2,1)S(1)} %copy-done.3, bf16[2,8,128,128]{3,2,1,0:T(8,128)(2,1)S(1)} %copy-done.5, bf16[2,8,128,128]{3,2,1,0:T(8,128)(2,1)S(1)} %copy-done.1, ...), custom_call_target="tpu_custom_call" | custom-call | flops 1048576 | bytes 2097152 | tf_op jit(solution)/shard_map/final/pallas_call | solution.py:344
  121.5 2.7 %all-to-all-done.2 = f32[16,8,512]{2,1,0:T(8,128)} async-done(((f32[16,8,512]{2,1,0:T(8,128)}), f32[16,8,512]{2,1,0:T(8,128)}, u32[]{:S(2)}, u32[]{:S(2)}) %all-to-all-start.2) | async-done | bytes 262176 | tf_op jit(solution)/shard_map/all_to_all | solution.py:64
  124.2 1.7 %copy.24 = f32[128,512]{1,0:T(8,128)} copy(f32[128,512]{1,0:T(8,128)} %bitcast.19) | data formatting | bytes 524288
  (68 shorter events, 17.5 us)
Async XLA Ops:
  0.6 18.5 %collective-permute-start.3 = (bf16[1024,128]{1,0:T(8,128)(2,1)}, bf16[1024,128]{1,0:T(8,128)(2,1)S(1)}, u32[]{:S(2)}, u32[]{:S(2)}) collective-permute-start(bf16[1024,128]{1,0:T(8,128)(2,1)} %param.7), channel_id=1, source_target_pairs={{0,2},{1,3},{2,0},{3,1},{4,6},{5,7},{6,4},{7,5},{8,10},{9,11},{10,... | collective-permute-start | bytes 786440 | tf_op jit(solution)/shard_map/ppermute | solution.py:29
  4.5 20.3 %collective-permute-start.1 = (bf16[1024,128]{1,0:T(8,128)(2,1)}, bf16[1024,128]{1,0:T(8,128)(2,1)S(1)}, u32[]{:S(2)}, u32[]{:S(2)}) collective-permute-start(bf16[1024,128]{1,0:T(8,128)(2,1)} %param.7), channel_id=1, source_target_pairs={{0,4},{1,5},{2,6},{3,7},{4,8},{5,9},{6,10},{7,11},{8,12},{9,13},{1... | collective-permute-start | bytes 786440 | tf_op jit(solution)/shard_map/ppermute | solution.py:48
  7.6 18.5 %collective-permute-start = (bf16[1024,128]{1,0:T(8,128)(2,1)}, bf16[1024,128]{1,0:T(8,128)(2,1)S(1)}, u32[]{:S(2)}, u32[]{:S(2)}) collective-permute-start(bf16[1024,128]{1,0:T(8,128)(2,1)} %param.7), channel_id=1, source_target_pairs={{124,128},{125,129},{126,130},{127,131},{252,0},{253,1},{254,2},{2... | collective-permute-start | bytes 786440 | tf_op jit(solution)/shard_map/ppermute | solution.py:58
  15.5 14.2 %collective-permute-start.2 = (bf16[1024,128]{1,0:T(8,128)(2,1)}, bf16[1024,128]{1,0:T(8,128)(2,1)S(1)}, u32[]{:S(2)}, u32[]{:S(2)}) collective-permute-start(bf16[1024,128]{1,0:T(8,128)(2,1)} %param.7), channel_id=1, source_target_pairs={{124,130},{125,131},{126,128},{127,129},{252,2},{253,3},{254,0},{2... | collective-permute-start | bytes 786440 | tf_op jit(solution)/shard_map/ppermute | solution.py:58
  17.8 25.0 %collective-permute-start.9 = (bf16[1024,128]{1,0:T(8,128)(2,1)}, bf16[1024,128]{1,0:T(8,128)(2,1)S(1)}, u32[]{:S(2)}, u32[]{:S(2)}) collective-permute-start(bf16[1024,128]{1,0:T(8,128)(2,1)} %param.7), channel_id=1, source_target_pairs={{0,1},{1,0},{2,3},{3,2},{4,5},{5,4},{6,7},{7,6},{8,9},{9,8},{10,11... | collective-permute-start | bytes 786440 | tf_op jit(solution)/shard_map/ppermute | solution.py:29
  19.2 12.6 %collective-permute-start.4 = (bf16[1024,128]{1,0:T(8,128)(2,1)S(1)}, bf16[1024,128]{1,0:T(8,128)(2,1)S(1)}, u32[]{:S(2)}, u32[]{:S(2)}) collective-permute-start(bf16[1024,128]{1,0:T(8,128)(2,1)S(1)} %collective-permute-done.3), channel_id=1, source_target_pairs={{0,4},{1,5},{2,6},{3,7},{4,8},{5,9},{6,10},{7,11},{8,12},{9,13},{1... | collective-permute-start | bytes 786440 | tf_op jit(solution)/shard_map/ppermute | solution.py:48
  24.8 9.7 %collective-permute-start.5 = (bf16[1024,128]{1,0:T(8,128)(2,1)S(1)}, bf16[1024,128]{1,0:T(8,128)(2,1)S(1)}, u32[]{:S(2)}, u32[]{:S(2)}) collective-permute-start(bf16[1024,128]{1,0:T(8,128)(2,1)S(1)} %copy-done.9), channel_id=1, source_target_pairs={{4,0},{5,1},{6,2},{7,3},{8,4},{9,5},{10,6},{11,7},{12,8},{13,9},{1... | collective-permute-start | bytes 786440 | tf_op jit(solution)/shard_map/ppermute | solution.py:48
  26.2 16.4 %collective-permute-start.7 = (bf16[1024,128]{1,0:T(8,128)(2,1)S(1)}, bf16[1024,128]{1,0:T(8,128)(2,1)S(1)}, u32[]{:S(2)}, u32[]{:S(2)}) collective-permute-start(bf16[1024,128]{1,0:T(8,128)(2,1)S(1)} %get-tuple-element.27), channel_id=1, source_target_pairs={{0,1},{1,0},{2,3},{3,2},{4,5},{5,4},{6,7},{7,6},{8,9},{9,8},{10,11... | collective-permute-start | bytes 786440 | tf_op jit(solution)/shard_map/ppermute | solution.py:29
  29.7 13.2 %collective-permute-start.10 = (bf16[1024,128]{1,0:T(8,128)(2,1)S(1)}, bf16[1024,128]{1,0:T(8,128)(2,1)S(1)}, u32[]{:S(2)}, u32[]{:S(2)}) collective-permute-start(bf16[1024,128]{1,0:T(8,128)(2,1)S(1)} %collective-permute-done.3), channel_id=1, source_target_pairs={{0,1},{1,0},{2,3},{3,2},{4,5},{5,4},{6,7},{7,6},{8,9},{9,8},{10,11... | collective-permute-start | bytes 786440 | tf_op jit(solution)/shard_map/ppermute | solution.py:29
  31.8 9.7 %collective-permute-start.6 = (bf16[1024,128]{1,0:T(8,128)(2,1)S(1)}, bf16[1024,128]{1,0:T(8,128)(2,1)S(1)}, u32[]{:S(2)}, u32[]{:S(2)}) collective-permute-start(bf16[1024,128]{1,0:T(8,128)(2,1)S(1)} %collective-permute-done.3), channel_id=1, source_target_pairs={{4,0},{5,1},{6,2},{7,3},{8,4},{9,5},{10,6},{11,7},{12,8},{13,9},{1... | collective-permute-start | bytes 786440 | tf_op jit(solution)/shard_map/ppermute | solution.py:48
  33.2 11.1 %copy-start.6 = (bf16[1024,512]{1,0:T(8,128)(2,1)S(1)}, bf16[1024,512]{1,0:T(8,128)(2,1)}, u32[]{:S(2)}) copy-start(bf16[1024,512]{1,0:T(8,128)(2,1)} %grad_ref.1) | copy-start | bytes 3145732
  33.2 11.1 %copy-start.7 = (bf16[128,512]{1,0:T(8,128)(2,1)S(1)}, bf16[128,512]{1,0:T(8,128)(2,1)}, u32[]{:S(2)}) copy-start(bf16[128,512]{1,0:T(8,128)(2,1)} %weight_ref.1) | copy-start | bytes 393220
  33.2 11.1 %copy-start.8 = (f32[512]{0:T(512)S(1)}, f32[512]{0:T(512)}, u32[]{:S(2)}) copy-start(f32[512]{0:T(512)} %param.9) | copy-start | bytes 6148
  34.5 8.3 %collective-permute-start.8 = (bf16[1024,128]{1,0:T(8,128)(2,1)S(1)}, bf16[1024,128]{1,0:T(8,128)(2,1)S(1)}, u32[]{:S(2)}, u32[]{:S(2)}) collective-permute-start(bf16[1024,128]{1,0:T(8,128)(2,1)S(1)} %get-tuple-element.25), channel_id=1, source_target_pairs={{0,1},{1,0},{2,3},{3,2},{4,5},{5,4},{6,7},{7,6},{8,9},{9,8},{10,11... | collective-permute-start | bytes 786440 | tf_op jit(solution)/shard_map/ppermute | solution.py:29
  41.7 2.5 %collective-permute-start.12 = (bf16[1024,128]{1,0:T(8,128)(2,1)S(1)}, bf16[1024,128]{1,0:T(8,128)(2,1)S(1)}, u32[]{:S(2)}, u32[]{:S(2)}) collective-permute-start(bf16[1024,128]{1,0:T(8,128)(2,1)S(1)} %get-tuple-element.21), channel_id=1, source_target_pairs={{0,1},{1,0},{2,3},{3,2},{4,5},{5,4},{6,7},{7,6},{8,9},{9,8},{10,11... | collective-permute-start | bytes 786440 | tf_op jit(solution)/shard_map/ppermute | solution.py:29
  42.6 1.5 %collective-permute-start.11 = (bf16[1024,128]{1,0:T(8,128)(2,1)S(1)}, bf16[1024,128]{1,0:T(8,128)(2,1)S(1)}, u32[]{:S(2)}, u32[]{:S(2)}) collective-permute-start(bf16[1024,128]{1,0:T(8,128)(2,1)S(1)} %get-tuple-element.23), channel_id=1, source_target_pairs={{0,1},{1,0},{2,3},{3,2},{4,5},{5,4},{6,7},{7,6},{8,9},{9,8},{10,11... | collective-permute-start | bytes 786440 | tf_op jit(solution)/shard_map/ppermute | solution.py:29
  59.8 13.3 %collective-permute-start.14 = (bf16[48,128,128]{2,1,0:T(8,128)(2,1)}, bf16[48,128,128]{2,1,0:T(8,128)(2,1)S(1)}, u32[]{:S(2)}, u32[]{:S(2)}) collective-permute-start(bf16[48,128,128]{2,1,0:T(8,128)(2,1)} %get-tuple-element.17), channel_id=1, source_target_pairs={{0,1},{1,0},{2,3},{3,2},{4,5},{5,4},{6,7},{7,6},{8,9},{9,8},{10,11... | collective-permute-start | bytes 4718600 | tf_op jit(solution)/shard_map/ppermute | solution.py:29
  60.1 3.5 %collective-permute-start.13 = (f32[8,8,640]{2,1,0:T(8,128)S(1)}, f32[8,8,640]{2,1,0:T(8,128)S(1)}, u32[]{:S(2)}, u32[]{:S(2)}) collective-permute-start(f32[8,8,640]{2,1,0:T(8,128)S(1)} %get-tuple-element.16), channel_id=1, source_target_pairs={{0,1},{1,0},{2,3},{3,2},{4,5},{5,4},{6,7},{7,6},{8,9},{9,8},{10,11... | collective-permute-start | bytes 491528 | tf_op jit(solution)/shard_map/ppermute | solution.py:29
  73.8 33.9 %all-to-all-start.1 = ((f32[16,8,640]{2,1,0:T(8,128)}), f32[16,8,640]{2,1,0:T(8,128)}, u32[]{:S(2)}, u32[]{:S(2)}) async-start(f32[16,8,640]{2,1,0:T(8,128)} %broadcast_in_dim.9), calls=%async_computation.1 | async-start | bytes 655360 | tf_op jit(solution)/shard_map/all_to_all | solution.py:64
  82.2 22.2 %collective-permute-start.17 = (bf16[2,8,128,128]{3,2,1,0:T(8,128)(2,1)S(1)}, bf16[2,8,128,128]{3,2,1,0:T(8,128)(2,1)S(1)}, u32[]{:S(2)}, u32[]{:S(2)}) collective-permute-start(bf16[2,8,128,128]{3,2,1,0:T(8,128)(2,1)S(1)} %broadcast_select_fusion), channel_id=1, source_target_pairs={{124,128},{125,129},{126,130},{127,131},{252,0},{253,1},{254,2},{2... | collective-permute-start | bytes 1572872 | tf_op jit(solution)/shard_map/ppermute | solution.py:58
  88.0 16.5 %collective-permute-start.15 = (bf16[2,8,128,128]{3,2,1,0:T(8,128)(2,1)S(1)}, bf16[2,8,128,128]{3,2,1,0:T(8,128)(2,1)S(1)}, u32[]{:S(2)}, u32[]{:S(2)}) collective-permute-start(bf16[2,8,128,128]{3,2,1,0:T(8,128)(2,1)S(1)} %bitcast.43), channel_id=1, source_target_pairs={{0,4},{1,5},{2,6},{3,7},{4,8},{5,9},{6,10},{7,11},{8,12},{9,13},{1... | collective-permute-start | bytes 1572872 | tf_op jit(solution)/shard_map/ppermute | solution.py:48
  89.3 15.2 %collective-permute-start.16 = (bf16[2,8,128,128]{3,2,1,0:T(8,128)(2,1)S(1)}, bf16[2,8,128,128]{3,2,1,0:T(8,128)(2,1)S(1)}, u32[]{:S(2)}, u32[]{:S(2)}) collective-permute-start(bf16[2,8,128,128]{3,2,1,0:T(8,128)(2,1)S(1)} %bitcast.41), channel_id=1, source_target_pairs={{4,0},{5,1},{6,2},{7,3},{8,4},{9,5},{10,6},{11,7},{12,8},{13,9},{1... | collective-permute-start | bytes 1572872 | tf_op jit(solution)/shard_map/ppermute | solution.py:48
  106.2 9.5 %collective-permute-start.18 = (bf16[1024,128]{1,0:T(8,128)(2,1)S(1)}, bf16[1024,128]{1,0:T(8,128)(2,1)}, u32[]{:S(2)}, u32[]{:S(2)}) collective-permute-start(bf16[1024,128]{1,0:T(8,128)(2,1)S(1)} %merge.1), channel_id=1, source_target_pairs={{0,2},{1,3},{2,0},{3,1},{4,6},{5,7},{6,4},{7,5},{8,10},{9,11},{10,... | collective-permute-start | bytes 786440 | tf_op jit(solution)/shard_map/ppermute | solution.py:29
  109.5 14.7 %all-to-all-start.2 = ((f32[16,8,512]{2,1,0:T(8,128)}), f32[16,8,512]{2,1,0:T(8,128)}, u32[]{:S(2)}, u32[]{:S(2)}) async-start(f32[16,8,512]{2,1,0:T(8,128)} %broadcast_in_dim.10), calls=%async_computation.2 | async-start | bytes 524288 | tf_op jit(solution)/shard_map/all_to_all | solution.py:64
  (7 other events, 9.2 us)

commit v5 on v3

--- a/solution.py
+++ b/solution.py
@@ -21,6 +21,7 @@
 FAR = ("y_lo", "z")
 VMEM_LIMIT = 14 << 20
 SPLIT = (2, 8, 4, 2, 2)
+AHEAD = 3
 STEP_TILES = 1
 
 
@@ -147,27 +148,36 @@
 
 
 def backward_kernel(
-    place_ref, back_ref, values_ref, keep_ref, send_ref, total_ref
+    place_ref, back_ref, source_ref, keep_ref, send_ref, total_ref, held_ref, arrived
 ):
     step = pl.program_id(0)
+    count = held_ref.shape[0]
+
+    def copy(tile):
+        rows = pl.ds(pl.multiple_of(tile * TILE, TILE), TILE)
+        return pltpu.make_async_copy(source_ref.at[rows], held_ref.at[tile], arrived.at[tile])
 
     @pl.when(step == 0)
     def _():
+        for tile in range(AHEAD):
+            copy(tile).start()
         total_ref[...] = jnp.zeros_like(total_ref)
 
-    for sub in range(STEP_TILES):
-        tile = step * STEP_TILES + sub
-        back = back_ref[tile]
-        place = pl.ds(pl.multiple_of(tile * TILE, TILE), TILE)
-        for pair in range(SLOTS // 2):
-            term = jnp.dot(
-                back,
-                values_ref[place, 2 * pair * TILE : (2 * pair + 2) * TILE],
-                preferred_element_type=jnp.float32,
-            )
-            for half in range(2):
-                spot = place_ref[step * STEP_TILES + sub, 2 * pair + half]
-                total_ref[spot] += term[:, half * TILE : (half + 1) * TILE]
+    @pl.when(step + AHEAD < count)
+    def _():
+        copy(step + AHEAD).start()
+
+    copy(step).wait()
+    back = back_ref[step]
+    for pair in range(SLOTS // 2):
+        term = jnp.dot(
+            back,
+            held_ref[step, :, 2 * pair * TILE : (2 * pair + 2) * TILE],
+            preferred_element_type=jnp.float32,
+        )
+        for half in range(2):
+            spot = place_ref[step, 2 * pair + half]
+            total_ref[spot] += term[:, half * TILE : (half + 1) * TILE]
 
     @pl.when(step == pl.num_programs(0) - 1)
     def _():
@@ -217,7 +227,8 @@
         cost_estimate=pl.CostEstimate(flops=0, bytes_accessed=16 << 20, transcendentals=0),
         name="load",
     )
-    tile_values = load(pltpu.with_memory_space_constraint(tile_values, pltpu.HBM))
+    tile_values = pltpu.with_memory_space_constraint(tile_values, pltpu.HBM)
+    near_values = load(tile_values)
     whole = pl.BlockSpec(memory_space=pltpu.VMEM)
     act, back, own_sums, other_sums = pl.pallas_call(
         functools.partial(forward_kernel, factor),
@@ -252,7 +263,7 @@
         compiler_params=pltpu.CompilerParams(vmem_limit_bytes=VMEM_LIMIT),
         cost_estimate=pl.CostEstimate(flops=3 << 30, bytes_accessed=15 << 20, transcendentals=1 << 19),
         name="forward",
-    )(place, core.reshape(1).astype(jnp.int32), window, tile_values, out_grad, weight, bias.reshape(1, -1))
+    )(place, core.reshape(1).astype(jnp.int32), window, near_values, out_grad, weight, bias.reshape(1, -1))
 
     half_tiles = DUMMY // 2
     backward = pl.pallas_call(
@@ -260,15 +271,19 @@
         out_shape=(jax.ShapeDtypeStruct((half_tiles, in_dim, TILE), jnp.bfloat16),) * 2,
         grid_spec=pltpu.PrefetchScalarGridSpec(
             num_scalar_prefetch=1,
-            grid=(row_tiles // STEP_TILES,),
+            grid=(row_tiles,),
             in_specs=[
                 whole,
-                whole,
+                pl.BlockSpec(memory_space=pltpu.HBM),
             ],
             out_specs=(whole,) * 2,
-            scratch_shapes=[pltpu.VMEM((DUMMY + 1, in_dim, TILE), jnp.float32)],
+            scratch_shapes=[
+                pltpu.VMEM((DUMMY + 1, in_dim, TILE), jnp.float32),
+                pltpu.VMEM((row_tiles, TILE, SLOTS * TILE), jnp.bfloat16),
+                pltpu.SemaphoreType.DMA((row_tiles,)),
+            ],
         ),
-        compiler_params=pltpu.CompilerParams(vmem_limit_bytes=VMEM_LIMIT),
+        compiler_params=pltpu.CompilerParams(vmem_limit_bytes=20 << 20),
         cost_estimate=pl.CostEstimate(flops=2 << 30, bytes_accessed=12 << 20, transcendentals=0),
         name="backward",
     )
@@ -278,8 +293,8 @@
     moved_sums = to_core(other_sums)
     part = own_sums + moved_sums
     from_core = to_core(send)
-    part = jnp.sum(lax.all_to_all(part, NEAR, 0, 0, tiled=True), axis=0)
-    part, from_core = lax.optimization_barrier((part, from_core))
+    part = lax.all_to_all(part, NEAR, 0, 0, tiled=True)
+    part = jnp.sum(part, axis=0)
     keep, from_core = (value.reshape(3, 2, -1, in_dim, TILE) for value in (keep, from_core))
     moved = []
     for steps in (1, -1):
@@ -289,7 +304,7 @@
     part = jnp.sum(part, axis=0)
     bias_grad = part[: out_dim // TILE, out_dim:].reshape(out_dim)
     operands = (keep, from_core, moved[0], moved[1])
-    other = pl.pallas_call(
+    merge = pl.pallas_call(
         merge_kernel,
         out_shape=jax.ShapeDtypeStruct((rows_dev, in_dim), jnp.bfloat16),
         in_specs=[whole] * 4,
@@ -297,7 +312,8 @@
         compiler_params=pltpu.CompilerParams(vmem_limit_bytes=6 << 20),
         cost_estimate=pl.CostEstimate(flops=1 << 20, bytes_accessed=2 << 20, transcendentals=0),
         name="merge",
-    )(*operands)
+    )
+    other = merge(*operands)
     last = to_row(other)
     mine = to_all(part[:, :out_dim], NEAR)
     theirs = to_core(mine)

time: 112 us -> 117 us (1.045)
  the two profiles are of different devices: /device:TPU:8 before, /device:TPU:2 now
where the time goes in v5:
time: 117 us; the launch traced here: 115 us
  waiting for transfers between devices  36 us (31%)
  starting transfers between devices  27.1 us (23%)
  Pallas kernels  24.1 us (21%)
  blocking collectives  21.1 us (18%)
  other arithmetic  2.91 us (2%)
  local copies, waits for them, and re-layouts  2.49 us (2%)
    ppermute x17, waiting for transfers between devices, sent(): lax.ppermute(value, AXES, [(source, target(source, count)) for source in...  22.7 us
    all_to_all x1, blocking collectives, layer(): part = lax.all_to_all(part, NEAR, 0, 0, tiled=True)  21.1 us
    all_to_all x2, starting transfers between devices, to_all(): return lax.all_to_all(copies, axes, 0, 0, tiled=True)  14.6 us
    all_to_all x2, waiting for transfers between devices, to_all(): return lax.all_to_all(copies, axes, 0, 0, tiled=True)  13.3 us
    ppermute x17, starting transfers between devices, sent(): lax.ppermute(value, AXES, [(source, target(source, count)) for source in...  12.5 us
    pallas_call x1, Pallas kernels, layer(): pl.pallas_call(functools.partial(forward_kernel, factor), out_shape=(jax....  9.12 us
    pallas_call x1, Pallas kernels, layer(): keep, send = backward(place, back, tile_values)  7.21 us
    pallas_call x1, Pallas kernels, layer(): near_values = load(tile_values)  3.51 us
  transfers between devices with their start and end apart: 19, of which 9 were waited for; matrix products, arithmetic and copies ran while one was open for 5% of the time, Pallas kernels for 4%

profile of v5, /device:TPU:2, one launch (start us, length us, event | category | flops | bytes accessed | tf_op | source)
XLA Modules:
  0.0 114.7 jit_solution(12039009458267443162)
XLA Ops:
  0.6 3.3 %collective-permute-start.1 = (bf16[1024,128]{1,0:T(8,128)(2,1)}, bf16[1024,128]{1,0:T(8,128)(2,1)S(1)}, u32[]{:S(2)}, u32[]{:S(2)}) collective-permute-start(bf16[1024,128]{1,0:T(8,128)(2,1)} %param.7), channel_id=1, source_target_pairs={{0,2},{1,3},{2,0},{3,1},{4,6},{5,7},{6,4},{7,5},{8,10},{9,11},{10,... | collective-permute-start | bytes 786440 | tf_op jit(solution)/shard_map/ppermute | solution.py:30
  3.9 1.5 %collective-permute-start = (bf16[1024,128]{1,0:T(8,128)(2,1)}, bf16[1024,128]{1,0:T(8,128)(2,1)S(1)}, u32[]{:S(2)}, u32[]{:S(2)}) collective-permute-start(bf16[1024,128]{1,0:T(8,128)(2,1)} %param.7), channel_id=1, source_target_pairs={{0,4},{1,5},{2,6},{3,7},{4,8},{5,9},{6,10},{7,11},{8,12},{9,13},{1... | collective-permute-start | bytes 786440 | tf_op jit(solution)/shard_map/ppermute | solution.py:30
  5.9 4.5 %collective-permute-done.1 = bf16[1024,128]{1,0:T(8,128)(2,1)S(1)} collective-permute-done((bf16[1024,128]{1,0:T(8,128)(2,1)}, bf16[1024,128]{1,0:T(8,128)(2,1)S(1)}, u32[]{:S(2)}, u32[]{:S(2)}) %collective-permute-start.1) | collective-permute-done | bytes 262176 | tf_op jit(solution)/shard_map/ppermute | solution.py:30
  10.5 1.5 %collective-permute-start.2 = (bf16[1024,128]{1,0:T(8,128)(2,1)S(1)}, bf16[1024,128]{1,0:T(8,128)(2,1)S(1)}, u32[]{:S(2)}, u32[]{:S(2)}) collective-permute-start(bf16[1024,128]{1,0:T(8,128)(2,1)S(1)} %collective-permute-done.1), channel_id=1, source_target_pairs={{0,4},{1,5},{2,6},{3,7},{4,8},{5,9},{6,10},{7,11},{8,12},{9,13},{1... | collective-permute-start | bytes 786440 | tf_op jit(solution)/shard_map/ppermute | solution.py:30
  12.0 0.8 fusion.6.place_ref
  12.7 3.5 %load.1.values_ref = bf16[1024,4096]{1,0:T(8,128)(2,1)S(1)} custom-call(bf16[1024,4096]{1,0:T(8,128)(2,1)} %source_ref.3), custom_call_target="tpu_custom_call" | custom-call | bytes 16777216 | tf_op jit(solution)/shard_map/load/pallas_call | solution.py:231
  17.7 1.9 %collective-permute-done.2 = bf16[1024,128]{1,0:T(8,128)(2,1)S(1)} collective-permute-done((bf16[1024,128]{1,0:T(8,128)(2,1)S(1)}, bf16[1024,128]{1,0:T(8,128)(2,1)S(1)}, u32[]{:S(2)}, u32[]{:S(2)}) %collective-permute-start.2) | collective-permute-done | bytes 262176 | tf_op jit(solution)/shard_map/ppermute | solution.py:30
  19.8 3.5 %collective-permute-done.4 = bf16[1024,128]{1,0:T(8,128)(2,1)S(1)} collective-permute-done((bf16[1024,128]{1,0:T(8,128)(2,1)S(1)}, bf16[1024,128]{1,0:T(8,128)(2,1)S(1)}, u32[]{:S(2)}, u32[]{:S(2)}) %collective-permute-start.4) | collective-permute-done | bytes 262176 | tf_op jit(solution)/shard_map/ppermute | solution.py:30
  24.0 0.9 collective-permute-done.6
  25.3 9.1 %forward.1 = (bf16[1024,512]{1,0:T(8,128)(2,1)}, bf16[8,128,128]{2,1,0:T(8,128)(2,1)S(1)}, f32[8,8,640]{2,1,0:T(8,128)S(1)}, f32[8,8,640]{2,1,0:T(8,128)S(1)}) custom-call(s32[8,32]{1,0:T(8,128)S(1)} %fusion.6.place_ref, s32[1]{0:T(128)} %bitcast.core_ref, bf16[104,128,128]{2,1,0:T(8,128)(2,1)S(1)} %bitcast.44, bf16[1024,4096]{1,0:T(8,128)(2,1)S(1)} %load.1.values_ref, ...), custom_call_target="tpu_custom_call" | custom-call | flops 3221225472 | bytes 15728640 | tf_op jit(solution)/shard_map/forward/pallas_call | solution.py:233
  34.4 7.2 %backward.1 = (bf16[48,128,128]{2,1,0:T(8,128)(2,1)S(1)}, bf16[48,128,128]{2,1,0:T(8,128)(2,1)}) custom-call(s32[8,32]{1,0:T(8,128)S(1)} %fusion.6.place_ref, bf16[8,128,128]{2,1,0:T(8,128)(2,1)S(1)} %get-tuple-element.11.back_ref, bf16[1024,4096]{1,0:T(8,128)(2,1)} %source_ref.3), custom_call_target="tpu_custom_call" | custom-call | flops 2147483648 | bytes 12582912 | tf_op jit(solution)/shard_map/backward/pallas_call | solution.py:290
  42.2 3.3 %collective-permute-done.15 = f32[8,8,640]{2,1,0:T(8,128)S(1)} collective-permute-done((f32[8,8,640]{2,1,0:T(8,128)S(1)}, f32[8,8,640]{2,1,0:T(8,128)S(1)}, u32[]{:S(2)}, u32[]{:S(2)}) %collective-permute-start.15) | collective-permute-done | bytes 163872 | tf_op jit(solution)/shard_map/ppermute | solution.py:30
  45.6 21.1 %all_to_all.15 = f32[8,8,640]{2,1,0:T(8,128)S(1)} all-to-all(f32[8,8,640]{2,1,0:T(8,128)S(1)} %add.43), channel_id=1, replica_groups=mesh['y_lo'=2,'z'=8,'x'=4,'y_hi'=2,'core'=2] {'x','y_hi'}, dimensions={0} | all-to-all | bytes 327680 | tf_op jit(solution)/shard_map/all_to_all | solution.py:296
  67.5 7.5 %all-to-all-start.1 = ((f32[16,8,640]{2,1,0:T(8,128)}), f32[16,8,640]{2,1,0:T(8,128)S(1)}, u32[]{:S(2)}, u32[]{:S(2)}) async-start(f32[16,8,640]{2,1,0:T(8,128)} %broadcast_in_dim.9), calls=%async_computation.1 | async-start | bytes 655360 | tf_op jit(solution)/shard_map/all_to_all | solution.py:48
  75.0 1.4 %add_convert_fusion = (bf16[16,128,128]{2,1,0:T(8,128)(2,1)}, bf16[16,128,128]{2,1,0:T(8,128)(2,1)}) fusion(bf16[48,128,128]{2,1,0:T(8,128)(2,1)S(1)} %collective-permute-done.11, bf16[48,128,128]{2,1,0:T(8,128)(2,1)S(1)} %get-tuple-element.12), kind=kLoop, calls=%fused_computation | loop fusion | flops 2097152 | bytes 3145728 | tf_op jit(solution)/shard_map/convert_element_type | solution.py:302
  76.4 0.9 collective-permute-start.12
  77.3 1.1 collective-permute-start.13
  78.4 6.9 %all-to-all-done.1 = f32[16,8,640]{2,1,0:T(8,128)S(1)} async-done(((f32[16,8,640]{2,1,0:T(8,128)}), f32[16,8,640]{2,1,0:T(8,128)S(1)}, u32[]{:S(2)}, u32[]{:S(2)}) %all-to-all-start.1) | async-done | bytes 327712 | tf_op jit(solution)/shard_map/all_to_all | solution.py:48
  86.0 7.1 %all-to-all-start.2 = ((f32[8,8,512]{2,1,0:T(8,128)}), f32[8,8,512]{2,1,0:T(8,128)S(1)}, u32[]{:S(2)}, u32[]{:S(2)}) async-start(f32[8,8,512]{2,1,0:T(8,128)} %broadcast_in_dim.10), calls=%async_computation.2 | async-start | bytes 262144 | tf_op jit(solution)/shard_map/all_to_all | solution.py:48
  93.1 6.4 %all-to-all-done.2 = f32[8,8,512]{2,1,0:T(8,128)S(1)} async-done(((f32[8,8,512]{2,1,0:T(8,128)}), f32[8,8,512]{2,1,0:T(8,128)S(1)}, u32[]{:S(2)}, u32[]{:S(2)}) %all-to-all-start.2) | async-done | bytes 131104 | tf_op jit(solution)/shard_map/all_to_all | solution.py:48
  100.1 1.4 %merge.1 = bf16[1024,128]{1,0:T(8,128)(2,1)S(1)} custom-call(bf16[3,2,8,128,128]{4,3,2,1,0:T(8,128)(2,1)S(1)} %bitcast.40, bf16[3,2,8,128,128]{4,3,2,1,0:T(8,128)(2,1)S(1)} %bitcast.42, bf16[2,8,128,128]{3,2,1,0:T(8,128)(2,1)} %collective-permute-done.12.up_ref, bf16[2,8,128,128]{3,2,1,0:T(8,128)(2,1)} %collective-permute-done.13.down_ref), custom_call_target="tpu_custom_call" | custom-call | flops 1048576 | bytes 2097152 | tf_op jit(solution)/shard_map/merge/pallas_call | solution.py:316
  101.5 1.2 %collective-permute-start.14 = (bf16[1024,128]{1,0:T(8,128)(2,1)S(1)}, bf16[1024,128]{1,0:T(8,128)(2,1)S(1)}, u32[]{:S(2)}, u32[]{:S(2)}) collective-permute-start(bf16[1024,128]{1,0:T(8,128)(2,1)S(1)} %merge.1), channel_id=1, source_target_pairs={{0,2},{1,3},{2,0},{3,1},{4,6},{5,7},{6,4},{7,5},{8,10},{9,11},{10,... | collective-permute-start | bytes 786440 | tf_op jit(solution)/shard_map/ppermute | solution.py:30
  103.4 8.4 %collective-permute-done.14.last_ref = bf16[1024,128]{1,0:T(8,128)(2,1)S(1)} collective-permute-done((bf16[1024,128]{1,0:T(8,128)(2,1)S(1)}, bf16[1024,128]{1,0:T(8,128)(2,1)S(1)}, u32[]{:S(2)}, u32[]{:S(2)}) %collective-permute-start.14) | collective-permute-done | bytes 262176 | tf_op jit(solution)/shard_map/ppermute | solution.py:30
  111.8 2.8 %final.1 = f32[1024,128]{1,0:T(8,128)} custom-call(bf16[3,2,8,128,128]{4,3,2,1,0:T(8,128)(2,1)S(1)} %bitcast.41, bf16[3,2,8,128,128]{4,3,2,1,0:T(8,128)(2,1)S(1)} %bitcast.43, bf16[2,8,128,128]{3,2,1,0:T(8,128)(2,1)} %collective-permute-done.12.up_ref, bf16[2,8,128,128]{3,2,1,0:T(8,128)(2,1)} %collective-permute-done.13.down_ref, ...), custom_call_target="tpu_custom_call" | custom-call | flops 1048576 | bytes 2097152 | tf_op jit(solution)/shard_map/final/pallas_call | solution.py:335
  (52 shorter events, 6.6 us)
Async XLA Ops:
  0.6 9.8 %collective-permute-start.1 = (bf16[1024,128]{1,0:T(8,128)(2,1)}, bf16[1024,128]{1,0:T(8,128)(2,1)S(1)}, u32[]{:S(2)}, u32[]{:S(2)}) collective-permute-start(bf16[1024,128]{1,0:T(8,128)(2,1)} %param.7), channel_id=1, source_target_pairs={{0,2},{1,3},{2,0},{3,1},{4,6},{5,7},{6,4},{7,5},{8,10},{9,11},{10,... | collective-permute-start | bytes 786440 | tf_op jit(solution)/shard_map/ppermute | solution.py:30
  3.9 13.1 %collective-permute-start = (bf16[1024,128]{1,0:T(8,128)(2,1)}, bf16[1024,128]{1,0:T(8,128)(2,1)S(1)}, u32[]{:S(2)}, u32[]{:S(2)}) collective-permute-start(bf16[1024,128]{1,0:T(8,128)(2,1)} %param.7), channel_id=1, source_target_pairs={{0,4},{1,5},{2,6},{3,7},{4,8},{5,9},{6,10},{7,11},{8,12},{9,13},{1... | collective-permute-start | bytes 786440 | tf_op jit(solution)/shard_map/ppermute | solution.py:30
  5.4 11.9 %collective-permute-start.3 = (bf16[1024,128]{1,0:T(8,128)(2,1)}, bf16[1024,128]{1,0:T(8,128)(2,1)S(1)}, u32[]{:S(2)}, u32[]{:S(2)}) collective-permute-start(bf16[1024,128]{1,0:T(8,128)(2,1)} %param.7), channel_id=1, source_target_pairs={{0,252},{1,253},{2,254},{3,255},{4,0},{5,1},{6,2},{7,3},{8,4},{9,5... | collective-permute-start | bytes 786440 | tf_op jit(solution)/shard_map/ppermute | solution.py:30
  5.9 18.9 %collective-permute-start.7 = (bf16[1024,128]{1,0:T(8,128)(2,1)}, bf16[1024,128]{1,0:T(8,128)(2,1)S(1)}, u32[]{:S(2)}, u32[]{:S(2)}) collective-permute-start(bf16[1024,128]{1,0:T(8,128)(2,1)} %param.7), channel_id=1, source_target_pairs={{0,1},{1,0},{2,3},{3,2},{4,5},{5,4},{6,7},{7,6},{8,9},{9,8},{10,11... | collective-permute-start | bytes 786440 | tf_op jit(solution)/shard_map/ppermute | solution.py:30
  10.5 9.1 %collective-permute-start.2 = (bf16[1024,128]{1,0:T(8,128)(2,1)S(1)}, bf16[1024,128]{1,0:T(8,128)(2,1)S(1)}, u32[]{:S(2)}, u32[]{:S(2)}) collective-permute-start(bf16[1024,128]{1,0:T(8,128)(2,1)S(1)} %collective-permute-done.1), channel_id=1, source_target_pairs={{0,4},{1,5},{2,6},{3,7},{4,8},{5,9},{6,10},{7,11},{8,12},{9,13},{1... | collective-permute-start | bytes 786440 | tf_op jit(solution)/shard_map/ppermute | solution.py:30
  12.7 6.9 %copy-start.3 = (bf16[1024,128]{1,0:T(8,128)(2,1)S(1)}, bf16[1024,128]{1,0:T(8,128)(2,1)}, u32[]{:S(2)}) copy-start(bf16[1024,128]{1,0:T(8,128)(2,1)} %param.7) | copy-start | bytes 786436
  16.2 9.0 %copy-start = (bf16[1024,512]{1,0:T(8,128)(2,1)S(1)}, bf16[1024,512]{1,0:T(8,128)(2,1)}, u32[]{:S(2)}) copy-start(bf16[1024,512]{1,0:T(8,128)(2,1)} %grad_ref.1) | copy-start | bytes 3145732
  16.3 9.0 %copy-start.1 = (bf16[128,512]{1,0:T(8,128)(2,1)S(1)}, bf16[128,512]{1,0:T(8,128)(2,1)}, u32[]{:S(2)}) copy-start(bf16[128,512]{1,0:T(8,128)(2,1)} %weight_ref.1) | copy-start | bytes 393220
  16.3 9.0 %copy-start.2 = (f32[512]{0:T(512)S(1)}, f32[512]{0:T(512)}, u32[]{:S(2)}) copy-start(f32[512]{0:T(512)} %param.9) | copy-start | bytes 6148
  16.3 7.0 %collective-permute-start.4 = (bf16[1024,128]{1,0:T(8,128)(2,1)S(1)}, bf16[1024,128]{1,0:T(8,128)(2,1)S(1)}, u32[]{:S(2)}, u32[]{:S(2)}) collective-permute-start(bf16[1024,128]{1,0:T(8,128)(2,1)S(1)} %collective-permute-done.1), channel_id=1, source_target_pairs={{0,252},{1,253},{2,254},{3,255},{4,0},{5,1},{6,2},{7,3},{8,4},{9,5... | collective-permute-start | bytes 786440 | tf_op jit(solution)/shard_map/ppermute | solution.py:30
  17.0 6.3 %collective-permute-start.5 = (bf16[1024,128]{1,0:T(8,128)(2,1)S(1)}, bf16[1024,128]{1,0:T(8,128)(2,1)S(1)}, u32[]{:S(2)}, u32[]{:S(2)}) collective-permute-start(bf16[1024,128]{1,0:T(8,128)(2,1)S(1)} %collective-permute-done), channel_id=1, source_target_pairs={{0,1},{1,0},{2,3},{3,2},{4,5},{5,4},{6,7},{7,6},{8,9},{9,8},{10,11... | collective-permute-start | bytes 786440 | tf_op jit(solution)/shard_map/ppermute | solution.py:30
  17.3 7.6 %collective-permute-start.8 = (bf16[1024,128]{1,0:T(8,128)(2,1)S(1)}, bf16[1024,128]{1,0:T(8,128)(2,1)S(1)}, u32[]{:S(2)}, u32[]{:S(2)}) collective-permute-start(bf16[1024,128]{1,0:T(8,128)(2,1)S(1)} %collective-permute-done.1), channel_id=1, source_target_pairs={{0,1},{1,0},{2,3},{3,2},{4,5},{5,4},{6,7},{7,6},{8,9},{9,8},{10,11... | collective-permute-start | bytes 786440 | tf_op jit(solution)/shard_map/ppermute | solution.py:30
  19.6 5.4 %collective-permute-start.9 = (bf16[1024,128]{1,0:T(8,128)(2,1)S(1)}, bf16[1024,128]{1,0:T(8,128)(2,1)S(1)}, u32[]{:S(2)}, u32[]{:S(2)}) collective-permute-start(bf16[1024,128]{1,0:T(8,128)(2,1)S(1)} %collective-permute-done.3), channel_id=1, source_target_pairs={{0,1},{1,0},{2,3},{3,2},{4,5},{5,4},{6,7},{7,6},{8,9},{9,8},{10,11... | collective-permute-start | bytes 786440 | tf_op jit(solution)/shard_map/ppermute | solution.py:30
  23.3 1.5 %collective-permute-start.6 = (bf16[1024,128]{1,0:T(8,128)(2,1)S(1)}, bf16[1024,128]{1,0:T(8,128)(2,1)S(1)}, u32[]{:S(2)}, u32[]{:S(2)}) collective-permute-start(bf16[1024,128]{1,0:T(8,128)(2,1)S(1)} %collective-permute-done.2), channel_id=1, source_target_pairs={{0,1},{1,0},{2,3},{3,2},{4,5},{5,4},{6,7},{7,6},{8,9},{9,8},{10,11... | collective-permute-start | bytes 786440 | tf_op jit(solution)/shard_map/ppermute | solution.py:30
  23.3 1.9 %collective-permute-start.10 = (bf16[1024,128]{1,0:T(8,128)(2,1)S(1)}, bf16[1024,128]{1,0:T(8,128)(2,1)S(1)}, u32[]{:S(2)}, u32[]{:S(2)}) collective-permute-start(bf16[1024,128]{1,0:T(8,128)(2,1)S(1)} %collective-permute-done.4), channel_id=1, source_target_pairs={{0,1},{1,0},{2,3},{3,2},{4,5},{5,4},{6,7},{7,6},{8,9},{9,8},{10,11... | collective-permute-start | bytes 786440 | tf_op jit(solution)/shard_map/ppermute | solution.py:30
  41.6 33.4 %collective-permute-start.11 = (bf16[48,128,128]{2,1,0:T(8,128)(2,1)}, bf16[48,128,128]{2,1,0:T(8,128)(2,1)S(1)}, u32[]{:S(2)}, u32[]{:S(2)}) collective-permute-start(bf16[48,128,128]{2,1,0:T(8,128)(2,1)} %get-tuple-element.13), channel_id=1, source_target_pairs={{0,1},{1,0},{2,3},{3,2},{4,5},{5,4},{6,7},{7,6},{8,9},{9,8},{10,11... | collective-permute-start | bytes 4718600 | tf_op jit(solution)/shard_map/ppermute | solution.py:30
  42.0 3.6 %collective-permute-start.15 = (f32[8,8,640]{2,1,0:T(8,128)S(1)}, f32[8,8,640]{2,1,0:T(8,128)S(1)}, u32[]{:S(2)}, u32[]{:S(2)}) collective-permute-start(f32[8,8,640]{2,1,0:T(8,128)S(1)} %get-tuple-element.15), channel_id=1, source_target_pairs={{0,1},{1,0},{2,3},{3,2},{4,5},{5,4},{6,7},{7,6},{8,9},{9,8},{10,11... | collective-permute-start | bytes 491528 | tf_op jit(solution)/shard_map/ppermute | solution.py:30
  67.5 17.8 %all-to-all-start.1 = ((f32[16,8,640]{2,1,0:T(8,128)}), f32[16,8,640]{2,1,0:T(8,128)S(1)}, u32[]{:S(2)}, u32[]{:S(2)}) async-start(f32[16,8,640]{2,1,0:T(8,128)} %broadcast_in_dim.9), calls=%async_computation.1 | async-start | bytes 655360 | tf_op jit(solution)/shard_map/all_to_all | solution.py:48
  76.4 23.7 %collective-permute-start.12 = (bf16[2,8,128,128]{3,2,1,0:T(8,128)(2,1)}, bf16[2,8,128,128]{3,2,1,0:T(8,128)(2,1)}, u32[]{:S(2)}, u32[]{:S(2)}) collective-permute-start(bf16[2,8,128,128]{3,2,1,0:T(8,128)(2,1)} %bitcast.17), channel_id=1, source_target_pairs={{0,4},{1,5},{2,6},{3,7},{4,8},{5,9},{6,10},{7,11},{8,12},{9,13},{1... | collective-permute-start | bytes 1572872 | tf_op jit(solution)/shard_map/ppermute | solution.py:30
  77.3 22.8 %collective-permute-start.13 = (bf16[2,8,128,128]{3,2,1,0:T(8,128)(2,1)}, bf16[2,8,128,128]{3,2,1,0:T(8,128)(2,1)}, u32[]{:S(2)}, u32[]{:S(2)}) collective-permute-start(bf16[2,8,128,128]{3,2,1,0:T(8,128)(2,1)} %bitcast.18), channel_id=1, source_target_pairs={{0,252},{1,253},{2,254},{3,255},{4,0},{5,1},{6,2},{7,3},{8,4},{9,5... | collective-permute-start | bytes 1572872 | tf_op jit(solution)/shard_map/ppermute | solution.py:30
  86.0 13.5 %all-to-all-start.2 = ((f32[8,8,512]{2,1,0:T(8,128)}), f32[8,8,512]{2,1,0:T(8,128)S(1)}, u32[]{:S(2)}, u32[]{:S(2)}) async-start(f32[8,8,512]{2,1,0:T(8,128)} %broadcast_in_dim.10), calls=%async_computation.2 | async-start | bytes 262144 | tf_op jit(solution)/shard_map/all_to_all | solution.py:48
  99.5 3.2 %collective-permute-start.16 = (f32[8,8,512]{2,1,0:T(8,128)S(1)}, f32[8,8,512]{2,1,0:T(8,128)S(1)}, u32[]{:S(2)}, u32[]{:S(2)}) collective-permute-start(f32[8,8,512]{2,1,0:T(8,128)S(1)} %all-to-all-done.2), channel_id=1, source_target_pairs={{0,1},{1,0},{2,3},{3,2},{4,5},{5,4},{6,7},{7,6},{8,9},{9,8},{10,11... | collective-permute-start | bytes 393224 | tf_op jit(solution)/shard_map/ppermute | solution.py:30
  101.5 10.3 %collective-permute-start.14 = (bf16[1024,128]{1,0:T(8,128)(2,1)S(1)}, bf16[1024,128]{1,0:T(8,128)(2,1)S(1)}, u32[]{:S(2)}, u32[]{:S(2)}) collective-permute-start(bf16[1024,128]{1,0:T(8,128)(2,1)S(1)} %merge.1), channel_id=1, source_target_pairs={{0,2},{1,3},{2,0},{3,1},{4,6},{5,7},{6,4},{7,5},{8,10},{9,11},{10,... | collective-permute-start | bytes 786440 | tf_op jit(solution)/shard_map/ppermute | solution.py:30
